TPU v7x, 32 devices: a whole 2x2x4 slice. The times are simulated.
32 devices in a mesh: replica: 4 (over z), fsdp: 8 (over y, x, core).
Axes of the slice: x: 2, y: 2, z: 4, core: 2. Of those that a mesh axis runs over, the one named last changes fastest.
Arguments:
- prompt_hidden: bfloat16 [16, 1024, 1024], P('replica', 'fsdp'), may hold values from -6 to 6
- sequel_hidden: bfloat16 [128, 128, 1024], P(('replica', 'fsdp')), may hold values from -6 to 6
- parents: int32 [128], P(('replica', 'fsdp')), may hold values from 0 to 3, as said below
- prompt_cotangent: bfloat16 [16, 1024, 1024], P('replica', 'fsdp'), may hold values from -6 to 6
- sequel_cotangent: bfloat16 [128, 128, 1024], P(('replica', 'fsdp')), may hold values from -6 to 6
- norm_gain: bfloat16 [1024], P('fsdp'), may hold values from 0.5 to 1.5
- input_weight: bfloat16 [1024, 4096], P('fsdp'), may hold values from -0.1875 to 0.1875
- filter_weight: bfloat16 [4, 2048], P(None, 'fsdp'), may hold values from -3 to 3
- depthwise_filter_bias: bfloat16 [2048], P('fsdp'), may hold values from -0.5 to 0.5
- select_weight: bfloat16 [2048, 96], P('fsdp'), may hold values from -0.125 to 0.125
- step_weight: bfloat16 [64, 2048], P(None, 'fsdp'), may hold values from -0.75 to 0.75
- step_bias: bfloat16 [2048], P('fsdp'), may hold values from -7 to -2
- decay_log: bfloat16 [2048, 16], P('fsdp'), may hold values from 0 to 2.765625
- skip_gain: bfloat16 [2048], P('fsdp'), may hold values from 0.5 to 1.5
- output_weight: bfloat16 [2048, 1024], P('fsdp'), may hold values from -0.5 to 0.5
Outputs:
- prompt_output: bfloat16 [16, 1024, 1024], P('replica', 'fsdp')
- sequel_output: bfloat16 [128, 128, 1024], P(('replica', 'fsdp'))
- prompt_input_gradient: float32 [16, 1024, 1024], P('replica', 'fsdp')
- sequel_input_gradient: float32 [128, 128, 1024], P(('replica', 'fsdp'))
- norm_gain_gradient: float32 [1024], P('fsdp')
- input_weight_gradient: float32 [1024, 4096], P('fsdp')
- filter_weight_gradient: float32 [4, 2048], P(None, 'fsdp')
- filter_bias_gradient: float32 [2048], P('fsdp')
- select_weight_gradient: float32 [2048, 96], P('fsdp')
- step_weight_gradient: float32 [64, 2048], P(None, 'fsdp')
- step_bias_gradient: float32 [2048], P('fsdp')
- decay_log_gradient: float32 [2048, 16], P('fsdp')
- skip_gain_gradient: float32 [2048], P('fsdp')
- output_weight_gradient: float32 [2048, 1024], P('fsdp')
Inputs may be any that keep to these rules, and one draw needn't show every extreme that they name: `parents`: in each aligned block of 32 continuations (those of one replica index) every value appears exactly 8 times; value p in block r names prompt r * 4 + p.
All inputs are finite; a program needn't handle non-finite values.
Results may differ from a plain program's by a relative error of at most 0.012.
Values may be sent and summed in bfloat16 or wider, within the bound.
A program may use at most 448 MiB of HBM per device.

v0:
```python
import functools
import math

import jax
import jax.numpy as jnp
from jax import lax
from jax.experimental import pallas as pl
from jax.experimental.pallas import tpu as pltpu
from jax.sharding import PartitionSpec as P

D = 1024
INNER = 2048
STATES = 16
RANK = 64
KERNEL = 4
PROMPTS = 4

SEQS = 8
HALO = 4
LANES = 128
WIDE = 256
LOG2E = math.log2(math.e)
LN2 = math.log(2.0)
f32 = jnp.float32
bf16 = jnp.bfloat16

VMEM_LIMIT = 62 * 1024 * 1024


def cost(microseconds):
    return pl.CostEstimate(flops=int(microseconds * 1e9), bytes_accessed=0, transcendentals=0)


def params(**kw):
    return pltpu.CompilerParams(vmem_limit_bytes=VMEM_LIMIT, **kw)


def sigmoid(x):
    return 1.0 / (1.0 + jnp.exp(-x))


def softplus(x):
    return jnp.maximum(x, 0.0) + jnp.log1p(jnp.exp(-jnp.abs(x)))


def front_kernel(mix_ref, fw_ref, fb_ref, sel_ref, act_ref, proj_ref):
    j = pl.program_id(0)
    steps = act_ref.shape[0]
    chunk = 16
    taps = [fw_ref[k : k + 1, :] for k in range(KERNEL)]
    bias = fb_ref[0:1, :]

    @pl.when(j == 0)
    def _():
        proj_ref[...] = jnp.zeros_like(proj_ref)

    def step(i, _):
        t = i * chunk
        x = mix_ref[pl.ds(t, chunk + HALO)].astype(bf16).astype(f32)
        v = bias[None] + taps[0][None] * x[1 : 1 + chunk]
        for k in range(1, KERNEL):
            v = v + taps[k][None] * x[1 + k : 1 + k + chunk]
        act = v * sigmoid(v)
        act_ref[pl.ds(t, chunk)] = act
        low = act.reshape(chunk * SEQS, act.shape[-1]).astype(bf16)
        r = pl.multiple_of(t * SEQS, chunk * SEQS)
        proj_ref[pl.ds(r, chunk * SEQS), :] += jnp.dot(low, sel_ref[...], preferred_element_type=f32)
        return 0

    lax.fori_loop(0, steps // chunk, step, 0)


def front(mixture, fw, fb, select_pad, steps):
    channels = fw.shape[1]
    return pl.pallas_call(
        front_kernel,
        grid=(channels // WIDE,),
        in_specs=[
            pl.BlockSpec((steps + HALO, SEQS, WIDE), lambda j: (0, 0, j)),
            pl.BlockSpec((KERNEL, WIDE), lambda j: (0, j)),
            pl.BlockSpec((1, WIDE), lambda j: (0, j)),
            pl.BlockSpec((WIDE, LANES), lambda j: (j, 0)),
        ],
        out_specs=[
            pl.BlockSpec((steps, SEQS, WIDE), lambda j: (0, 0, j)),
            pl.BlockSpec((steps * SEQS, LANES), lambda j: (0, 0)),
        ],
        out_shape=[
            jax.ShapeDtypeStruct((steps, SEQS, channels), f32),
            jax.ShapeDtypeStruct((steps * SEQS, LANES), f32),
        ],
        compiler_params=params(),
        cost_estimate=cost(16),
        name="front",
    )(mixture, fw, fb, select_pad)


def pair(a, b):
    return jnp.concatenate([a, b], axis=0).astype(bf16)


def both(v):
    return pair(v, v)


def halves(v):
    v = v.astype(f32)
    return v[:SEQS], v[SEQS:]


def folded(v):
    a, b = halves(v)
    return a + b


def spread_maps(proj_ref, select_ref, first, count, store):
    steps = proj_ref.shape[0] // SEQS
    chunk = 32

    def step(i, _):
        r = pl.multiple_of(i * chunk * SEQS, chunk * SEQS)
        rows = proj_ref[pl.ds(r, chunk * SEQS), :].astype(bf16)
        for n in range(0, count, 2):
            at = (first - RANK + n) * LANES
            wide = jnp.dot(rows, select_ref[:, at : at + 2 * LANES], preferred_element_type=f32)
            wide = wide.reshape(chunk, SEQS, 2 * LANES)
            store(i * chunk, chunk, n, wide[:, :, :LANES], wide[:, :, LANES:])
        return 0

    lax.fori_loop(0, steps // chunk, step, 0)


def store_plain(ref):
    def store(t, count, n, a, b):
        ref[pl.ds(t, count), n] = a
        ref[pl.ds(t, count), n + 1] = b

    return store


def store_pairs(ref):
    def store(t, count, n, a, b):
        ref[pl.ds(t, count), n // 2] = jnp.concatenate([a, b], axis=1).astype(bf16)

    return store


PAIRS = STATES // 2
RUN = 8


def piece_kernel(
    proj_ref, act_ref, gate_ref, gg_ref, stepw_ref, sbias_ref, rate_ref, select_ref,
    dt_ref, sig_ref, yg_ref, silu_ref, slope_ref, fwd_ref, bwd_ref, tot_ref,
    b_scr, c_scr, time_scr, acc_scr,
):
    j = pl.program_id(0)
    steps = dt_ref.shape[0]
    half = SEQS // 2
    groups = fwd_ref.shape[0]

    @pl.when(j == 0)
    def _():
        def store_groups(t, count, n, a, b):
            for group in range(groups):
                rows = slice(group * half, (group + 1) * half)
                parts = [a[:, rows], a[:, rows], b[:, rows], b[:, rows]]
                b_scr[group, pl.ds(t, count), n // 2] = jnp.concatenate(parts, axis=1).astype(bf16)

        spread_maps(proj_ref, select_ref, RANK, STATES, store_groups)
        spread_maps(proj_ref, select_ref, RANK + STATES, STATES, store_pairs(c_scr))

    chunk = 8
    sbias = sbias_ref[0:1, :]

    def prep(i, total):
        t = i * chunk
        r = pl.multiple_of(t * SEQS, chunk * SEQS)
        rank = proj_ref[pl.ds(r, chunk * SEQS), :].astype(bf16)
        pre = jnp.dot(rank, stepw_ref[...], preferred_element_type=f32).reshape(chunk, SEQS, WIDE)
        pre = pre + sbias[None]
        small = jnp.exp2(jnp.abs(pre) * -LOG2E)
        one = 1.0 + small
        inverse = 1.0 / one
        dt = jnp.maximum(pre, 0.0) + (jnp.log(one) + (small - (one - 1.0)) * inverse)
        dt_ref[pl.ds(t, chunk)] = dt
        sig_ref[pl.ds(t, chunk)] = jnp.where(pre >= 0.0, inverse, small * inverse).astype(bf16)
        gate = gate_ref[pl.ds(t + HALO, chunk)]
        gg = gg_ref[pl.ds(t, chunk)]
        sig = sigmoid(gate)
        silu = gate * sig
        yg_ref[pl.ds(t, chunk)] = gg * silu
        silu_ref[pl.ds(t, chunk)] = silu.astype(bf16)
        slope_ref[pl.ds(t, chunk)] = (gg * (sig + silu * (1.0 - sig))).astype(bf16)
        for k in range(chunk):
            total = total + dt[k]
            time_scr[t + k] = total
        return total

    total = lax.fori_loop(0, steps // chunk, prep, jnp.zeros((SEQS, WIDE), f32))
    tot_ref[...] = total

    def weighted(rates, vectors, map_at, out):
        acc_scr[...] = jnp.zeros_like(acc_scr)

        def run(i, _):
            sums = [None] * PAIRS
            for k in range(RUN):
                t = i * RUN + k
                time, drive = vectors(t)
                for p in range(PAIRS):
                    term = jnp.exp2(time * rates[p]) * drive * map_at(t, p)
                    sums[p] = term if k == 0 else sums[p] + term
            for p in range(PAIRS):
                a, b = halves(sums[p])
                acc_scr[2 * p] += a
                acc_scr[2 * p + 1] += b
            return 0

        lax.fori_loop(0, steps // RUN, run, 0)
        for n in range(STATES):
            out(n, acc_scr[n])

    low = lax.broadcasted_iota(jnp.int32, (SEQS, LANES), 0) < half
    packed = [
        jnp.where(low, rate_ref[n : n + 1, :LANES], rate_ref[n : n + 1, LANES:])
        for n in range(STATES)
    ]
    packed = [pair(packed[2 * p], packed[2 * p + 1]) for p in range(PAIRS)]
    for group in range(groups):
        rows = slice(group * half, (group + 1) * half)

        def pack(v):
            return jnp.concatenate([v[rows, :LANES], v[rows, LANES:]], axis=0)

        whole = pack(total)

        def vectors(t):
            return both(whole - pack(time_scr[t])), both(pack(dt_ref[t] * act_ref[t]))

        def map_at(t, p):
            return b_scr[group, t, p]

        def out(n, value):
            fwd_ref[group, 0, n] = value

        weighted(packed, vectors, map_at, out)

    for part in range(WIDE // LANES):
        cols = slice(part * LANES, (part + 1) * LANES)
        mine = [jnp.broadcast_to(rate_ref[n : n + 1, cols], (SEQS, LANES)) for n in range(STATES)]
        mine = [pair(mine[2 * p], mine[2 * p + 1]) for p in range(PAIRS)]

        def vectors(t):
            return both(time_scr[t, :, cols]), both(yg_ref[t, :, cols])

        def map_at(t, p):
            return c_scr[t, p]

        def out(n, value):
            bwd_ref[n, :, cols] = value

        weighted(mine, vectors, map_at, out)


def piece(proj, act, mixture, gated_grad, step_pad, sbias, rate, select, groups):
    steps, _, channels = act.shape
    grid = channels // WIDE
    wide = lambda j: (0, 0, j)
    flat = pl.BlockSpec((steps, SEQS, WIDE), wide)
    shape = (steps, SEQS, channels)
    return pl.pallas_call(
        piece_kernel,
        grid=(grid,),
        in_specs=[
            pl.BlockSpec((steps * SEQS, LANES), lambda j: (0, 0)),
            flat,
            pl.BlockSpec((steps + HALO, SEQS, WIDE), lambda j: (0, 0, j + grid)),
            flat,
            pl.BlockSpec((LANES, WIDE), lambda j: (0, j)),
            pl.BlockSpec((1, WIDE), lambda j: (0, j)),
            pl.BlockSpec((STATES, WIDE), lambda j: (0, j)),
            pl.BlockSpec(select.shape, lambda j: (0, 0)),
        ],
        out_specs=[
            flat, flat, flat, flat, flat,
            pl.BlockSpec((groups, 1, STATES, SEQS, LANES), lambda j: (0, j, 0, 0, 0)),
            pl.BlockSpec((STATES, SEQS, WIDE), wide),
            pl.BlockSpec((SEQS, WIDE), lambda j: (0, j)),
        ],
        out_shape=[
            jax.ShapeDtypeStruct(shape, f32),
            jax.ShapeDtypeStruct(shape, bf16),
            jax.ShapeDtypeStruct(shape, f32),
            jax.ShapeDtypeStruct(shape, bf16),
            jax.ShapeDtypeStruct(shape, bf16),
            jax.ShapeDtypeStruct((groups, grid, STATES, SEQS, LANES), f32),
            jax.ShapeDtypeStruct((STATES, SEQS, channels), f32),
            jax.ShapeDtypeStruct((SEQS, channels), f32),
        ],
        scratch_shapes=[
            pltpu.VMEM((groups, steps, PAIRS, 2 * SEQS, LANES), bf16),
            pltpu.VMEM((steps, PAIRS, 2 * SEQS, LANES), bf16),
            pltpu.VMEM((steps, SEQS, WIDE), f32),
            pltpu.VMEM((STATES, SEQS, LANES), f32),
        ],
        compiler_params=params(),
        cost_estimate=cost(60),
        name="piece",
    )(proj, act, mixture, gated_grad, step_pad, sbias, rate, select)


TILES = [slice(k * LANES, (k + 1) * LANES) for k in range(WIDE // LANES)]


def forward_kernel(
    proj_ref, dt_ref, act_ref, yg_ref, silu_ref, slope_ref, rate_ref, start_ref, skip_ref, select_ref,
    gated_ref, hist_ref, gategrad_ref, skipg_ref,
    b_scr, c_scr,
):
    j = pl.program_id(0)
    steps = dt_ref.shape[0]

    @pl.when(j == 0)
    def _():
        spread_maps(proj_ref, select_ref, RANK, STATES, store_plain(b_scr))
        spread_maps(proj_ref, select_ref, RANK + STATES, STATES, store_pairs(c_scr))

    rates = [jnp.broadcast_to(rate_ref[n : n + 1, :], (SEQS, LANES)) for n in range(STATES)]
    skip = jnp.broadcast_to(skip_ref[0:1, :], (SEQS, LANES))
    unroll = 8

    def run(i, carry):
        h, skip_sum = carry
        for k in range(unroll):
            t = i * unroll + k
            dt = dt_ref[t]
            act = act_ref[t]
            u = dt * act
            new = []
            y = None
            for p in range(PAIRS):
                for n in (2 * p, 2 * p + 1):
                    new.append(jnp.exp2(dt * rates[n]) * h[n] + u * b_scr[t, n])
                low = pair(new[2 * p], new[2 * p + 1])
                hist_ref[t + 1, p] = low
                term = low * c_scr[t, p]
                y = term if p == 0 else y + term
            h = tuple(new)
            mixed = folded(y) + skip * act
            gated_ref[t] = (mixed * silu_ref[t].astype(f32)).astype(bf16)
            gategrad_ref[t] = (mixed * slope_ref[t].astype(f32)).astype(bf16)
            skip_sum = skip_sum + yg_ref[t] * act
        return h, skip_sum

    start = tuple(start_ref[n] for n in range(STATES))
    for p in range(PAIRS):
        hist_ref[0, p] = pair(start[2 * p], start[2 * p + 1])
    _, skip_sum = lax.fori_loop(0, steps // unroll, run, (start, jnp.zeros((SEQS, LANES), f32)))
    skipg_ref[...] = jnp.sum(skip_sum, axis=0, keepdims=True)


def forward(proj, dt, act, yg, silu, slope, rate, start, skip, select):
    steps, _, channels = act.shape
    grid = channels // LANES
    tile = lambda j: (0, 0, j)
    flat = pl.BlockSpec((steps, SEQS, LANES), tile)
    parts = len(TILES)
    return pl.pallas_call(
        forward_kernel,
        grid=(grid,),
        in_specs=[
            pl.BlockSpec((steps * SEQS, LANES), lambda j: (0, 0)),
            flat, flat, flat, flat, flat,
            pl.BlockSpec((STATES, LANES), lambda j: (0, j)),
            pl.BlockSpec((STATES, SEQS, LANES), tile),
            pl.BlockSpec((1, LANES), lambda j: (0, j)),
            pl.BlockSpec(select.shape, lambda j: (0, 0)),
        ],
        out_specs=[
            flat,
            pl.BlockSpec(
                (None, None, steps + 1, PAIRS, 2 * SEQS, LANES),
                lambda j: (j // parts, j % parts, 0, 0, 0, 0),
            ),
            flat,
            pl.BlockSpec((1, LANES), lambda j: (0, j)),
        ],
        out_shape=[
            jax.ShapeDtypeStruct((steps, SEQS, channels), bf16),
            jax.ShapeDtypeStruct((grid // parts, parts, steps + 1, PAIRS, 2 * SEQS, LANES), bf16),
            jax.ShapeDtypeStruct((steps, SEQS, channels), bf16),
            jax.ShapeDtypeStruct((1, channels), f32),
        ],
        scratch_shapes=[
            pltpu.VMEM((steps, STATES, SEQS, LANES), f32),
            pltpu.VMEM((steps, PAIRS, 2 * SEQS, LANES), bf16),
        ],
        compiler_params=params(),
        cost_estimate=cost(50),
        name="forward_scan",
    )(proj, dt, act, yg, silu, slope, rate, start, skip, select)


def backward_kernel(
    proj_ref, dt_ref, sig_ref, act_ref, yg_ref, rate_ref, end_ref, skip_ref,
    hist_ref, rank_t_ref, stepw_t_ref, pick_ref, select_ref,
    act_grad_ref, stepg_ref, biasg_ref, decayg_ref, projg_ref,
    b_scr, c_scr, db_scr, dc_scr, pre_scr, acc_scr, decay_scr, ge_scr, sum_scr,
):
    j = pl.program_id(0)
    steps = dt_ref.shape[0]

    @pl.when(j == 0)
    def _():
        spread_maps(proj_ref, select_ref, RANK, STATES, store_pairs(b_scr))
        spread_maps(proj_ref, select_ref, RANK + STATES, STATES, store_plain(c_scr))

        def clear(t, _):
            for p in range(PAIRS):
                db_scr[t, p] = jnp.zeros((2 * SEQS, LANES), bf16)
                dc_scr[t, p] = jnp.zeros((2 * SEQS, LANES), bf16)
            return 0

        lax.fori_loop(0, steps, clear, 0)
        acc_scr[...] = jnp.zeros_like(acc_scr)

    decay_scr[...] = jnp.zeros_like(decay_scr)
    sum_scr[...] = jnp.zeros_like(sum_scr)
    for n in range(STATES):
        ge_scr[n] = end_ref[n]

    def run(i, _):
        base = steps - (i + 1) * RUN
        db = [[None] * PAIRS for _ in range(RUN)]
        dc = [[None] * PAIRS for _ in range(RUN)]
        for part, cols in enumerate(TILES):
            rates = [jnp.broadcast_to(rate_ref[n : n + 1, cols], (SEQS, LANES)) for n in range(STATES)]
            low_rates = [pair(rates[2 * p], rates[2 * p + 1]) for p in range(PAIRS)]
            skip = jnp.broadcast_to(skip_ref[0:1, cols], (SEQS, LANES))
            ge = [ge_scr[n, :, cols] for n in range(STATES)]
            bias_sum = jnp.zeros((SEQS, LANES), f32)
            decay = [None] * PAIRS
            for k in range(RUN - 1, -1, -1):
                t = base + k
                dt = dt_ref[t, :, cols]
                act = act_ref[t, :, cols]
                yg = yg_ref[t, :, cols]
                u2 = both(dt * act)
                dt2 = both(dt)
                yg2 = both(yg)
                du = None
                ddt = None
                for p in range(PAIRS):
                    g = [ge[n] + yg * c_scr[t, n] for n in (2 * p, 2 * p + 1)]
                    g2 = pair(*g)
                    term = yg2 * hist_ref[part, t + 1, p]
                    dc[k][p] = term if part == 0 else dc[k][p] + term
                    term = g2 * u2
                    db[k][p] = term if part == 0 else db[k][p] + term
                    term = g2 * b_scr[t, p]
                    du = term if p == 0 else du + term
                    gn = [jnp.exp2(dt * rates[2 * p + m]) * g[m] for m in (0, 1)]
                    ge[2 * p], ge[2 * p + 1] = gn
                    q = pair(*gn) * hist_ref[part, t, p]
                    term = q * dt2
                    decay[p] = term if decay[p] is None else decay[p] + term
                    term = q * low_rates[p]
                    ddt = term if p == 0 else ddt + term
                du = folded(du)
                pre_grad = (du * act + folded(ddt) * LN2) * sig_ref[t, :, cols].astype(f32)
                pre_scr[t, :, cols] = pre_grad.astype(bf16)
                act_grad_ref[t, :, cols] = yg * skip + du * dt
                bias_sum = bias_sum + pre_grad
                if part == len(TILES) - 1:
                    for p in range(PAIRS):
                        dc_scr[t, p] = dc[k][p] + dc_scr[t, p]
                        db_scr[t, p] = db[k][p] + db_scr[t, p]
            for p in range(PAIRS):
                a, b = halves(decay[p])
                decay_scr[2 * p, :, cols] += a
                decay_scr[2 * p + 1, :, cols] += b
            for n in range(STATES):
                ge_scr[n, :, cols] = ge[n]
            sum_scr[:, cols] += bias_sum
        return 0

    lax.fori_loop(0, steps // RUN, run, 0)
    for n in range(STATES):
        decayg_ref[n : n + 1, :] = jnp.sum(decay_scr[n] * rate_ref[n : n + 1, :], axis=0, keepdims=True) * LN2
    biasg_ref[...] = jnp.sum(sum_scr[...], axis=0, keepdims=True)

    pre_low = pre_scr[...].reshape(steps * SEQS, WIDE)
    stepg_ref[...] = jnp.dot(rank_t_ref[...], pre_low, preferred_element_type=f32)
    acc_scr[...] += jnp.dot(pre_low, stepw_t_ref[...], preferred_element_type=f32)

    @pl.when(j == pl.num_programs(0) - 1)
    def _():
        chunk = 32
        even = lax.broadcasted_iota(jnp.int32, (chunk, SEQS, LANES), 2) % 2 == 0

        def step(i, _):
            t = i * chunk
            total = jnp.zeros((chunk * 2 * SEQS, LANES), f32)
            for p in range(PAIRS):
                rows = jnp.concatenate([db_scr[pl.ds(t, chunk), p], dc_scr[pl.ds(t, chunk), p]], axis=2)
                rows = rows.reshape(chunk * 2 * SEQS, 2 * LANES)
                total = total + jnp.dot(rows, pick_ref[p], preferred_element_type=f32)
            total = total.reshape(chunk, 2 * SEQS, LANES)
            total = jnp.where(even, total[:, :SEQS], total[:, SEQS:]).reshape(chunk * SEQS, LANES)
            r = pl.multiple_of(t * SEQS, chunk * SEQS)
            projg_ref[pl.ds(r, chunk * SEQS), :] = (acc_scr[pl.ds(r, chunk * SEQS), :] + total).astype(bf16)
            return 0

        lax.fori_loop(0, steps // chunk, step, 0)


def backward(proj, dt, sig, act, yg, rate, end, skip, hist, rank_t, stepw_t, pick, select):
    steps, _, channels = act.shape
    grid = channels // WIDE
    tile = lambda j: (0, 0, j)
    whole = lambda j: (0, 0)
    flat = pl.BlockSpec((steps, SEQS, WIDE), tile)
    sums = pltpu.VMEM((steps, PAIRS, 2 * SEQS, LANES), bf16)
    return pl.pallas_call(
        backward_kernel,
        grid=(grid,),
        in_specs=[
            pl.BlockSpec((steps * SEQS, LANES), whole),
            flat, flat, flat, flat,
            pl.BlockSpec((STATES, WIDE), lambda j: (0, j)),
            pl.BlockSpec((STATES, SEQS, WIDE), tile),
            pl.BlockSpec((1, WIDE), lambda j: (0, j)),
            pl.BlockSpec(
                (None, len(TILES), steps + 1, PAIRS, 2 * SEQS, LANES), lambda j: (j, 0, 0, 0, 0, 0)
            ),
            pl.BlockSpec((RANK, steps * SEQS), whole),
            pl.BlockSpec((WIDE, LANES), lambda j: (j, 0)),
            pl.BlockSpec(pick.shape, lambda j: (0, 0, 0)),
            pl.BlockSpec(select.shape, whole),
        ],
        out_specs=[
            flat,
            pl.BlockSpec((RANK, WIDE), lambda j: (0, j)),
            pl.BlockSpec((1, WIDE), lambda j: (0, j)),
            pl.BlockSpec((STATES, WIDE), lambda j: (0, j)),
            pl.BlockSpec((steps * SEQS, LANES), whole),
        ],
        out_shape=[
            jax.ShapeDtypeStruct((steps, SEQS, channels), f32),
            jax.ShapeDtypeStruct((RANK, channels), f32),
            jax.ShapeDtypeStruct((1, channels), f32),
            jax.ShapeDtypeStruct((STATES, channels), f32),
            jax.ShapeDtypeStruct((steps * SEQS, LANES), bf16),
        ],
        scratch_shapes=[
            sums,
            pltpu.VMEM((steps, STATES, SEQS, LANES), f32),
            sums, sums,
            pltpu.VMEM((steps, SEQS, WIDE), bf16),
            pltpu.VMEM((steps * SEQS, LANES), f32),
            pltpu.VMEM((STATES, SEQS, WIDE), f32),
            pltpu.VMEM((STATES, SEQS, WIDE), f32),
            pltpu.VMEM((SEQS, WIDE), f32),
        ],
        compiler_params=params(),
        cost_estimate=cost(90),
        name="backward_scan",
    )(proj, dt, sig, act, yg, rate, end, skip, hist, rank_t, stepw_t, pick, select)


def filter_back_kernel(
    mix_ref, act_ref, act_grad_ref, projg_ref, projg_t_ref, sel_t_ref, fw_ref, fb_ref,
    mixgrad_ref, selg_ref, fwg_ref, fbg_ref,
    dv_scr,
):
    steps = act_ref.shape[0]
    chunk = 16
    taps = [fw_ref[k : k + 1, :] for k in range(KERNEL)]
    bias = fb_ref[0:1, :]
    zero = jnp.zeros((HALO, SEQS, WIDE), f32)
    dv_scr[0:HALO] = zero
    dv_scr[steps + HALO :] = zero

    def step(i, sums):
        t = i * chunk
        x = mix_ref[pl.ds(t, chunk + HALO)].astype(bf16).astype(f32)
        v = bias[None] + taps[0][None] * x[1 : 1 + chunk]
        for k in range(1, KERNEL):
            v = v + taps[k][None] * x[1 + k : 1 + k + chunk]
        sig = sigmoid(v)
        r = pl.multiple_of(t * SEQS, chunk * SEQS)
        more = jnp.dot(projg_ref[pl.ds(r, chunk * SEQS), :], sel_t_ref[...], preferred_element_type=f32)
        total = act_grad_ref[pl.ds(t, chunk)] + more.reshape(chunk, SEQS, WIDE)
        dv = total * (sig * (1.0 + v * (1.0 - sig)))
        dv_scr[pl.ds(t + HALO, chunk)] = dv
        new = [sums[0] + jnp.sum(dv, axis=0)]
        for k in range(KERNEL):
            new.append(sums[1 + k] + jnp.sum(dv * x[1 + k : 1 + k + chunk], axis=0))
        return tuple(new)

    sums = lax.fori_loop(
        0, steps // chunk, step, tuple(jnp.zeros((SEQS, WIDE), f32) for _ in range(KERNEL + 1))
    )
    fbg_ref[...] = jnp.sum(sums[0], axis=0, keepdims=True)
    for k in range(KERNEL):
        fwg_ref[k : k + 1, :] = jnp.sum(sums[1 + k], axis=0, keepdims=True)

    def spread(t, count):
        dv = dv_scr[pl.ds(t, count + HALO)]
        out = taps[KERNEL - 1][None] * dv[0:count]
        for k in range(KERNEL - 1):
            s = KERNEL - 1 - k
            out = out + taps[k][None] * dv[s : s + count]
        mixgrad_ref[pl.ds(t, count)] = out.astype(bf16)

    def out_step(i, _):
        spread(i * chunk, chunk)
        return 0

    lax.fori_loop(0, steps // chunk, out_step, 0)
    spread(steps, HALO)
    low = act_ref[...].reshape(steps * SEQS, WIDE).astype(bf16)
    selg_ref[...] = jnp.dot(projg_t_ref[...], low, preferred_element_type=f32)


def filter_back(mixture, act, act_grad, projg, projg_t, sel_t, fw, fb):
    steps, _, channels = act.shape
    grid = channels // WIDE
    wide = lambda j: (0, 0, j)
    whole = lambda j: (0, 0)
    cols = lambda j: (0, j)
    return pl.pallas_call(
        filter_back_kernel,
        grid=(grid,),
        in_specs=[
            pl.BlockSpec((steps + HALO, SEQS, WIDE), wide),
            pl.BlockSpec((steps, SEQS, WIDE), wide),
            pl.BlockSpec((steps, SEQS, WIDE), wide),
            pl.BlockSpec((steps * SEQS, LANES), whole),
            pl.BlockSpec((LANES, steps * SEQS), whole),
            pl.BlockSpec((LANES, WIDE), cols),
            pl.BlockSpec((KERNEL, WIDE), cols),
            pl.BlockSpec((1, WIDE), cols),
        ],
        out_specs=[
            pl.BlockSpec((steps + HALO, SEQS, WIDE), wide),
            pl.BlockSpec((LANES, WIDE), cols),
            pl.BlockSpec((KERNEL, WIDE), cols),
            pl.BlockSpec((1, WIDE), cols),
        ],
        out_shape=[
            jax.ShapeDtypeStruct((steps + HALO, SEQS, channels), bf16),
            jax.ShapeDtypeStruct((LANES, channels), f32),
            jax.ShapeDtypeStruct((KERNEL, channels), f32),
            jax.ShapeDtypeStruct((1, channels), f32),
        ],
        scratch_shapes=[pltpu.VMEM((steps + 2 * HALO, SEQS, WIDE), f32)],
        compiler_params=params(),
        cost_estimate=cost(20),
        name="filter_back",
    )(mixture, act, act_grad, projg, projg_t, sel_t, fw, fb)


def normalized(hidden, norm_gain):
    return hidden * lax.rsqrt(jnp.mean(hidden * hidden, axis=-1, keepdims=True) + 1e-05) * norm_gain


def contract_rows(left_side, right_side):
    return lax.dot_general(
        left_side, right_side, (((0,), (0,)), ((), ())), preferred_element_type=f32
    )


def contract_cols(left_side, right_side):
    return lax.dot_general(
        left_side, right_side, (((1,), (1,)), ((), ())), preferred_element_type=f32
    )


def exchanged(block, axis, distance):
    return lax.ppermute(block, axis, [(i, i ^ distance) for i in range(lax.axis_size(axis))])


def pick_row(block, index, axis=0):
    return lax.dynamic_index_in_dim(block, index, axis, keepdims=False)


def over_cores(blocks):
    blocks = blocks.reshape((-1, 2) + blocks.shape[1:])
    core = lax.axis_index("fsdp") % 2
    got = exchanged(pick_row(blocks, 1 - core, 1), "fsdp", 1)
    return (pick_row(blocks, core, 1).astype(f32) + got.astype(f32)).astype(bf16)


def to_chips(blocks):
    chip = lax.axis_index("fsdp") // 2
    got = [exchanged(pick_row(blocks, chip ^ d), "fsdp", 2 * d) for d in range(1, blocks.shape[0])]
    return pick_row(blocks, chip), got


def summed(own, got):
    total = own.astype(f32)
    for block in got:
        total = total + block.astype(f32)
    return total


def to_replicas(block):
    size, here = lax.axis_size("replica"), lax.axis_index("replica")
    parts = block.astype(bf16).reshape((size, -1) + block.shape[1:])
    own = pick_row(block.reshape(parts.shape), here)
    return own, [exchanged(pick_row(parts, here ^ d), "replica", d) for d in range(1, size)]


def from_replicas(part):
    return [part] + [exchanged(part, "replica", d) for d in range(1, lax.axis_size("replica"))]


def joined(parts):
    here = lax.axis_index("replica")
    parts = jnp.stack(parts)
    return jnp.concatenate([pick_row(parts, here ^ i) for i in range(parts.shape[0])]).astype(f32)


def gathered(block, axis):
    return lax.all_gather(block, "fsdp", axis=axis, tiled=True)


def body(
    prompt_hidden, sequel_hidden, parents, prompt_cotangent, sequel_cotangent,
    norm_gain, input_weight, filter_weight, depthwise_filter_bias, select_weight,
    step_weight, step_bias, decay_log, skip_gain, output_weight,
):
    size, here = lax.axis_size("fsdp"), lax.axis_index("fsdp")
    prompts, steps = prompt_hidden.shape[:2]
    sequels, sequel_len = sequel_hidden.shape[:2]
    split = sequel_len // steps
    assert prompts == PROMPTS and sequels * split == SEQS - prompts
    rim = KERNEL - 1
    half = SEQS // 2
    rows = steps * SEQS

    small = jnp.concatenate(
        [
            filter_weight,
            depthwise_filter_bias[None],
            step_bias[None],
            skip_gain[None],
            decay_log.T,
            step_weight,
            select_weight.T,
            jnp.pad(norm_gain, (0, step_bias.shape[0] - norm_gain.shape[0]))[None],
        ],
        axis=0,
    )
    small = gathered(small, 1)
    at = 0

    def take(count):
        nonlocal at
        at += count
        return small[at - count : at]

    fw = take(KERNEL).astype(f32)
    fb = take(1).astype(f32)
    sbias = take(1).astype(f32)
    skip = take(1).astype(f32)
    rate = -jnp.exp(take(STATES).astype(f32)) * LOG2E
    step_full = take(RANK)
    sel_t = jnp.pad(take(RANK + 2 * STATES), ((0, LANES - RANK - 2 * STATES), (0, 0)))
    gain = take(1).reshape(size, -1)[:, : norm_gain.shape[0]].reshape(-1).astype(f32)
    select_pad = sel_t.T
    step_pad = jnp.pad(step_full, ((0, LANES - RANK), (0, 0)))
    full_output = gathered(output_weight, 0)
    full_input = gathered(input_weight, 0)

    tails = lax.all_gather(prompt_hidden[:, steps - rim :], "fsdp")
    before = jnp.where(here > 0, tails[jnp.maximum(here - 1, 0)], jnp.zeros_like(tails[0]))
    pieces = sequel_hidden.reshape(sequels, split, steps, D)
    inner = jnp.concatenate([tails[size - 1][parents][:, None], pieces[:, :-1, steps - rim :]], axis=1)
    halo = jnp.concatenate([before, inner.reshape(-1, rim, D)], axis=0)
    halo = jnp.pad(halo, ((0, 0), (HALO - rim, 0), (0, 0)))
    hidden = jnp.concatenate([prompt_hidden, sequel_hidden.reshape(-1, steps, D)], axis=0)
    hidden = jnp.swapaxes(jnp.concatenate([halo, hidden], axis=1), 0, 1).reshape(-1, D).astype(f32)
    cot = jnp.concatenate([prompt_cotangent, sequel_cotangent.reshape(-1, steps, D)], axis=0)
    cotangent = jnp.swapaxes(cot, 0, 1).reshape(rows, D)

    gated_grad = contract_cols(cotangent, full_output).reshape(steps, SEQS, INNER)
    scaled = normalized(hidden, gain).astype(bf16)
    mixture = jnp.dot(scaled, full_input, preferred_element_type=f32)
    mixture = mixture.reshape(steps + HALO, SEQS, 2 * INNER)
    act, proj = front(mixture, fw, fb, select_pad, steps)
    groups = 1 if split == 1 else 2
    lane = jnp.arange(2 * STATES * LANES)[None, :]
    select = (jnp.arange(LANES)[:, None] == RANK + lane // LANES).astype(bf16)
    dt, sig, yg, silu, slope, ahead, behind, total = piece(
        proj, act, mixture, gated_grad, step_pad, sbias, rate, select, groups
    )

    ahead = ahead.reshape(groups, -1, STATES, 2, half, LANES).transpose(2, 0, 4, 1, 3, 5)
    ahead = ahead.reshape(STATES, groups * half, INNER)
    one_hot = (parents[:, None] == jnp.arange(PROMPTS, dtype=jnp.int32)[None, :]).astype(f32)
    own = total[half:].reshape(sequels, split, INNER)
    own_behind = behind[:, half:].reshape(STATES, sequels, split, INNER)
    own_decay = jnp.exp2(rate[:, None, None, :] * own[None])
    back = jnp.zeros((STATES, sequels, INNER), f32)
    own_end = []
    for p in range(split - 1, -1, -1):
        own_end.insert(0, back)
        back = own_behind[:, :, p] + (own_decay[:, :, p] * back if p < split - 1 else 0.0)
    branch = jnp.sum(back[:, :, None, :] * one_hot[None, :, :, None], axis=1)
    branch = lax.psum(branch, "fsdp")
    moved = jnp.concatenate([ahead[:, :half], behind[:, :half]], axis=0)
    moved, totals = lax.all_gather((moved, total[:half]), "fsdp")
    decays = jnp.exp2(rate[None, :, None, :] * totals[:, None, :, :])
    state = jnp.zeros_like(branch)
    start = state
    for k in range(size):
        start = jnp.where(here == k, state, start)
        state = decays[k] * state + moved[k, :STATES]
    back = branch
    end = back
    for k in range(size - 1, -1, -1):
        end = jnp.where(here == k, back, end)
        back = decays[k] * back + moved[k, STATES:]
    state = jnp.sum(state[:, None] * one_hot[None, :, :, None], axis=2)
    own_start = [state]
    for p in range(split - 1):
        state = own_decay[:, :, p] * state + ahead[:, half:].reshape(STATES, sequels, split, INNER)[:, :, p]
        own_start.append(state)
    own_start = jnp.stack(own_start, axis=2).reshape(STATES, half, INNER)
    own_end = jnp.stack(own_end, axis=2).reshape(STATES, half, INNER)
    start = jnp.concatenate([start, own_start], axis=1)
    end = jnp.concatenate([end, own_end], axis=1)

    gated, hist, gate_grad, skip_grad = forward(
        proj, dt, act, yg, silu, slope, rate, start, skip, select
    )
    gated = gated.reshape(rows, INNER)
    gate_grad = gate_grad.reshape(rows, INNER)
    after = lax.optimization_barrier
    output_grad = contract_rows(gated, cotangent).astype(bf16).reshape(size, -1, D)
    gate_weight_grad = contract_rows(scaled[HALO * SEQS :], gate_grad).astype(bf16)
    early = [over_cores(output_grad), over_cores(gate_weight_grad.reshape(size, -1, INNER))]
    result = hidden[HALO * SEQS :] + jnp.dot(gated, full_output, preferred_element_type=f32)
    result = jnp.swapaxes(result.reshape(steps, SEQS, D), 0, 1).astype(bf16)
    end, early = after((end, early))
    early = [to_chips(block) for block in early]

    rank_t = proj[:, :RANK].astype(bf16).T
    lane = jnp.arange(LANES)[None, None, :]
    which = jnp.arange(PAIRS)[:, None, None]
    source = jnp.arange(2 * LANES)[None, :, None]
    pick = (lane // 2 == jnp.where(source < LANES, RANK, RANK + STATES) // 2 + which).astype(bf16)
    act_grad, step_grad, bias_grad, decay_grad, projg = backward(
        proj, dt, sig, act, yg, rate, end, skip, hist, rank_t, step_pad.T, pick, select
    )
    projg, early = after((projg, early))
    early = [summed(*block) for block in early]
    projg, early = after((projg, early))
    early = [to_replicas(block) for block in early]
    filter_in_grad, select_grad, filter_grad, filter_bias_grad = filter_back(
        mixture, act, act_grad, projg, projg.T, sel_t, fw, fb
    )
    filter_in_grad, early = after((filter_in_grad, early))
    early = [summed(*block).astype(bf16) for block in early]
    filter_in_grad = filter_in_grad.reshape(-1, INNER)
    filter_weight_grad = contract_rows(scaled, filter_in_grad).astype(bf16)
    late = [over_cores(filter_weight_grad.reshape(size, -1, INNER))]
    early = [from_replicas(block) for block in early]
    scaled_grad = contract_cols(filter_in_grad, full_input[:, :INNER])
    more = contract_cols(gate_grad, full_input[:, INNER:])
    scaled_grad = scaled_grad + jnp.pad(more, ((HALO * SEQS, 0), (0, 0)))
    unused_norm, norm_back = jax.vjp(normalized, hidden, gain)
    hidden_grad, gain_grad = norm_back(scaled_grad)
    hidden_grad = jnp.swapaxes(hidden_grad.reshape(steps + HALO, SEQS, D), 0, 1)
    main = hidden_grad[:, HALO:]
    extra = hidden_grad[:, HALO - rim : HALO]
    own_extra = extra[half:].reshape(sequels, split, rim, D)
    child = jnp.einsum("sp,srd->prd", one_hot, own_extra[:, 0], precision=lax.Precision.HIGHEST)
    shared = lax.all_gather(jnp.stack([extra[:half], child]), "fsdp")
    following = jnp.where(
        here < size - 1, shared[jnp.minimum(here + 1, size - 1), 0], jnp.sum(shared[:, 1], axis=0)
    )
    own_following = jnp.pad(own_extra[:, 1:], ((0, 0), (0, 1), (0, 0), (0, 0))).reshape(half, rim, D)
    tail = jnp.concatenate([following, own_following], axis=0)
    main = main + jnp.pad(tail, ((0, 0), (steps - rim, 0), (0, 0))) + cot.astype(f32)

    small_grad = jnp.concatenate(
        [
            filter_grad,
            filter_bias_grad,
            bias_grad,
            skip_grad,
            decay_grad,
            step_grad,
            select_grad[: RANK + 2 * STATES],
            jnp.pad(gain_grad.reshape(size, -1), ((0, 0), (0, (INNER - D) // size))).reshape(1, -1),
            jnp.zeros((8, INNER), f32),
        ],
        axis=0,
    )
    small_grad = jnp.swapaxes(small_grad.astype(bf16).reshape(small_grad.shape[0], size, -1), 0, 1)
    late = late + [over_cores(small_grad)]
    late = [summed(*to_chips(block)) for block in late]
    late = [summed(*to_replicas(block)).astype(bf16) for block in late]
    filter_weight_grad, small_grad = [joined(from_replicas(block)) for block in late]
    output_grad, gate_weight_grad = [joined(block) for block in early]
    input_grad = jnp.concatenate([filter_weight_grad, gate_weight_grad], axis=1)
    at = 0
    taken = []
    for count in (KERNEL, 1, 1, 1, STATES, RANK, RANK + 2 * STATES, 1):
        taken.append(small_grad[at : at + count])
        at += count
    g_filter, g_fbias, g_sbias, g_skip, g_decay, g_step, g_select, g_gain = taken
    return (
        result[:half],
        result[half:].reshape(sequel_hidden.shape),
        main[:half],
        main[half:].reshape(sequel_hidden.shape),
        g_gain[0, : norm_gain.shape[0]],
        input_grad,
        g_filter,
        g_fbias[0],
        g_select.T,
        g_step,
        g_sbias[0],
        g_decay.T,
        g_skip[0],
        output_grad,
    )


def solution(mesh):
    rows = P("replica", "fsdp", None)
    own = P(("replica", "fsdp"), None, None)
    return jax.shard_map(
        body,
        mesh=mesh,
        in_specs=(
            rows, own, P(("replica", "fsdp")), rows, own,
            P("fsdp"), P("fsdp", None), P(None, "fsdp"), P("fsdp"), P("fsdp", None),
            P(None, "fsdp"), P("fsdp"), P("fsdp", None), P("fsdp"), P("fsdp", None),
        ),
        out_specs=(
            rows, own, rows, own,
            P("fsdp"), P("fsdp", None), P(None, "fsdp"), P("fsdp"), P("fsdp", None),
            P(None, "fsdp"), P("fsdp"), P("fsdp", None), P("fsdp"), P("fsdp", None),
        ),
        check_vma=False,
    )
```

profile of v0, /device:TPU:0, one launch (start us, length us, event | category | flops | bytes accessed | tf_op | source)
XLA Modules:
  0.0 698.6 jit_solution(13410931215647418774)
XLA Ops:
  14.6 18.8 %all_gather.35 = bf16[184,2048]{1,0:T(8,128)(2,1)S(1)} all-gather(bf16[184,256]{1,0:T(8,128)(2,1)S(1)} %concatenate.69), channel_id=1, replica_groups=mesh['replica'=4,'fsdp'=8] {'fsdp'}, dimensions={1}, use_global_device_ids=true | all-gather | bytes 847872 | tf_op jit(solution)/shard_map/all_gather | solution.py:727
  35.9 10.0 %all-gather = bf16[32,3,1024]{2,1,0:T(4,128)(2,1)S(1)} all-gather(bf16[4,3,1024]{2,1,0:T(4,128)(2,1)S(1)} %slice.194), channel_id=2, replica_groups=mesh['replica'=4,'fsdp'=8] {'fsdp'}, dimensions={0}, use_global_device_ids=true | all-gather | bytes 221184 | tf_op jit(solution)/shard_map/all_gather | solution.py:778
  63.9 11.3 %fusion.20.gg_ref = f32[128,8,2048]{2,1,0:T(8,128)} fusion(bf16[2048,1024]{1,0:T(8,128)(2,1)} %all-gather.11.cloned.1.call-done, bf16[128,8,1024]{2,0,1:T(8,128)(2,1)} %bitcast.9), kind=kOutput, calls=%fused_computation.38 | convolution fusion | flops 4294967296 | bytes 14680064 | tf_op jit(solution)/shard_map/dot_general | solution.py:676
  75.2 35.2 %all-gather.9.cloned.1.call-done = bf16[1024,4096]{1,0:T(8,128)(2,1)} async-done(((bf16[128,4096]{1,0:T(8,128)(2,1)}), bf16[1024,4096]{1,0:T(8,128)(2,1)}) %all-gather.9.cloned.1.call-update) | async-done | bytes 8388624 | tf_op jit(solution)/shard_map/all_gather | solution.py:727
  110.5 17.7 %fusion.mix_ref.gate_ref = f32[132,8,4096]{2,1,0:T(8,128)} fusion(bf16[1024,4096]{1,0:T(8,128)(2,1)} %all-gather.9.cloned.1.call-done, bf16[132,8,1024]{2,0,1:T(8,128)(2,1)S(1)} %copy-done.16), kind=kOutput, calls=%fused_computation.3 | convolution fusion | flops 8858370048 | bytes 27852800 | tf_op jit(solution)/shard_map/dot_general | solution.py:791
  128.1 16.1 %front.1 = (f32[128,8,2048]{2,1,0:T(8,128)}, f32[1024,128]{1,0:T(8,128)}) custom-call(f32[132,8,4096]{2,1,0:T(8,128)} %fusion.mix_ref.gate_ref, f32[4,2048]{1,0:T(4,128)} %slice_convert_fusion.2.fw_ref, f32[1,2048]{1,0:T(1,128)} %get-tuple-element.141.fb_ref, bf16[2048,128]{1,0:T(8,128)(2,1)} %copy.167.sel_ref), custom_call_target="tpu_custom_call" | custom-call | flops 16000000000 | tf_op jit(solution)/shard_map/front/pallas_call | solution.py:75
  144.2 64.6 %piece.1 = (f32[128,8,2048]{2,1,0:T(8,128)}, bf16[128,8,2048]{2,1,0:T(8,128)(2,1)}, f32[128,8,2048]{2,1,0:T(8,128)}, bf16[128,8,2048]{2,1,0:T(8,128)(2,1)}, bf16...) custom-call(f32[1024,128]{1,0:T(8,128)} %get-tuple-element.61.proj_ref, ...), custom_call_target="tpu_custom_call" | custom-call | flops 60000002048 | tf_op jit(solution)/shard_map/piece/pallas_call | solution.py:272
  223.9 7.4 %bitcast_multiply_fusion.2 = f32[1056,1024]{1,0:T(8,128)} fusion(f32[132,8,1024]{2,0,1:T(8,128)} %copy-done, f32[1056]{0:T(1024)S(1)} %rsqrt.15), kind=kLoop, calls=%fused_computation.17 | loop fusion | flops 1081344 | bytes 8654976 | tf_op jit(solution)/shard_map/mul | solution.py:666
  231.9 22.7 %all-gather.4 = f32[8,4,2048]{2,1,0:T(4,128)S(1)} all-gather(f32[1,4,2048]{2,1,0:T(4,128)S(1)} %slice_bitcast_fusion.23), channel_id=3, replica_groups=mesh['replica'=4,'fsdp'=8] {'fsdp'}, dimensions={0}, use_global_device_ids=true | all-gather | bytes 294912 | tf_op jit(solution)/shard_map/all_gather | solution.py:815
  258.5 13.0 %all-gather.13.cloned.1.call-done = f32[256,4,2048]{2,1,0:T(4,128)} async-done(((f32[32,4,2048]{2,1,0:T(4,128)}), f32[256,4,2048]{2,1,0:T(4,128)}) %all-gather.13.cloned.1.call-update) | async-done | bytes 8388624 | tf_op jit(solution)/shard_map/all_gather | solution.py:815
  283.0 51.3 %forward_scan.1 = (bf16[128,8,2048]{2,1,0:T(8,128)(2,1)}, bf16[8,2,129,8,16,128]{5,4,3,2,1,0:T(8,128)(2,1)}, bf16[128,8,2048]{2,1,0:T(8,128)(2,1)}, f32[1,2048]{1,0:T(1,128)}) custom-call(f32[1024,128]{1,0:T(8,128)} %get-tuple-element.61.proj_ref, f32[128,8,2048]{2,1,0:T(8,128)} %get-tuple-element.63.dt_ref, f32[128,8,2048]{2,1,0:T(8,128)} %get-tuple-element.62.act_ref, ...), custom_call_target="tpu_custom_call" | custom-call | flops 49999998976 | tf_op jit(solution)/shard_map/forward_scan/pallas_call | solution.py:369
  334.3 8.0 %fusion.25 = bf16[1024,2048]{1,0:T(8,128)(2,1)S(1)} fusion(bf16[128,8,2048]{2,1,0:T(8,128)(2,1)} %get-tuple-element.72, f32[1056,1024]{1,0:T(8,128)} %bitcast_multiply_fusion.2, f32[1024]{0:T(1024)S(1)} %copy-done.34), kind=kOutput, calls=%fused_computation.43 | convolution fusion | flops 4299161600 | bytes 12587008 | tf_op jit(solution)/shard_map/dot_general | solution.py:670
  346.9 6.7 bitcast_convert_fusion.1
  358.0 9.5 %fusion.29 = bf16[128,8,1024]{2,1,0:T(8,128)(2,1)S(1)} fusion(f32[128,8,1024]{2,0,1:T(8,128)S(1)} %copy-done.15, bf16[2048,1024]{1,0:T(8,128)(2,1)} %all-gather.11.cloned.1.call-done, bf16[128,8,2048]{2,1,0:T(8,128)(2,1)S(1)} %copy-done.46), kind=kOutput, calls=%fused_computation.46 | convolution fusion | flops 4297064448 | bytes 14680064 | tf_op jit(solution)/shard_map/dot_general | solution.py:846
  367.6 6.5 fusion.8
  375.8 5.1 fusion.41
  398.1 6.5 collective-permute-done.4
  406.0 90.9 %backward_scan.1 = (f32[128,8,2048]{2,1,0:T(8,128)}, f32[64,2048]{1,0:T(8,128)}, f32[1,2048]{1,0:T(1,128)}, f32[16,2048]{1,0:T(8,128)}, bf16[1024,128]{1,0:T(8,128)(2,1)}) custom-call(f32[1024,128]{1,0:T(8,128)} %get-tuple-element.61.proj_ref, f32[128,8,2048]{2,1,0:T(8,128)} %get-tuple-element.63.dt_ref, bf16[128,8,2048]{2,1,0:T(8,128)(2,1)} %get-tuple-element.71.sig_ref, ...), custom_call_target="tpu_custom_call" | custom-call | flops 89999998976 | tf_op jit(solution)/shard_map/backward_scan/pallas_call | solution.py:525
  507.1 3.3 collective-permute-start.10
  512.3 3.3 collective-permute-start.13
  515.6 20.8 %filter_back.1 = (bf16[132,8,2048]{2,1,0:T(8,128)(2,1)}, f32[128,2048]{1,0:T(8,128)}, f32[4,2048]{1,0:T(4,128)}, f32[1,2048]{1,0:T(1,128)}) custom-call(f32[132,8,4096]{2,1,0:T(8,128)} %fusion.mix_ref.gate_ref, f32[128,8,2048]{2,1,0:T(8,128)} %get-tuple-element.62.act_ref, f32[128,8,2048]{2,1,0:T(8,128)} %get-tuple-element.75.act_grad_ref, ...), custom_call_target="tpu_custom_call" | custom-call | flops 20000000000 | tf_op jit(solution)/shard_map/filter_back/pallas_call | solution.py:633
  543.6 3.3 collective-permute-start.36
  549.9 3.3 collective-permute-start.39
  553.2 15.6 %bitcast_convert_fusion = bf16[1024,2048]{1,0:T(8,128)(2,1)S(1)} fusion(bf16[132,8,2048]{2,1,0:T(8,128)(2,1)} %get-tuple-element.92, f32[1024]{0:T(1024)S(1)} %copy-done.35, f32[132,8]{0,1:T(8,128)S(1)} %copy-done.37, bf16[4,128,1024]{2,1,0:T(8,128)(2,1)S(1)} %copy-done.7, bf16[4,128,1024]{2,1,0:T(8,128)(2,1)S(1)} %copy-done.4, ...), kind=kOutput, calls=%fused_computation.1 | convolution fusion | flops 4441014272 | bytes 10690688 | tf_op jit(solution)/shard_map/dot_general | solution.py:670
  572.1 11.3 %multiply_reduce_fusion.1 = (bf16[1024]{0:T(1024)(128)(2,1)S(1)}, f32[1056]{0:T(1024)S(1)}, f32[1056,1024]{1,0:T(8,128)S(1)}) fusion(f32[1024]{0:T(1024)S(1)} %copy-done.35, f32[132,8,1024]{2,0,1:T(8,128)} %copy-done, f32[1024,1024]{1,0:T(8,128)S(1)} %copy-done.45, bf16[1024,4096]{1,0:T(8,128)(2,1)} %all-gather.9.cloned.1.call-done, ...), kind=kOutput, calls=%fused_computation.19 | convolution fusion | flops 4436752384 | bytes 21510400 | tf_op jit(solution)/shard_map/dot_general | solution.py:676
  589.4 9.7 %all-gather.3 = f32[16,4,3,1024]{3,1,2,0:T(4,128)S(1)} all-gather(f32[2,4,3,1024]{3,1,2,0:T(4,128)S(1)} %copy.185), channel_id=5, replica_groups=mesh['replica'=4,'fsdp'=8] {'fsdp'}, dimensions={0}, use_global_device_ids=true | all-gather | bytes 884736 | tf_op jit(solution)/shard_map/all_gather | solution.py:882
  605.7 4.1 concatenate.83
  612.3 5.9 collective-permute-done.38
  645.2 10.6 %collective-permute-done.25 = bf16[128,2048]{1,0:T(8,128)(2,1)S(1)} collective-permute-done((bf16[128,2048]{1,0:T(8,128)(2,1)S(1)}, bf16[128,2048]{1,0:T(8,128)(2,1)S(1)}, u32[]{:S(2)}, u32[]{:S(2)}) %collective-permute-start.25) | collective-permute-done | bytes 524320 | tf_op jit(solution)/shard_map/ppermute | solution.py:682
  655.8 6.8 collective-permute-done.27
  672.4 7.2 %collective-permute-done.29 = bf16[32,2048]{1,0:T(8,128)(2,1)S(1)} collective-permute-done((bf16[32,2048]{1,0:T(8,128)(2,1)S(1)}, bf16[32,2048]{1,0:T(8,128)(2,1)S(1)}, u32[]{:S(2)}, u32[]{:S(2)}) %collective-permute-start.29) | collective-permute-done | bytes 131104 | tf_op jit(solution)/shard_map/ppermute | solution.py:682
  679.7 4.1 collective-permute-start.33
  (323 shorter events, 172.5 us)
Async XLA Ops:
  7.2 56.7 %all-gather.11.cloned.1.call-start = ((), (), s32[]{:S(2)}) async-start(), calls=%async_computation.1 | async-start | bytes 4718592 | tf_op jit(solution)/shard_map/all_gather | solution.py:727
  7.9 102.5 %all-gather.9.cloned.1.call-start = ((), (), s32[]{:S(2)}) async-start(), calls=%async_computation | async-start | bytes 9437184 | tf_op jit(solution)/shard_map/all_gather | solution.py:727
  8.7 262.8 %all-gather.13.cloned.1.call-start = ((), (), s32[]{:S(2)}) async-start(), calls=%async_computation.3 | async-start | bytes 9437184 | tf_op jit(solution)/shard_map/all_gather | solution.py:815
  215.9 159.9 %all-reduce.11.cloned.1.call-start = ((), (), s32[]{:S(2)}) async-start(), calls=%async_computation.2 | async-start | bytes 1048576 | tf_op jit(solution)/shard_map/psum | solution.py:813
  346.0 36.1 %collective-permute-start.1 = (bf16[4,128,2048]{2,1,0:T(8,128)(2,1)}, bf16[4,128,2048]{2,1,0:T(8,128)(2,1)}, u32[]{:S(2)}, u32[]{:S(2)}) collective-permute-start(bf16[4,128,2048]{2,1,0:T(8,128)(2,1)} %dynamic-slice_bitcast_fusion.1), channel_id=1, source_target_pairs={{0,1},{1,0},{2,3},{3,2},{4,5},{5,4},{6,7},{7,6},{8,9},{9,8},{10,11... | collective-permute-start | bytes 6291464 | tf_op jit(solution)/shard_map/ppermute | solution.py:682
  355.1 29.8 %collective-permute-start = (bf16[4,256,1024]{2,1,0:T(8,128)(2,1)}, bf16[4,256,1024]{2,1,0:T(8,128)(2,1)}, u32[]{:S(2)}, u32[]{:S(2)}) collective-permute-start(bf16[4,256,1024]{2,1,0:T(8,128)(2,1)} %dynamic-slice_bitcast_fusion.2), channel_id=1, source_target_pairs={{0,1},{1,0},{2,3},{3,2},{4,5},{5,4},{6,7},{7,6},{8,9},{9,8},{10,11... | collective-permute-start | bytes 6291464 | tf_op jit(solution)/shard_map/ppermute | solution.py:682
  388.7 15.8 %collective-permute-start.4 = (bf16[256,1024]{1,0:T(8,128)(2,1)S(1)}, bf16[256,1024]{1,0:T(8,128)(2,1)}, u32[]{:S(2)}, u32[]{:S(2)}) collective-permute-start(bf16[256,1024]{1,0:T(8,128)(2,1)S(1)} %get-tuple-element.131), channel_id=1, source_target_pairs={{0,6},{1,7},{2,4},{3,5},{4,2},{5,3},{6,0},{7,1},{8,14},{9,15},{10,... | collective-permute-start | bytes 1572872 | tf_op jit(solution)/shard_map/ppermute | solution.py:682
  391.8 109.1 %collective-permute-start.3 = (bf16[256,1024]{1,0:T(8,128)(2,1)}, bf16[256,1024]{1,0:T(8,128)(2,1)S(1)}, u32[]{:S(2)}, u32[]{:S(2)}) collective-permute-start(bf16[256,1024]{1,0:T(8,128)(2,1)} %get-tuple-element.132), channel_id=1, source_target_pairs={{0,4},{1,5},{2,6},{3,7},{4,0},{5,1},{6,2},{7,3},{8,12},{9,13},{10,... | collective-permute-start | bytes 1572872 | tf_op jit(solution)/shard_map/ppermute | solution.py:682
  393.2 107.7 %collective-permute-start.2 = (bf16[256,1024]{1,0:T(8,128)(2,1)}, bf16[256,1024]{1,0:T(8,128)(2,1)S(1)}, u32[]{:S(2)}, u32[]{:S(2)}) collective-permute-start(bf16[256,1024]{1,0:T(8,128)(2,1)} %get-tuple-element.133), channel_id=1, source_target_pairs={{0,2},{1,3},{2,0},{3,1},{4,6},{5,7},{6,4},{7,5},{8,10},{9,11},{10,... | collective-permute-start | bytes 1572872 | tf_op jit(solution)/shard_map/ppermute | solution.py:682
  395.2 105.8 %collective-permute-start.7 = (bf16[128,2048]{1,0:T(8,128)(2,1)}, bf16[128,2048]{1,0:T(8,128)(2,1)}, u32[]{:S(2)}, u32[]{:S(2)}) collective-permute-start(bf16[128,2048]{1,0:T(8,128)(2,1)} %get-tuple-element.127), channel_id=1, source_target_pairs={{0,6},{1,7},{2,4},{3,5},{4,2},{5,3},{6,0},{7,1},{8,14},{9,15},{10,... | collective-permute-start | bytes 1572872 | tf_op jit(solution)/shard_map/ppermute | solution.py:682
  396.6 104.3 %collective-permute-start.6 = (bf16[128,2048]{1,0:T(8,128)(2,1)}, bf16[128,2048]{1,0:T(8,128)(2,1)}, u32[]{:S(2)}, u32[]{:S(2)}) collective-permute-start(bf16[128,2048]{1,0:T(8,128)(2,1)} %get-tuple-element.128), channel_id=1, source_target_pairs={{0,4},{1,5},{2,6},{3,7},{4,0},{5,1},{6,2},{7,3},{8,12},{9,13},{10,... | collective-permute-start | bytes 1572872 | tf_op jit(solution)/shard_map/ppermute | solution.py:682
  404.5 96.4 %collective-permute-start.5 = (bf16[128,2048]{1,0:T(8,128)(2,1)}, bf16[128,2048]{1,0:T(8,128)(2,1)}, u32[]{:S(2)}, u32[]{:S(2)}) collective-permute-start(bf16[128,2048]{1,0:T(8,128)(2,1)} %get-tuple-element.129), channel_id=1, source_target_pairs={{0,2},{1,3},{2,0},{3,1},{4,6},{5,7},{6,4},{7,5},{8,10},{9,11},{10,... | collective-permute-start | bytes 1572872 | tf_op jit(solution)/shard_map/ppermute | solution.py:682
  507.1 29.4 %collective-permute-start.10 = (bf16[64,1024]{1,0:T(8,128)(2,1)S(1)}, bf16[64,1024]{1,0:T(8,128)(2,1)S(1)}, u32[]{:S(2)}, u32[]{:S(2)}) collective-permute-start(bf16[64,1024]{1,0:T(8,128)(2,1)S(1)} %get-tuple-element.161), channel_id=1, source_target_pairs={{0,24},{8,16},{16,8},{24,0},{1,25},{9,17},{17,9},{25,1},{2,26},{10... | collective-permute-start | bytes 393224 | tf_op jit(solution)/shard_map/ppermute | solution.py:682
  510.4 31.5 %collective-permute-start.9 = (bf16[64,1024]{1,0:T(8,128)(2,1)}, bf16[64,1024]{1,0:T(8,128)(2,1)}, u32[]{:S(2)}, u32[]{:S(2)}) collective-permute-start(bf16[64,1024]{1,0:T(8,128)(2,1)} %get-tuple-element.162), channel_id=1, source_target_pairs={{0,16},{8,24},{16,0},{24,8},{1,17},{9,25},{17,1},{25,9},{2,18},{10... | collective-permute-start | bytes 393224 | tf_op jit(solution)/shard_map/ppermute | solution.py:682
  510.4 31.5 %collective-permute-start.8 = (bf16[64,1024]{1,0:T(8,128)(2,1)}, bf16[64,1024]{1,0:T(8,128)(2,1)}, u32[]{:S(2)}, u32[]{:S(2)}) collective-permute-start(bf16[64,1024]{1,0:T(8,128)(2,1)} %get-tuple-element.163), channel_id=1, source_target_pairs={{0,8},{8,0},{16,24},{24,16},{1,9},{9,1},{17,25},{25,17},{2,10},{10... | collective-permute-start | bytes 393224 | tf_op jit(solution)/shard_map/ppermute | solution.py:682
  512.3 29.6 %collective-permute-start.13 = (bf16[32,2048]{1,0:T(8,128)(2,1)}, bf16[32,2048]{1,0:T(8,128)(2,1)}, u32[]{:S(2)}, u32[]{:S(2)}) collective-permute-start(bf16[32,2048]{1,0:T(8,128)(2,1)} %get-tuple-element.158), channel_id=1, source_target_pairs={{0,24},{8,16},{16,8},{24,0},{1,25},{9,17},{17,9},{25,1},{2,26},{10... | collective-permute-start | bytes 393224 | tf_op jit(solution)/shard_map/ppermute | solution.py:682
  515.6 26.3 %collective-permute-start.12 = (bf16[32,2048]{1,0:T(8,128)(2,1)}, bf16[32,2048]{1,0:T(8,128)(2,1)}, u32[]{:S(2)}, u32[]{:S(2)}) collective-permute-start(bf16[32,2048]{1,0:T(8,128)(2,1)} %get-tuple-element.159), channel_id=1, source_target_pairs={{0,16},{8,24},{16,0},{24,8},{1,17},{9,25},{17,1},{25,9},{2,18},{10... | collective-permute-start | bytes 393224 | tf_op jit(solution)/shard_map/ppermute | solution.py:682
  543.6 66.2 %collective-permute-start.36 = (bf16[32,2048]{1,0:T(8,128)(2,1)}, bf16[32,2048]{1,0:T(8,128)(2,1)}, u32[]{:S(2)}, u32[]{:S(2)}) collective-permute-start(bf16[32,2048]{1,0:T(8,128)(2,1)} %add_convert_fusion.1), channel_id=1, source_target_pairs={{0,24},{8,16},{16,8},{24,0},{1,25},{9,17},{17,9},{25,1},{2,26},{10... | collective-permute-start | bytes 393224 | tf_op jit(solution)/shard_map/ppermute | solution.py:682
  547.0 63.0 %collective-permute-start.35 = (bf16[32,2048]{1,0:T(8,128)(2,1)}, bf16[32,2048]{1,0:T(8,128)(2,1)}, u32[]{:S(2)}, u32[]{:S(2)}) collective-permute-start(bf16[32,2048]{1,0:T(8,128)(2,1)} %add_convert_fusion.1), channel_id=1, source_target_pairs={{0,16},{8,24},{16,0},{24,8},{1,17},{9,25},{17,1},{25,9},{2,18},{10... | collective-permute-start | bytes 393224 | tf_op jit(solution)/shard_map/ppermute | solution.py:682
  547.0 64.0 %collective-permute-start.34 = (bf16[32,2048]{1,0:T(8,128)(2,1)}, bf16[32,2048]{1,0:T(8,128)(2,1)}, u32[]{:S(2)}, u32[]{:S(2)}) collective-permute-start(bf16[32,2048]{1,0:T(8,128)(2,1)} %add_convert_fusion.1), channel_id=1, source_target_pairs={{0,8},{8,0},{16,24},{24,16},{1,9},{9,1},{17,25},{25,17},{2,10},{10... | collective-permute-start | bytes 393224 | tf_op jit(solution)/shard_map/ppermute | solution.py:682
  549.9 62.5 %collective-permute-start.39 = (bf16[64,1024]{1,0:T(8,128)(2,1)}, bf16[64,1024]{1,0:T(8,128)(2,1)}, u32[]{:S(2)}, u32[]{:S(2)}) collective-permute-start(bf16[64,1024]{1,0:T(8,128)(2,1)} %add_convert_fusion), channel_id=1, source_target_pairs={{0,24},{8,16},{16,8},{24,0},{1,25},{9,17},{17,9},{25,1},{2,26},{10... | collective-permute-start | bytes 393224 | tf_op jit(solution)/shard_map/ppermute | solution.py:682
  572.0 67.8 %collective-permute-start.24 = (bf16[4,128,2048]{2,1,0:T(8,128)(2,1)}, bf16[4,128,2048]{2,1,0:T(8,128)(2,1)S(1)}, u32[]{:S(2)}, u32[]{:S(2)}) collective-permute-start(bf16[4,128,2048]{2,1,0:T(8,128)(2,1)} %dynamic-slice_bitcast_fusion), channel_id=1, source_target_pairs={{0,1},{1,0},{2,3},{3,2},{4,5},{5,4},{6,7},{7,6},{8,9},{9,8},{10,11... | collective-permute-start | bytes 6291464 | tf_op jit(solution)/shard_map/ppermute | solution.py:682
  609.8 8.4 %collective-permute-start.38 = (bf16[64,1024]{1,0:T(8,128)(2,1)}, bf16[64,1024]{1,0:T(8,128)(2,1)S(1)}, u32[]{:S(2)}, u32[]{:S(2)}) collective-permute-start(bf16[64,1024]{1,0:T(8,128)(2,1)} %add_convert_fusion), channel_id=1, source_target_pairs={{0,16},{8,24},{16,0},{24,8},{1,17},{9,25},{17,1},{25,9},{2,18},{10... | collective-permute-start | bytes 393224 | tf_op jit(solution)/shard_map/ppermute | solution.py:682
  609.9 8.8 %collective-permute-start.37 = (bf16[64,1024]{1,0:T(8,128)(2,1)}, bf16[64,1024]{1,0:T(8,128)(2,1)S(1)}, u32[]{:S(2)}, u32[]{:S(2)}) collective-permute-start(bf16[64,1024]{1,0:T(8,128)(2,1)} %add_convert_fusion), channel_id=1, source_target_pairs={{0,8},{8,0},{16,24},{24,16},{1,9},{9,1},{17,25},{25,17},{2,10},{10... | collective-permute-start | bytes 393224 | tf_op jit(solution)/shard_map/ppermute | solution.py:682
  611.0 8.9 %collective-permute-start.14 = (bf16[4,192,256]{2,1,0:T(8,128)(2,1)S(1)}, bf16[4,192,256]{2,1,0:T(8,128)(2,1)S(1)}, u32[]{:S(2)}, u32[]{:S(2)}) collective-permute-start(bf16[4,192,256]{2,1,0:T(8,128)(2,1)S(1)} %dynamic-slice_bitcast_fusion.14), channel_id=1, source_target_pairs={{0,1},{1,0},{2,3},{3,2},{4,5},{5,4},{6,7},{7,6},{8,9},{9,8},{10,11... | collective-permute-start | bytes 1179656 | tf_op jit(solution)/shard_map/ppermute | solution.py:682
  635.4 7.6 %collective-permute-start.23 = (bf16[48,256]{1,0:T(8,128)(2,1)S(1)}, bf16[48,256]{1,0:T(8,128)(2,1)S(1)}, u32[]{:S(2)}, u32[]{:S(2)}) collective-permute-start(bf16[48,256]{1,0:T(8,128)(2,1)S(1)} %fusion.67), channel_id=1, source_target_pairs={{0,24},{8,16},{16,8},{24,0},{1,25},{9,17},{17,9},{25,1},{2,26},{10... | collective-permute-start | bytes 73736 | tf_op jit(solution)/shard_map/ppermute | solution.py:682
  640.9 14.9 %collective-permute-start.25 = (bf16[128,2048]{1,0:T(8,128)(2,1)S(1)}, bf16[128,2048]{1,0:T(8,128)(2,1)S(1)}, u32[]{:S(2)}, u32[]{:S(2)}) collective-permute-start(bf16[128,2048]{1,0:T(8,128)(2,1)S(1)} %get-tuple-element.124), channel_id=1, source_target_pairs={{0,2},{1,3},{2,0},{3,1},{4,6},{5,7},{6,4},{7,5},{8,10},{9,11},{10,... | collective-permute-start | bytes 1572872 | tf_op jit(solution)/shard_map/ppermute | solution.py:682
  641.5 21.0 %collective-permute-start.27 = (bf16[128,2048]{1,0:T(8,128)(2,1)S(1)}, bf16[128,2048]{1,0:T(8,128)(2,1)S(1)}, u32[]{:S(2)}, u32[]{:S(2)}) collective-permute-start(bf16[128,2048]{1,0:T(8,128)(2,1)S(1)} %get-tuple-element.125), channel_id=1, source_target_pairs={{0,6},{1,7},{2,4},{3,5},{4,2},{5,3},{6,0},{7,1},{8,14},{9,15},{10,... | collective-permute-start | bytes 1572872 | tf_op jit(solution)/shard_map/ppermute | solution.py:682
  643.0 20.9 %collective-permute-start.26 = (bf16[128,2048]{1,0:T(8,128)(2,1)S(1)}, bf16[128,2048]{1,0:T(8,128)(2,1)S(1)}, u32[]{:S(2)}, u32[]{:S(2)}) collective-permute-start(bf16[128,2048]{1,0:T(8,128)(2,1)S(1)} %get-tuple-element.126), channel_id=1, source_target_pairs={{0,4},{1,5},{2,6},{3,7},{4,0},{5,1},{6,2},{7,3},{8,12},{9,13},{10,... | collective-permute-start | bytes 1572872 | tf_op jit(solution)/shard_map/ppermute | solution.py:682
  665.5 6.9 collective-permute-start.30
  667.9 11.7 %collective-permute-start.29 = (bf16[32,2048]{1,0:T(8,128)(2,1)S(1)}, bf16[32,2048]{1,0:T(8,128)(2,1)S(1)}, u32[]{:S(2)}, u32[]{:S(2)}) collective-permute-start(bf16[32,2048]{1,0:T(8,128)(2,1)S(1)} %get-tuple-element.153), channel_id=1, source_target_pairs={{0,16},{8,24},{16,0},{24,8},{1,17},{9,25},{17,1},{25,9},{2,18},{10... | collective-permute-start | bytes 393224 | tf_op jit(solution)/shard_map/ppermute | solution.py:682
  679.7 7.1 %collective-permute-start.33 = (bf16[32,2048]{1,0:T(8,128)(2,1)S(1)}, bf16[32,2048]{1,0:T(8,128)(2,1)S(1)}, u32[]{:S(2)}, u32[]{:S(2)}) collective-permute-start(bf16[32,2048]{1,0:T(8,128)(2,1)S(1)} %fusion.58), channel_id=1, source_target_pairs={{0,24},{8,16},{16,8},{24,0},{1,25},{9,17},{17,9},{25,1},{2,26},{10... | collective-permute-start | bytes 393224 | tf_op jit(solution)/shard_map/ppermute | solution.py:682
  (65 other events, 718.7 us)
Sparse Core Ops, SparseCore 0:
  9.9 44.2 all-gather.10
  56.0 54.3 all-gather.8
  216.0 55.4 all-gather.12
  281.6 54.5 all-reduce.10
where the time goes:
time: 707 us; the launch traced here: 699 us
  Pallas kernels  244 us (35%)
  waiting for transfers between devices  103 us (15%)
  matrix products  86.9 us (12%)
  other arithmetic  70.6 us (10%)
  local copies, waits for them, and re-layouts  68.6 us (10%)
  blocking collectives  61.2 us (9%)
  starting transfers between devices  49.8 us (7%)
  between operations  15.3 us (2%)
    pallas_call x1, Pallas kernels, backward(): pl.pallas_call(backward_kernel, grid=(grid,), in_specs=[pl.BlockSpec((ste...  90.9 us
    pallas_call x1, Pallas kernels, piece(): pl.pallas_call(piece_kernel, grid=(grid,), in_specs=[pl.BlockSpec((steps...  64.6 us
    ppermute x40, waiting for transfers between devices, exchanged(): lax.ppermute(block, axis, [(i, i ^ distance) for i in range(lax.axis_size...  53 us
    pallas_call x1, Pallas kernels, forward(): pl.pallas_call(forward_kernel, grid=(grid,), in_specs=[pl.BlockSpec((step...  51.3 us
    ppermute x40, starting transfers between devices, exchanged(): lax.ppermute(block, axis, [(i, i ^ distance) for i in range(lax.axis_size...  49.7 us
    all_gather x2, waiting for transfers between devices, gathered(): return lax.all_gather(block, 'fsdp', axis=axis, tiled=True)  35.2 us
    dot_general x3, matrix products, contract_rows(): lax.dot_general(left_side, right_side, (((0,), (0,)), ((), ())), preferre...  30.4 us
    dot_general x3, matrix products, contract_cols(): lax.dot_general(left_side, right_side, (((1,), (1,)), ((), ())), preferre...  29.2 us
  transfers between devices with their start and end apart: 44, of which 19 were waited for; matrix products, arithmetic and copies ran while one was open for 24% of the time, Pallas kernels for 23%

commit v1 on v0

--- a/solution.py
+++ b/solution.py
@@ -43,6 +43,130 @@
     return jnp.maximum(x, 0.0) + jnp.log1p(jnp.exp(-jnp.abs(x)))
 
 
+def scale_of(rows):
+    return lax.rsqrt(jnp.mean(rows * rows, axis=-1, keepdims=True) + 1e-05)
+
+
+def by_time(prompt_ref, piece_ref):
+    both_kinds = jnp.concatenate([prompt_ref[...], piece_ref[...]], axis=0).astype(f32)
+    return jnp.swapaxes(both_kinds, 0, 1)
+
+
+def prepare_kernel(prompt_ref, piece_ref, prompt_cot_ref, piece_cot_ref, halo_ref, gain_ref, scaled_ref, cot_ref):
+    i = pl.program_id(0)
+    gain = gain_ref[...]
+
+    @pl.when(i == 0)
+    def _():
+        rows = halo_ref[...]
+        scaled_ref[0 : HALO * SEQS, :] = (rows * scale_of(rows) * gain).astype(bf16)
+
+    rows = by_time(prompt_ref, piece_ref)
+    count = rows.shape[0] * SEQS
+    rows = rows.reshape(count, D)
+    at = pl.multiple_of(HALO * SEQS + i * count, HALO * SEQS)
+    scaled_ref[pl.ds(at, count), :] = (rows * scale_of(rows) * gain).astype(bf16)
+    cot_ref[...] = by_time(prompt_cot_ref, piece_cot_ref).reshape(count, D).astype(bf16)
+
+
+CHUNK = 16
+
+
+def prepare(prompt, piece, prompt_cot, piece_cot, halo, gain):
+    steps = prompt.shape[1]
+    part = pl.BlockSpec((SEQS // 2, CHUNK, D), lambda i: (0, i, 0))
+    rows = steps * SEQS
+    return pl.pallas_call(
+        prepare_kernel,
+        grid=(steps // CHUNK,),
+        in_specs=[
+            part, part, part, part,
+            pl.BlockSpec((HALO * SEQS, D), lambda i: (0, 0)),
+            pl.BlockSpec((1, D), lambda i: (0, 0)),
+        ],
+        out_specs=[
+            pl.BlockSpec((HALO * SEQS + rows, D), lambda i: (0, 0)),
+            pl.BlockSpec((CHUNK * SEQS, D), lambda i: (i, 0)),
+        ],
+        out_shape=[
+            jax.ShapeDtypeStruct((HALO * SEQS + rows, D), bf16),
+            jax.ShapeDtypeStruct((rows, D), bf16),
+        ],
+        compiler_params=params(),
+        cost_estimate=cost(5),
+        name="prepare",
+    )(prompt, piece, prompt_cot, piece_cot, halo, gain)
+
+
+def norm_back(rows, scaled_grad, gain):
+    inverse = scale_of(rows)
+    unit = rows * inverse
+    grad = scaled_grad * gain
+    back = inverse * (grad - unit * jnp.mean(grad * unit, axis=-1, keepdims=True))
+    return back, scaled_grad * unit
+
+
+def finish_kernel(
+    mixed_ref, grad_ref, more_ref, grad_halo_ref, more_halo_ref,
+    prompt_ref, piece_ref, prompt_cot_ref, piece_cot_ref, halo_ref, gain_ref,
+    prompt_out, piece_out, prompt_grad, piece_grad, halo_grad, gain_grad,
+):
+    i = pl.program_id(0)
+    gain = gain_ref[...]
+
+    @pl.when(i == 0)
+    def _():
+        back, sums = norm_back(halo_ref[...], grad_halo_ref[...] + more_halo_ref[...], gain)
+        halo_grad[...] = back
+        gain_grad[...] = jnp.sum(sums, axis=0, keepdims=True)
+
+    half = SEQS // 2
+    rows = by_time(prompt_ref, piece_ref)
+    shape = rows.shape
+    rows = rows.reshape(-1, D)
+    back, sums = norm_back(rows, grad_ref[...] + more_ref[...], gain)
+    gain_grad[...] += jnp.sum(sums, axis=0, keepdims=True)
+    back = jnp.swapaxes(back.reshape(shape), 0, 1)
+    prompt_grad[...] = back[:half] + prompt_cot_ref[...].astype(f32)
+    piece_grad[...] = back[half:] + piece_cot_ref[...].astype(f32)
+    mixed = jnp.swapaxes((mixed_ref[...] + rows).reshape(shape), 0, 1)
+    prompt_out[...] = mixed[:half].astype(bf16)
+    piece_out[...] = mixed[half:].astype(bf16)
+
+
+def finish(mixed, grad, more, prompt, piece, prompt_cot, piece_cot, halo, gain):
+    steps = prompt.shape[1]
+    part = pl.BlockSpec((SEQS // 2, CHUNK, D), lambda i: (0, i, 0))
+    first = pl.BlockSpec((HALO * SEQS, D), lambda i: (0, 0))
+    shifted = pl.BlockSpec(
+        (pl.Element(CHUNK * SEQS), pl.Element(D)),
+        lambda i: (pl.multiple_of(HALO * SEQS + i * (CHUNK * SEQS), HALO * SEQS), 0),
+    )
+    return pl.pallas_call(
+        finish_kernel,
+        grid=(steps // CHUNK,),
+        in_specs=[
+            pl.BlockSpec((CHUNK * SEQS, D), lambda i: (i, 0)),
+            shifted, shifted, first, first,
+            part, part, part, part,
+            first,
+            pl.BlockSpec((1, D), lambda i: (0, 0)),
+        ],
+        out_specs=[part, part, part, part, first, pl.BlockSpec((1, D), lambda i: (0, 0))],
+        out_shape=[
+            jax.ShapeDtypeStruct(prompt.shape, bf16),
+            jax.ShapeDtypeStruct(piece.shape, bf16),
+            jax.ShapeDtypeStruct(prompt.shape, f32),
+            jax.ShapeDtypeStruct(piece.shape, f32),
+            jax.ShapeDtypeStruct((HALO * SEQS, D), f32),
+            jax.ShapeDtypeStruct((1, D), f32),
+        ],
+        compiler_params=params(),
+        cost_estimate=cost(8),
+        name="finish",
+    )(mixed, grad, more, grad, more, prompt, piece, prompt_cot, piece_cot, halo, gain)
+
+
 def front_kernel(mix_ref, fw_ref, fb_ref, sel_ref, act_ref, proj_ref):
     j = pl.program_id(0)
     steps = act_ref.shape[0]
@@ -56,7 +180,7 @@
 
     def step(i, _):
         t = i * chunk
-        x = mix_ref[pl.ds(t, chunk + HALO)].astype(bf16).astype(f32)
+        x = mix_ref[pl.ds(t, chunk + HALO)].astype(f32)
         v = bias[None] + taps[0][None] * x[1 : 1 + chunk]
         for k in range(1, KERNEL):
             v = v + taps[k][None] * x[1 + k : 1 + k + chunk]
@@ -157,7 +281,7 @@
     j = pl.program_id(0)
     steps = dt_ref.shape[0]
     half = SEQS // 2
-    groups = fwd_ref.shape[0]
+    groups = fwd_ref.shape[0] // half
 
     @pl.when(j == 0)
     def _():
@@ -242,7 +366,8 @@
             return b_scr[group, t, p]
 
         def out(n, value):
-            fwd_ref[group, 0, n] = value
+            fwd_ref[rows, n, :LANES] = value[:half]
+            fwd_ref[rows, n, LANES:] = value[half:]
 
         weighted(packed, vectors, map_at, out)
 
@@ -258,12 +383,12 @@
             return c_scr[t, p]
 
         def out(n, value):
-            bwd_ref[n, :, cols] = value
+            bwd_ref[:, n, cols] = value
 
         weighted(mine, vectors, map_at, out)
 
 
-def piece(proj, act, mixture, gated_grad, step_pad, sbias, rate, select, groups):
+def piece(proj, act, gate, gated_grad, step_pad, sbias, rate, select, groups):
     steps, _, channels = act.shape
     grid = channels // WIDE
     wide = lambda j: (0, 0, j)
@@ -275,7 +400,7 @@
         in_specs=[
             pl.BlockSpec((steps * SEQS, LANES), lambda j: (0, 0)),
             flat,
-            pl.BlockSpec((steps + HALO, SEQS, WIDE), lambda j: (0, 0, j + grid)),
+            pl.BlockSpec((steps + HALO, SEQS, WIDE), wide),
             flat,
             pl.BlockSpec((LANES, WIDE), lambda j: (0, j)),
             pl.BlockSpec((1, WIDE), lambda j: (0, j)),
@@ -284,8 +409,8 @@
         ],
         out_specs=[
             flat, flat, flat, flat, flat,
-            pl.BlockSpec((groups, 1, STATES, SEQS, LANES), lambda j: (0, j, 0, 0, 0)),
-            pl.BlockSpec((STATES, SEQS, WIDE), wide),
+            pl.BlockSpec((groups * SEQS // 2, STATES, WIDE), wide),
+            pl.BlockSpec((SEQS, STATES, WIDE), wide),
             pl.BlockSpec((SEQS, WIDE), lambda j: (0, j)),
         ],
         out_shape=[
@@ -294,8 +419,8 @@
             jax.ShapeDtypeStruct(shape, f32),
             jax.ShapeDtypeStruct(shape, bf16),
             jax.ShapeDtypeStruct(shape, bf16),
-            jax.ShapeDtypeStruct((groups, grid, STATES, SEQS, LANES), f32),
-            jax.ShapeDtypeStruct((STATES, SEQS, channels), f32),
+            jax.ShapeDtypeStruct((groups * SEQS // 2, STATES, channels), f32),
+            jax.ShapeDtypeStruct((SEQS, STATES, channels), f32),
             jax.ShapeDtypeStruct((SEQS, channels), f32),
         ],
         scratch_shapes=[
@@ -307,7 +432,134 @@
         compiler_params=params(),
         cost_estimate=cost(60),
         name="piece",
-    )(proj, act, mixture, gated_grad, step_pad, sbias, rate, select)
+    )(proj, act, gate, gated_grad, step_pad, sbias, rate, select)
+
+
+def chain_kernel(
+    one_hot_ref, ahead_ref, behind_ref, branch_ref, time_ref, rate_ref, start_out, end_out,
+    moved_ref, got, got_time, back, done, sems, time_sems, back_sems,
+):
+    size = got.shape[0]
+    width = got.shape[2]
+    count = PROMPTS * STATES
+    sequels = branch_ref.shape[0]
+    me = lax.axis_index("fsdp")
+    for p in range(PROMPTS):
+        rows = slice(p * STATES, (p + 1) * STATES)
+        total = one_hot_ref[0, p] * branch_ref[0]
+        for k in range(1, sequels):
+            total = total + one_hot_ref[k, p] * branch_ref[k]
+        moved_ref[0 * count + p * STATES : 0 * count + (p + 1) * STATES] = ahead_ref[p].astype(bf16)
+        moved_ref[1 * count + p * STATES : 1 * count + (p + 1) * STATES] = behind_ref[p].astype(bf16)
+        moved_ref[2 * count + p * STATES : 2 * count + (p + 1) * STATES] = total.astype(bf16)
+    barrier = pltpu.get_barrier_semaphore()
+    for d in range(1, size):
+        peer = lax.rem(me + d, size)
+        pl.semaphore_signal(barrier, inc=1, device_id={"fsdp": peer}, device_id_type=pl.DeviceIdType.MESH)
+    pl.semaphore_wait(barrier, size - 1)
+
+    def columns(device):
+        return pl.ds(pl.multiple_of(device * width, width), width)
+
+    copies = []
+    for d in range(1, size):
+        peer = lax.rem(me + d, size)
+        for src, dst, sem in ((moved_ref, got, sems), (time_ref, got_time, time_sems)):
+            copy = pltpu.make_async_remote_copy(
+                src_ref=src.at[:, columns(peer)],
+                dst_ref=dst.at[me],
+                send_sem=sem.at[0, d],
+                recv_sem=sem.at[1, d],
+                device_id={"fsdp": peer},
+                device_id_type=pl.DeviceIdType.MESH,
+            )
+            copy.start()
+            copies.append(copy)
+    got[me] = moved_ref[:, columns(me)]
+    got_time[me] = time_ref[:, columns(me)]
+    for copy in copies:
+        copy.wait()
+
+    rate = jnp.concatenate([rate_ref[...]] * PROMPTS, axis=0)
+    branch = jnp.zeros((count, width), f32)
+    state = jnp.zeros((count, width), f32)
+    decays = []
+    for k in range(size):
+        time = jnp.concatenate(
+            [jnp.broadcast_to(got_time[k, p : p + 1, :], (STATES, width)) for p in range(PROMPTS)], axis=0
+        )
+        decays.append(jnp.exp2(rate * time))
+        back[k, 0:count] = state.astype(bf16)
+        state = decays[k] * state + got[k, 0:count].astype(f32)
+        branch = branch + got[k, 2 * count : 3 * count].astype(f32)
+    grad = branch
+    for k in range(size - 1, -1, -1):
+        back[k, count : 2 * count] = grad.astype(bf16)
+        grad = decays[k] * grad + got[k, count : 2 * count].astype(f32)
+    last = state.astype(bf16)
+    for k in range(size):
+        back[k, 2 * count : 3 * count] = last
+    copies = []
+    for d in range(1, size):
+        peer = lax.rem(me + d, size)
+        copy = pltpu.make_async_remote_copy(
+            src_ref=back.at[peer],
+            dst_ref=done.at[me],
+            send_sem=back_sems.at[0, d],
+            recv_sem=back_sems.at[1, d],
+            device_id={"fsdp": peer},
+            device_id_type=pl.DeviceIdType.MESH,
+        )
+        copy.start()
+        copies.append(copy)
+    done[me] = back[me]
+    for copy in copies:
+        copy.wait()
+    for k in range(size):
+        columns_k = slice(k * width, (k + 1) * width)
+        last = []
+        for p in range(PROMPTS):
+            rows = slice(p * STATES, (p + 1) * STATES)
+            start_out[p, :, columns_k] = done[k, rows].astype(f32)
+            rows = slice(count + p * STATES, count + (p + 1) * STATES)
+            end_out[p, :, columns_k] = done[k, rows].astype(f32)
+            rows = slice(2 * count + p * STATES, 2 * count + (p + 1) * STATES)
+            last.append(done[k, rows].astype(f32))
+        for q in range(sequels):
+            total = one_hot_ref[q, 0] * last[0]
+            for p in range(1, PROMPTS):
+                total = total + one_hot_ref[q, p] * last[p]
+            start_out[PROMPTS + q, :, columns_k] = total
+            end_out[PROMPTS + q, :, columns_k] = jnp.zeros_like(total)
+
+
+def chain(one_hot, ahead, behind, branch, time, rate):
+    size = lax.axis_size("fsdp")
+    channels = ahead.shape[2]
+    rows = 3 * PROMPTS * STATES
+    width = channels // size
+    own = lax.dynamic_slice_in_dim(rate, lax.axis_index("fsdp") * width, width, 1)
+    whole = pl.BlockSpec(memory_space=pltpu.VMEM)
+    shape = (PROMPTS + branch.shape[0], STATES, channels)
+    return pl.pallas_call(
+        chain_kernel,
+        in_specs=[pl.BlockSpec(memory_space=pltpu.SMEM)] + [whole] * 5,
+        out_specs=[whole] * 2,
+        out_shape=[jax.ShapeDtypeStruct(shape, f32)] * 2,
+        scratch_shapes=[
+            pltpu.VMEM((rows, channels), bf16),
+            pltpu.VMEM((size, rows, width), bf16),
+            pltpu.VMEM((size, SEQS, width), f32),
+            pltpu.VMEM((size, rows, width), bf16),
+            pltpu.VMEM((size, rows, width), bf16),
+            pltpu.SemaphoreType.DMA((2, size)),
+            pltpu.SemaphoreType.DMA((2, size)),
+            pltpu.SemaphoreType.DMA((2, size)),
+        ],
+        compiler_params=params(collective_id=1, has_side_effects=True),
+        cost_estimate=cost(25),
+        name="chain",
+    )(one_hot, ahead, behind, branch, time, own)
 
 
 TILES = [slice(k * LANES, (k + 1) * LANES) for k in range(WIDE // LANES)]
@@ -328,6 +580,7 @@
 
     rates = [jnp.broadcast_to(rate_ref[n : n + 1, :], (SEQS, LANES)) for n in range(STATES)]
     skip = jnp.broadcast_to(skip_ref[0:1, :], (SEQS, LANES))
+    gategrad_ref[0:HALO] = jnp.zeros((HALO, SEQS, LANES), bf16)
     unroll = 8
 
     def run(i, carry):
@@ -349,11 +602,11 @@
             h = tuple(new)
             mixed = folded(y) + skip * act
             gated_ref[t] = (mixed * silu_ref[t].astype(f32)).astype(bf16)
-            gategrad_ref[t] = (mixed * slope_ref[t].astype(f32)).astype(bf16)
+            gategrad_ref[t + HALO] = (mixed * slope_ref[t].astype(f32)).astype(bf16)
             skip_sum = skip_sum + yg_ref[t] * act
         return h, skip_sum
 
-    start = tuple(start_ref[n] for n in range(STATES))
+    start = tuple(start_ref[:, n, :] for n in range(STATES))
     for p in range(PAIRS):
         hist_ref[0, p] = pair(start[2 * p], start[2 * p + 1])
     _, skip_sum = lax.fori_loop(0, steps // unroll, run, (start, jnp.zeros((SEQS, LANES), f32)))
@@ -373,7 +626,7 @@
             pl.BlockSpec((steps * SEQS, LANES), lambda j: (0, 0)),
             flat, flat, flat, flat, flat,
             pl.BlockSpec((STATES, LANES), lambda j: (0, j)),
-            pl.BlockSpec((STATES, SEQS, LANES), tile),
+            pl.BlockSpec((SEQS, STATES, LANES), tile),
             pl.BlockSpec((1, LANES), lambda j: (0, j)),
             pl.BlockSpec(select.shape, lambda j: (0, 0)),
         ],
@@ -383,13 +636,13 @@
                 (None, None, steps + 1, PAIRS, 2 * SEQS, LANES),
                 lambda j: (j // parts, j % parts, 0, 0, 0, 0),
             ),
-            flat,
+            pl.BlockSpec((steps + HALO, SEQS, LANES), tile),
             pl.BlockSpec((1, LANES), lambda j: (0, j)),
         ],
         out_shape=[
             jax.ShapeDtypeStruct((steps, SEQS, channels), bf16),
             jax.ShapeDtypeStruct((grid // parts, parts, steps + 1, PAIRS, 2 * SEQS, LANES), bf16),
-            jax.ShapeDtypeStruct((steps, SEQS, channels), bf16),
+            jax.ShapeDtypeStruct((steps + HALO, SEQS, channels), bf16),
             jax.ShapeDtypeStruct((1, channels), f32),
         ],
         scratch_shapes=[
@@ -428,7 +681,7 @@
     decay_scr[...] = jnp.zeros_like(decay_scr)
     sum_scr[...] = jnp.zeros_like(sum_scr)
     for n in range(STATES):
-        ge_scr[n] = end_ref[n]
+        ge_scr[n] = end_ref[:, n, :]
 
     def run(i, _):
         base = steps - (i + 1) * RUN
@@ -529,7 +782,7 @@
             pl.BlockSpec((steps * SEQS, LANES), whole),
             flat, flat, flat, flat,
             pl.BlockSpec((STATES, WIDE), lambda j: (0, j)),
-            pl.BlockSpec((STATES, SEQS, WIDE), tile),
+            pl.BlockSpec((SEQS, STATES, WIDE), tile),
             pl.BlockSpec((1, WIDE), lambda j: (0, j)),
             pl.BlockSpec(
                 (None, len(TILES), steps + 1, PAIRS, 2 * SEQS, LANES), lambda j: (j, 0, 0, 0, 0, 0)
@@ -570,7 +823,7 @@
 
 
 def filter_back_kernel(
-    mix_ref, act_ref, act_grad_ref, projg_ref, projg_t_ref, sel_t_ref, fw_ref, fb_ref,
+    mix_ref, act_ref, act_grad_ref, projg_ref, projg_t_ref, sel_ref, fw_ref, fb_ref,
     mixgrad_ref, selg_ref, fwg_ref, fbg_ref,
     dv_scr,
 ):
@@ -584,13 +837,13 @@
 
     def step(i, sums):
         t = i * chunk
-        x = mix_ref[pl.ds(t, chunk + HALO)].astype(bf16).astype(f32)
+        x = mix_ref[pl.ds(t, chunk + HALO)].astype(f32)
         v = bias[None] + taps[0][None] * x[1 : 1 + chunk]
         for k in range(1, KERNEL):
             v = v + taps[k][None] * x[1 + k : 1 + k + chunk]
         sig = sigmoid(v)
         r = pl.multiple_of(t * SEQS, chunk * SEQS)
-        more = jnp.dot(projg_ref[pl.ds(r, chunk * SEQS), :], sel_t_ref[...], preferred_element_type=f32)
+        more = contract_cols(projg_ref[pl.ds(r, chunk * SEQS), :], sel_ref[...])
         total = act_grad_ref[pl.ds(t, chunk)] + more.reshape(chunk, SEQS, WIDE)
         dv = total * (sig * (1.0 + v * (1.0 - sig)))
         dv_scr[pl.ds(t + HALO, chunk)] = dv
@@ -624,7 +877,7 @@
     selg_ref[...] = jnp.dot(projg_t_ref[...], low, preferred_element_type=f32)
 
 
-def filter_back(mixture, act, act_grad, projg, projg_t, sel_t, fw, fb):
+def filter_back(mixture, act, act_grad, projg, projg_t, select_pad, fw, fb):
     steps, _, channels = act.shape
     grid = channels // WIDE
     wide = lambda j: (0, 0, j)
@@ -639,7 +892,7 @@
             pl.BlockSpec((steps, SEQS, WIDE), wide),
             pl.BlockSpec((steps * SEQS, LANES), whole),
             pl.BlockSpec((LANES, steps * SEQS), whole),
-            pl.BlockSpec((LANES, WIDE), cols),
+            pl.BlockSpec((WIDE, LANES), lambda j: (j, 0)),
             pl.BlockSpec((KERNEL, WIDE), cols),
             pl.BlockSpec((1, WIDE), cols),
         ],
@@ -659,11 +912,313 @@
         compiler_params=params(),
         cost_estimate=cost(20),
         name="filter_back",
-    )(mixture, act, act_grad, projg, projg_t, sel_t, fw, fb)
-
-
-def normalized(hidden, norm_gain):
-    return hidden * lax.rsqrt(jnp.mean(hidden * hidden, axis=-1, keepdims=True) + 1e-05) * norm_gain
+    )(mixture, act, act_grad, projg, projg_t, select_pad, fw, fb)
+
+
+def send(src, dst, send_sem, recv_sem, peer, axis="fsdp"):
+    return pltpu.make_async_remote_copy(
+        src_ref=src,
+        dst_ref=dst,
+        send_sem=send_sem,
+        recv_sem=recv_sem,
+        device_id={axis: peer},
+        device_id_type=pl.DeviceIdType.MESH,
+    )
+
+
+def greet(others):
+    barrier = pltpu.get_barrier_semaphore()
+    for axis, peer in others:
+        pl.semaphore_signal(barrier, inc=1, device_id={axis: peer}, device_id_type=pl.DeviceIdType.MESH)
+    pl.semaphore_wait(barrier, len(others))
+
+
+def flipped(index, bit):
+    return index + (1 - 2 * (index // bit % 2)) * bit
+
+
+FIRST, SECOND = (0, 1, 2, 3), (4, 5)
+
+
+def gather_kernel(
+    rows_ref, select_ref, out_ref, in_ref, all_rows, all_select, all_out, all_in,
+    local_sems, own_send, own_recv, pass_send, pass_recv, core_send, core_recv,
+):
+    me = lax.axis_index("fsdp")
+    a, b = flipped(me, 2), flipped(me, 4)
+    corner = flipped(a, 4)
+    twin = flipped(me, 1)
+    greet([("fsdp", a), ("fsdp", b), ("fsdp", twin)])
+    kinds = ((rows_ref, all_rows), (select_ref, all_select), (out_ref, all_out), (in_ref, all_in))
+    table = [(0, 0, 1), (1, 0, 1), (2, 0, 2), (3, 0, 2), (2, 1, 2), (3, 1, 2)]
+
+    def place(owner, piece):
+        kind, part, parts = table[piece]
+        count = kinds[kind][0].shape[0]
+        step = count // parts
+        return kinds[kind][1].at[pl.ds(pl.multiple_of(owner * count + part * step, step), step)]
+
+    def mine(piece):
+        kind, part, parts = table[piece]
+        step = kinds[kind][0].shape[0] // parts
+        return kinds[kind][0].at[pl.ds(part * step, step)]
+
+    started = []
+
+    def start(copy):
+        copy.start()
+        started.append(copy)
+
+    def own_copy(piece, k, peer, owner):
+        return send(mine(piece), place(owner, piece), own_send.at[k, piece], own_recv.at[k, piece], peer)
+
+    def pass_copy(piece, peer, owner):
+        return send(place(owner, piece), place(owner, piece), pass_send.at[piece], pass_recv.at[piece], peer)
+
+    def core_copy(piece, k, owner):
+        src = mine(piece) if k == 0 else place(owner, piece)
+        return send(src, place(owner, piece), core_send.at[k, piece], core_recv.at[k, piece], twin)
+
+    for piece in FIRST + SECOND:
+        start(own_copy(piece, 0, a, me))
+    for piece in SECOND + FIRST:
+        start(own_copy(piece, 1, b, me))
+    local = []
+    for piece in FIRST + SECOND:
+        start(core_copy(piece, 0, me))
+        copy = pltpu.make_async_copy(mine(piece), place(me, piece), local_sems.at[piece])
+        copy.start()
+        local.append(copy)
+
+    def arrived(piece, k):
+        owner = (a, b, corner)[k]
+        if k == 2:
+            pass_copy(piece, a, owner).wait_recv()
+        else:
+            own_copy(piece, k, a, owner).wait_recv()
+            if k == 0 and piece in FIRST:
+                start(pass_copy(piece, b, owner))
+            if k == 1 and piece in SECOND:
+                start(pass_copy(piece, a, owner))
+        start(core_copy(piece, k + 1, owner))
+
+    for piece, k in (
+        (0, 0), (1, 0), (2, 0), (4, 1), (3, 0), (5, 1), (4, 0), (0, 1), (1, 1), (2, 1), (0, 2), (1, 2), (2, 2),
+        (4, 2), (5, 0), (3, 1), (3, 2), (5, 2),
+    ):
+        arrived(piece, k)
+    for k, owner in enumerate((twin, flipped(twin, 2), flipped(twin, 4), flipped(corner, 1))):
+        for piece in FIRST + SECOND:
+            core_copy(piece, k, owner).wait_recv()
+    for copy in started:
+        copy.wait_send()
+    for copy in local:
+        copy.wait()
+
+
+def gather(*shards):
+    size = lax.axis_size("fsdp")
+    if size != 8:
+        return [lax.all_gather(shard, "fsdp", axis=0, tiled=True) for shard in shards]
+    vmem = pl.BlockSpec(memory_space=pltpu.VMEM)
+    hbm = pl.BlockSpec(memory_space=pl.ANY)
+    pieces = len(FIRST + SECOND)
+    dma = pltpu.SemaphoreType.DMA
+    return pl.pallas_call(
+        gather_kernel,
+        in_specs=[vmem] * 4,
+        out_specs=[hbm] * 4,
+        out_shape=[jax.ShapeDtypeStruct((size * shard.shape[0], shard.shape[1]), bf16) for shard in shards],
+        scratch_shapes=[
+            dma((pieces,)), dma((2, pieces)), dma((2, pieces)), dma((pieces,)), dma((pieces,)),
+            dma((4, pieces)), dma((4, pieces)),
+        ],
+        compiler_params=params(collective_id=2, has_side_effects=True),
+        cost_estimate=cost(55),
+        name="gather",
+    )(*shards)
+
+
+SMALL = (KERNEL, 1, 1, 1, STATES, RANK, RANK + 2 * STATES, 1)
+SMALL_ROWS = 192
+
+
+def xor(index, bits):
+    for bit in (1, 2, 4, 8):
+        if bits & bit:
+            index = flipped(index, bit)
+    return index
+
+
+def tail_kernel(
+    one_hot_ref, b0, b1, b2, b3, filter_ref, fbias_ref, sbias_ref, skip_ref, decay_ref, step_ref, select_ref,
+    gain_ref, halo_ref, *rest,
+):
+    depth = lax.axis_size("replica")
+    early_refs, rest = rest[:depth], rest[depth:]
+    (
+        in_out, out_out, filter_out, fbias_out, sbias_out, skip_out, decay_out, step_out, select_out, gain_out,
+        rim_out,
+        total, to_z, from_z, part, parts, small_f, small_ref, got_small, small_z, small_from_z, small_part,
+        small_parts, rim, child, got_rim, got_child, early,
+        sems_s, sems_z, sems_p, sems_sz, sems_sp, sems_r, sems_cs, sems_cr,
+    ) = rest
+    me, size = lax.axis_index("fsdp"), lax.axis_size("fsdp")
+    mz = lax.axis_index("replica")
+    last = size - 1
+    near = [lax.rem(me + d, size) for d in range(1, size)]
+    far = [lax.rem(mz + d, depth) for d in range(1, depth)]
+    greet([("fsdp", peer) for peer in near] + [("replica", peer) for peer in far])
+
+    def spread(src, dst, sems, peers, axis, index):
+        copies = []
+        for d, peer in enumerate(peers):
+            source = src.at[peer] if src.shape[0] == len(peers) + 1 and len(src.shape) == len(dst.shape) else src
+            copy = send(source, dst.at[index], sems.at[0, d], sems.at[1, d], peer, axis)
+            copy.start()
+            copies.append(copy)
+        return copies
+
+    width = small_f.shape[2]
+    small_f[...] = jnp.zeros_like(small_f)
+    refs = (filter_ref, fbias_ref, sbias_ref, skip_ref, decay_ref, step_ref, select_ref)
+    for k in range(size):
+        at = 0
+        for ref, count in zip(refs, SMALL):
+            small_f[k, at : at + count] = ref[0:count, k * width : (k + 1) * width]
+            at += count
+        some = gain_ref.shape[1] // size
+        small_f[k, at : at + 1, 0:some] = gain_ref[:, k * some : (k + 1) * some]
+    small_ref[...] = small_f[...].astype(bf16)
+    sequels = one_hot_ref.shape[0]
+    pieces = (SEQS - PROMPTS) // sequels
+    for t in range(HALO):
+        rim[t * PROMPTS : (t + 1) * PROMPTS] = halo_ref[t, 0:PROMPTS]
+        for p in range(PROMPTS):
+            sums = None
+            for q in range(sequels):
+                row = PROMPTS + q * pieces
+                term = one_hot_ref[q, p] * halo_ref[t, row : row + 1]
+                sums = term if q == 0 else sums + term
+            child[t * PROMPTS + p : t * PROMPTS + p + 1] = sums
+    block = b0[...].astype(f32) + b1[...].astype(f32) + b2[...].astype(f32) + b3[...].astype(f32)
+    total[...] = block.reshape(total.shape)
+    to_z[...] = total[...].astype(bf16)
+    to_left = send(rim, got_rim, sems_r.at[0], sems_r.at[1], lax.rem(me + last, size))
+    to_left.start()
+
+    @pl.when(me != last)
+    def _():
+        send(child, got_child.at[me], sems_cs.at[me], sems_cr.at[me], last).start()
+
+    copies = spread(small_ref, got_small, sems_s, near, "fsdp", me)
+    z_copies = spread(to_z, from_z, sems_z, far, "replica", mz)
+    small = small_ref[me].astype(f32)
+    got_small[me] = jnp.zeros(got_small.shape[1:], bf16)
+    from_z[mz] = jnp.zeros(from_z.shape[1:], bf16)
+    small_from_z[mz] = jnp.zeros(small_from_z.shape[1:], bf16)
+    for copy in copies:
+        copy.wait()
+    for k in range(size):
+        small = small + got_small[k].astype(f32)
+    small_z[...] = small.reshape(small_z.shape)
+    small_to_z = small_part
+    small_to_z[...] = small_z[...].astype(bf16)
+    s_copies = spread(small_to_z, small_from_z, sems_sz, far, "replica", mz)
+    for copy in z_copies:
+        copy.wait()
+    own = total[mz]
+    for k in range(depth):
+        own = own + from_z[k].astype(f32)
+    part[...] = own.astype(bf16)
+    p_copies = spread(part, parts, sems_p, far, "replica", mz)
+    parts[mz] = part[...]
+    for copy in s_copies:
+        copy.wait()
+    own = small_z[mz]
+    for k in range(depth):
+        own = own + small_from_z[k].astype(f32)
+    small_parts[mz] = own.astype(bf16)
+    small_own = small_to_z.at[mz]
+    small_own[...] = own.astype(bf16)
+    q_copies = []
+    for d, peer in enumerate(far):
+        copy = send(small_own, small_parts.at[mz], sems_sp.at[0, d], sems_sp.at[1, d], peer, "replica")
+        copy.start()
+        q_copies.append(copy)
+    for copy in p_copies + q_copies:
+        copy.wait()
+    half = in_out.shape[1] // 2
+    in_out[:, 0:half] = parts[...].reshape(in_out.shape[0], half).astype(f32)
+    small = small_parts[...].reshape(SMALL_ROWS, width).astype(f32)
+    at = 0
+    for out, count in zip(
+        (filter_out, fbias_out, sbias_out, skip_out, decay_out, step_out, select_out, gain_out), SMALL
+    ):
+        out[...] = small[at : at + count, 0 : out.shape[1]]
+        at += count
+    for d, ref in enumerate(early_refs):
+        count = ref.shape[0]
+        total_rows = pl.ds(pl.multiple_of(xor(mz, d) * count, count), count)
+        early[total_rows, :] = ref[...].astype(f32)
+    rows = out_out.shape[0] // 2
+    features = out_out.shape[1]
+    out_out[0:rows, :] = early[0:rows, 0:features]
+    out_out[rows:, :] = early[0:rows, features:]
+    in_out[:, half:] = early[rows:, :]
+    to_left.wait()
+
+    @pl.when(me != last)
+    def _():
+        send(child, got_child.at[me], sems_cs.at[me], sems_cr.at[me], last).wait_send()
+        rim_out[...] = got_rim[...]
+
+    @pl.when(me == last)
+    def _():
+        sums = child[...]
+        for k in range(size - 1):
+            send(child, got_child.at[k], sems_cs.at[k], sems_cr.at[k], 0).wait_recv()
+            sums = sums + got_child[k]
+        rim_out[...] = sums
+
+
+def tail(one_hot, blocks, small, halo_grad, early):
+    size, depth = lax.axis_size("fsdp"), lax.axis_size("replica")
+    vmem = pl.BlockSpec(memory_space=pltpu.VMEM)
+    dma = pltpu.SemaphoreType.DMA
+    while len(blocks) > 4:
+        blocks = blocks[:3] + [summed(blocks[3], blocks[4:5]).astype(bf16)] + blocks[5:]
+    rows, channels = blocks[0].shape
+    features = small[-1].shape[1]
+    width = channels // size
+    cut = (depth, rows // depth, channels)
+    by_owner = (size, SMALL_ROWS, width)
+    small_cut = (depth, SMALL_ROWS // depth, width)
+    rim = (HALO * PROMPTS, features)
+    counts = [(count, width) for count in SMALL[:-1]] + [(1, features // size)]
+    return pl.pallas_call(
+        tail_kernel,
+        in_specs=[pl.BlockSpec(memory_space=pltpu.SMEM)] + [vmem] * (4 + len(small) + 1 + depth),
+        out_specs=[vmem] * (3 + len(counts)),
+        out_shape=[
+            jax.ShapeDtypeStruct(shape, f32)
+            for shape in [(rows, 2 * channels), (2 * rows, features)] + counts + [rim]
+        ],
+        scratch_shapes=[
+            pltpu.VMEM(cut, f32), pltpu.VMEM(cut, bf16), pltpu.VMEM(cut, bf16),
+            pltpu.VMEM(cut[1:], bf16), pltpu.VMEM(cut, bf16),
+            pltpu.VMEM(by_owner, f32), pltpu.VMEM(by_owner, bf16), pltpu.VMEM(by_owner, bf16),
+            pltpu.VMEM(small_cut, f32), pltpu.VMEM(small_cut, bf16),
+            pltpu.VMEM(small_cut, bf16), pltpu.VMEM(small_cut, bf16),
+            pltpu.VMEM(rim, f32), pltpu.VMEM(rim, f32), pltpu.VMEM(rim, f32), pltpu.VMEM((size,) + rim, f32),
+            pltpu.VMEM((2 * rows, channels), f32),
+            dma((2, size)), dma((2, depth)), dma((2, depth)), dma((2, depth)), dma((2, depth)),
+            dma((2,)), dma((size,)), dma((size,)),
+        ],
+        compiler_params=params(collective_id=4, has_side_effects=True),
+        cost_estimate=cost(30),
+        name="tail",
+    )(one_hot, *blocks, *small, halo_grad, *early)
 
 
 def contract_rows(left_side, right_side):
@@ -721,10 +1276,6 @@
     here = lax.axis_index("replica")
     parts = jnp.stack(parts)
     return jnp.concatenate([pick_row(parts, here ^ i) for i in range(parts.shape[0])]).astype(f32)
-
-
-def gathered(block, axis):
-    return lax.all_gather(block, "fsdp", axis=axis, tiled=True)
 
 
 def body(
@@ -741,112 +1292,90 @@
     half = SEQS // 2
     rows = steps * SEQS
 
-    small = jnp.concatenate(
+    after = lax.optimization_barrier
+    width = step_bias.shape[0]
+    tail_rows = prompt_hidden[:, steps - rim :]
+    shard = jnp.concatenate(
         [
+            step_weight,
+            tail_rows.reshape(-1, width),
             filter_weight,
             depthwise_filter_bias[None],
             step_bias[None],
             skip_gain[None],
-            decay_log.T,
-            step_weight,
-            select_weight.T,
-            jnp.pad(norm_gain, (0, step_bias.shape[0] - norm_gain.shape[0]))[None],
+            jnp.pad(norm_gain, (0, width - norm_gain.shape[0]))[None],
         ],
         axis=0,
     )
-    small = gathered(small, 1)
-    at = 0
-
-    def take(count):
-        nonlocal at
-        at += count
-        return small[at - count : at]
-
-    fw = take(KERNEL).astype(f32)
-    fb = take(1).astype(f32)
-    sbias = take(1).astype(f32)
-    skip = take(1).astype(f32)
-    rate = -jnp.exp(take(STATES).astype(f32)) * LOG2E
-    step_full = take(RANK)
-    sel_t = jnp.pad(take(RANK + 2 * STATES), ((0, LANES - RANK - 2 * STATES), (0, 0)))
-    gain = take(1).reshape(size, -1)[:, : norm_gain.shape[0]].reshape(-1).astype(f32)
-    select_pad = sel_t.T
+    shard = jnp.pad(shard, ((0, -shard.shape[0] % 16), (0, 0)))
+    lanes = jnp.concatenate([select_weight, decay_log], axis=1)
+    lanes = jnp.pad(lanes, ((0, 0), (0, LANES - lanes.shape[1])))
+    every, select_pad, full_output, full_input = gather(shard, lanes, output_weight, input_weight)
+    every = every.reshape(size, shard.shape[0], width)
+    at = RANK + tail_rows.size // width
+    tails = every[:, RANK:at].reshape((size,) + tail_rows.shape)
+    step_full = jnp.swapaxes(every[:, :RANK], 0, 1).reshape(RANK, -1)
+    vectors = jnp.swapaxes(every[:, at : at + SEQS], 0, 1).astype(f32)
+    gain = vectors[KERNEL + 3, :, : norm_gain.shape[0]].reshape(1, -1)
+    vectors = vectors.reshape(SEQS, -1)
+    fw, fb, sbias, skip = vectors[:KERNEL], vectors[4:5], vectors[5:6], vectors[6:7]
+    first = RANK + 2 * STATES
+    rate = -jnp.exp(select_pad[:, first : first + STATES].T.astype(f32)) * LOG2E
     step_pad = jnp.pad(step_full, ((0, LANES - RANK), (0, 0)))
-    full_output = gathered(output_weight, 0)
-    full_input = gathered(input_weight, 0)
-
-    tails = lax.all_gather(prompt_hidden[:, steps - rim :], "fsdp")
+
     before = jnp.where(here > 0, tails[jnp.maximum(here - 1, 0)], jnp.zeros_like(tails[0]))
-    pieces = sequel_hidden.reshape(sequels, split, steps, D)
-    inner = jnp.concatenate([tails[size - 1][parents][:, None], pieces[:, :-1, steps - rim :]], axis=1)
+    cut = sequel_hidden.reshape(sequels, split, steps, D)
+    inner = jnp.concatenate([tails[size - 1][parents][:, None], cut[:, :-1, steps - rim :]], axis=1)
     halo = jnp.concatenate([before, inner.reshape(-1, rim, D)], axis=0)
-    halo = jnp.pad(halo, ((0, 0), (HALO - rim, 0), (0, 0)))
-    hidden = jnp.concatenate([prompt_hidden, sequel_hidden.reshape(-1, steps, D)], axis=0)
-    hidden = jnp.swapaxes(jnp.concatenate([halo, hidden], axis=1), 0, 1).reshape(-1, D).astype(f32)
-    cot = jnp.concatenate([prompt_cotangent, sequel_cotangent.reshape(-1, steps, D)], axis=0)
-    cotangent = jnp.swapaxes(cot, 0, 1).reshape(rows, D)
-
+    halo = jnp.pad(jnp.swapaxes(halo, 0, 1), ((HALO - rim, 0), (0, 0), (0, 0))).reshape(-1, D).astype(f32)
+    pieces = sequel_hidden.reshape(-1, steps, D)
+    piece_cot = sequel_cotangent.reshape(-1, steps, D)
+    scaled, cotangent = prepare(prompt_hidden, pieces, prompt_cotangent, piece_cot, halo, gain)
+
+    mixture = jnp.dot(scaled, full_input[:, :INNER], preferred_element_type=f32).astype(bf16)
+    gate = jnp.dot(scaled, full_input[:, INNER:], preferred_element_type=f32)
+    mixture = mixture.reshape(steps + HALO, SEQS, INNER)
+    gate = gate.reshape(steps + HALO, SEQS, INNER)
     gated_grad = contract_cols(cotangent, full_output).reshape(steps, SEQS, INNER)
-    scaled = normalized(hidden, gain).astype(bf16)
-    mixture = jnp.dot(scaled, full_input, preferred_element_type=f32)
-    mixture = mixture.reshape(steps + HALO, SEQS, 2 * INNER)
     act, proj = front(mixture, fw, fb, select_pad, steps)
     groups = 1 if split == 1 else 2
     lane = jnp.arange(2 * STATES * LANES)[None, :]
     select = (jnp.arange(LANES)[:, None] == RANK + lane // LANES).astype(bf16)
     dt, sig, yg, silu, slope, ahead, behind, total = piece(
-        proj, act, mixture, gated_grad, step_pad, sbias, rate, select, groups
+        proj, act, gate, gated_grad, step_pad, sbias, rate, select, groups
     )
 
-    ahead = ahead.reshape(groups, -1, STATES, 2, half, LANES).transpose(2, 0, 4, 1, 3, 5)
-    ahead = ahead.reshape(STATES, groups * half, INNER)
     one_hot = (parents[:, None] == jnp.arange(PROMPTS, dtype=jnp.int32)[None, :]).astype(f32)
-    own = total[half:].reshape(sequels, split, INNER)
-    own_behind = behind[:, half:].reshape(STATES, sequels, split, INNER)
-    own_decay = jnp.exp2(rate[:, None, None, :] * own[None])
-    back = jnp.zeros((STATES, sequels, INNER), f32)
-    own_end = []
-    for p in range(split - 1, -1, -1):
+    own = total[half:].reshape(sequels, split, 1, INNER)
+    own_behind = behind[half:].reshape(sequels, split, STATES, INNER)
+    back = own_behind[:, split - 1]
+    own_end = [jnp.zeros_like(back)]
+    for p in range(split - 2, -1, -1):
         own_end.insert(0, back)
-        back = own_behind[:, :, p] + (own_decay[:, :, p] * back if p < split - 1 else 0.0)
-    branch = jnp.sum(back[:, :, None, :] * one_hot[None, :, :, None], axis=1)
-    branch = lax.psum(branch, "fsdp")
-    moved = jnp.concatenate([ahead[:, :half], behind[:, :half]], axis=0)
-    moved, totals = lax.all_gather((moved, total[:half]), "fsdp")
-    decays = jnp.exp2(rate[None, :, None, :] * totals[:, None, :, :])
-    state = jnp.zeros_like(branch)
-    start = state
-    for k in range(size):
-        start = jnp.where(here == k, state, start)
-        state = decays[k] * state + moved[k, :STATES]
-    back = branch
-    end = back
-    for k in range(size - 1, -1, -1):
-        end = jnp.where(here == k, back, end)
-        back = decays[k] * back + moved[k, STATES:]
-    state = jnp.sum(state[:, None] * one_hot[None, :, :, None], axis=2)
-    own_start = [state]
-    for p in range(split - 1):
-        state = own_decay[:, :, p] * state + ahead[:, half:].reshape(STATES, sequels, split, INNER)[:, :, p]
-        own_start.append(state)
-    own_start = jnp.stack(own_start, axis=2).reshape(STATES, half, INNER)
-    own_end = jnp.stack(own_end, axis=2).reshape(STATES, half, INNER)
-    start = jnp.concatenate([start, own_start], axis=1)
-    end = jnp.concatenate([end, own_end], axis=1)
+        back = own_behind[:, p] + jnp.exp2(rate * own[:, p]) * back
+    start, end = chain(one_hot, ahead[:half], behind[:half], back, total, rate)
+    if split > 1:
+        state = start[half:]
+        own_start = [state]
+        for p in range(split - 1):
+            state = jnp.exp2(rate * own[:, p]) * state + ahead[half:].reshape(own_behind.shape)[:, p]
+            own_start.append(state)
+        own_start = jnp.stack(own_start, axis=1).reshape(half, STATES, INNER)
+        start = jnp.concatenate([start[:half], own_start], axis=0)
+        end = jnp.concatenate([end[:half], jnp.stack(own_end, axis=1).reshape(half, STATES, INNER)], axis=0)
 
     gated, hist, gate_grad, skip_grad = forward(
         proj, dt, act, yg, silu, slope, rate, start, skip, select
     )
     gated = gated.reshape(rows, INNER)
-    gate_grad = gate_grad.reshape(rows, INNER)
-    after = lax.optimization_barrier
+    gate_grad = gate_grad.reshape(-1, INNER)
     output_grad = contract_rows(gated, cotangent).astype(bf16).reshape(size, -1, D)
-    gate_weight_grad = contract_rows(scaled[HALO * SEQS :], gate_grad).astype(bf16)
+    gate_weight_grad = contract_rows(scaled, gate_grad).astype(bf16)
     early = [over_cores(output_grad), over_cores(gate_weight_grad.reshape(size, -1, INNER))]
-    result = hidden[HALO * SEQS :] + jnp.dot(gated, full_output, preferred_element_type=f32)
-    result = jnp.swapaxes(result.reshape(steps, SEQS, D), 0, 1).astype(bf16)
+    wide = jnp.concatenate([early[0][:, : INNER // size // 2], early[0][:, INNER // size // 2 :]], axis=2)
+    early = jnp.concatenate([wide, early[1]], axis=1)
     end, early = after((end, early))
-    early = [to_chips(block) for block in early]
+    early = to_chips(early)
 
     rank_t = proj[:, :RANK].astype(bf16).T
     lane = jnp.arange(LANES)[None, None, :]
@@ -857,69 +1386,47 @@
         proj, dt, sig, act, yg, rate, end, skip, hist, rank_t, step_pad.T, pick, select
     )
     projg, early = after((projg, early))
-    early = [summed(*block) for block in early]
+    early = summed(*early)
     projg, early = after((projg, early))
-    early = [to_replicas(block) for block in early]
+    early = to_replicas(early)
     filter_in_grad, select_grad, filter_grad, filter_bias_grad = filter_back(
-        mixture, act, act_grad, projg, projg.T, sel_t, fw, fb
+        mixture, act, act_grad, projg, projg.T, select_pad, fw, fb
     )
     filter_in_grad, early = after((filter_in_grad, early))
-    early = [summed(*block).astype(bf16) for block in early]
+    early = summed(*early).astype(bf16)
     filter_in_grad = filter_in_grad.reshape(-1, INNER)
     filter_weight_grad = contract_rows(scaled, filter_in_grad).astype(bf16)
-    late = [over_cores(filter_weight_grad.reshape(size, -1, INNER))]
-    early = [from_replicas(block) for block in early]
+    filter_weight_grad, early = after((filter_weight_grad, early))
+    late = over_cores(filter_weight_grad.reshape(size, -1, INNER))
+    early = from_replicas(early)
+    more = contract_cols(gate_grad, full_input[:, INNER:])
+    late, more, filter_in_grad, gated = after((late, more, filter_in_grad, gated))
+    own_block, late = to_chips(late)
     scaled_grad = contract_cols(filter_in_grad, full_input[:, :INNER])
-    more = contract_cols(gate_grad, full_input[:, INNER:])
-    scaled_grad = scaled_grad + jnp.pad(more, ((HALO * SEQS, 0), (0, 0)))
-    unused_norm, norm_back = jax.vjp(normalized, hidden, gain)
-    hidden_grad, gain_grad = norm_back(scaled_grad)
-    hidden_grad = jnp.swapaxes(hidden_grad.reshape(steps + HALO, SEQS, D), 0, 1)
-    main = hidden_grad[:, HALO:]
-    extra = hidden_grad[:, HALO - rim : HALO]
-    own_extra = extra[half:].reshape(sequels, split, rim, D)
-    child = jnp.einsum("sp,srd->prd", one_hot, own_extra[:, 0], precision=lax.Precision.HIGHEST)
-    shared = lax.all_gather(jnp.stack([extra[:half], child]), "fsdp")
-    following = jnp.where(
-        here < size - 1, shared[jnp.minimum(here + 1, size - 1), 0], jnp.sum(shared[:, 1], axis=0)
+    mixed = jnp.dot(gated, full_output, preferred_element_type=f32)
+    prompt_out, piece_out, prompt_grad, piece_grad, halo_grad, gain_grad = finish(
+        mixed, scaled_grad, more, prompt_hidden, pieces, prompt_cotangent, piece_cot, halo, gain
     )
-    own_following = jnp.pad(own_extra[:, 1:], ((0, 0), (0, 1), (0, 0), (0, 0))).reshape(half, rim, D)
-    tail = jnp.concatenate([following, own_following], axis=0)
-    main = main + jnp.pad(tail, ((0, 0), (steps - rim, 0), (0, 0))) + cot.astype(f32)
-
-    small_grad = jnp.concatenate(
-        [
-            filter_grad,
-            filter_bias_grad,
-            bias_grad,
-            skip_grad,
-            decay_grad,
-            step_grad,
-            select_grad[: RANK + 2 * STATES],
-            jnp.pad(gain_grad.reshape(size, -1), ((0, 0), (0, (INNER - D) // size))).reshape(1, -1),
-            jnp.zeros((8, INNER), f32),
-        ],
-        axis=0,
-    )
-    small_grad = jnp.swapaxes(small_grad.astype(bf16).reshape(small_grad.shape[0], size, -1), 0, 1)
-    late = late + [over_cores(small_grad)]
-    late = [summed(*to_chips(block)) for block in late]
-    late = [summed(*to_replicas(block)).astype(bf16) for block in late]
-    filter_weight_grad, small_grad = [joined(from_replicas(block)) for block in late]
-    output_grad, gate_weight_grad = [joined(block) for block in early]
-    input_grad = jnp.concatenate([filter_weight_grad, gate_weight_grad], axis=1)
-    at = 0
-    taken = []
-    for count in (KERNEL, 1, 1, 1, STATES, RANK, RANK + 2 * STATES, 1):
-        taken.append(small_grad[at : at + count])
-        at += count
-    g_filter, g_fbias, g_sbias, g_skip, g_decay, g_step, g_select, g_gain = taken
+    halo_grad, own_block, late = after((halo_grad, own_block, late))
+    halo_grad = halo_grad.reshape(HALO, SEQS, D)
+    small = [
+        filter_grad, filter_bias_grad, bias_grad, skip_grad, decay_grad, step_grad, select_grad, gain_grad,
+    ]
+    (
+        input_grad, output_grad, g_filter, g_fbias, g_sbias, g_skip, g_decay, g_step, g_select, g_gain, following,
+    ) = tail(one_hot, [own_block] + late, small, halo_grad, early)
+    following = jnp.swapaxes(following.reshape(HALO, half, D), 0, 1)
+    prompt_grad = prompt_grad.at[:, steps - HALO :].add(following)
+    if split > 1:
+        own = jnp.swapaxes(halo_grad[:, half:], 0, 1).reshape(sequels, split, HALO, D)
+        own = jnp.pad(own[:, 1:], ((0, 0), (0, 1), (0, 0), (0, 0))).reshape(half, HALO, D)
+        piece_grad = piece_grad.at[:, steps - HALO :].add(own)
     return (
-        result[:half],
-        result[half:].reshape(sequel_hidden.shape),
-        main[:half],
-        main[half:].reshape(sequel_hidden.shape),
-        g_gain[0, : norm_gain.shape[0]],
+        prompt_out,
+        piece_out.reshape(sequel_hidden.shape),
+        prompt_grad,
+        piece_grad.reshape(sequel_hidden.shape),
+        g_gain[0],
         input_grad,
         g_filter,
         g_fbias[0],

time: 707 us -> 570 us (0.81)
  Pallas kernels: 244 us -> 393 us
  waiting for transfers between devices: 103 us -> 15.5 us
  blocking collectives: 61.2 us -> 0 us
  other arithmetic: 70.6 us -> 16 us
  starting transfers between devices: 49.8 us -> 17.6 us
  local copies, waits for them, and re-layouts: 68.6 us -> 40.7 us
  between operations: 15.3 us -> 1.85 us
  matrix products: 86.9 us -> 74.7 us
    pallas_call x0 -> x5, Pallas kernels: none -> 148 us  [the longest x1 66.1 us: gather(): pl.pallas_call(gather_kernel, in_specs=[vmem] * 4, out_specs=[hbm] * 4, o...]
    all_gather x4 -> x0, blocking collectives: 61.2 us -> none  [the longest x1 22.7 us: body(): moved, totals = lax.all_gather((moved, total[:half]), 'fsdp')]
    all_gather x3 -> x0, waiting for transfers between devices: 48.2 us -> none  [the longest x2 35.2 us: gathered(): return lax.all_gather(block, 'fsdp', axis=axis, tiled=True)]
    ppermute x40 -> x15, waiting for transfers between devices: 53 us -> 15.5 us  [exchanged(): lax.ppermute(block, axis, [(i, i ^ distance) for i in range(lax.axis_size...]
    ppermute x40 -> x15, starting transfers between devices: 49.7 us -> 17.6 us  [exchanged(): lax.ppermute(block, axis, [(i, i ^ distance) for i in range(lax.axis_size...]
    concatenate x9 -> x1, local copies, waits for them, and re-layouts: 12 us -> 1.46 us  [body(): jnp.concatenate([step_weight, tail_rows.reshape(-1, width), filter_weight...]
    another operation x11 -> x0, other arithmetic: 8.46 us -> none
    select_n x3 -> x0, other arithmetic: 8.31 us -> none  [the longest x1 5.14 us: body(): end = jnp.where(here == k, back, end)]
  transfers between devices with their start and end apart: 44 -> 15, of which waited for: 19 -> 1; matrix products, arithmetic and copies ran while one was open for 24% -> 7% of each run, Pallas kernels for 23% -> 22%
where the time goes in v1:
time: 570 us; the launch traced here: 559 us
  Pallas kernels  393 us (69%)
  matrix products  74.7 us (13%)
  local copies, waits for them, and re-layouts  40.7 us (7%)
  starting transfers between devices  17.6 us (3%)
  other arithmetic  16 us (3%)
  waiting for transfers between devices  15.5 us (3%)
    pallas_call x1, Pallas kernels, backward(): pl.pallas_call(backward_kernel, grid=(grid,), in_specs=[pl.BlockSpec((ste...  90.8 us
    pallas_call x1, Pallas kernels, gather(): pl.pallas_call(gather_kernel, in_specs=[vmem] * 4, out_specs=[hbm] * 4, o...  66.1 us
    pallas_call x1, Pallas kernels, piece(): pl.pallas_call(piece_kernel, grid=(grid,), in_specs=[pl.BlockSpec((steps...  65.4 us
    pallas_call x1, Pallas kernels, forward(): pl.pallas_call(forward_kernel, grid=(grid,), in_specs=[pl.BlockSpec((step...  51.5 us
    pallas_call x1, Pallas kernels, tail(): pl.pallas_call(tail_kernel, in_specs=[pl.BlockSpec(memory_space=pltpu.SME...  36.4 us
    dot_general x3, matrix products, contract_rows(): lax.dot_general(left_side, right_side, (((0,), (0,)), ((), ())), preferre...  26.1 us
    pallas_call x1, Pallas kernels, chain(): pl.pallas_call(chain_kernel, in_specs=[pl.BlockSpec(memory_space=pltpu.SM...  24.8 us
    dot_general x3, matrix products, contract_cols(): lax.dot_general(left_side, right_side, (((1,), (1,)), ((), ())), preferre...  23.6 us
  transfers between devices with their start and end apart: 15, of which 1 were waited for; matrix products, arithmetic and copies ran while one was open for 7% of the time, Pallas kernels for 22%

profile of v1, /device:TPU:0, one launch (start us, length us, event | category | flops | bytes accessed | tf_op | source)
XLA Modules:
  0.0 559.0 jit_solution(8526644586380704858)
XLA Ops:
  8.8 66.1 %gather.7 = (bf16[1024,256]{1,0:T(8,128)(2,1)}, bf16[2048,128]{1,0:T(8,128)(2,1)}, bf16[2048,1024]{1,0:T(8,128)(2,1)}, bf16[1024,4096]{1,0:T(8,128)(2,1)}) custom-call(bf16[128,256]{1,0:T(8,128)(2,1)} %pad.23.rows_ref, bf16[256,128]{1,0:T(8,128)(2,1)} %fusion.22.select_ref, bf16[256,1024]{1,0:T(8,128)(2,1)} %out_ref.1, bf16[128,4096]{1,0:T(8,128)(2,1)} %in_ref.1), custom_call_target="tpu_custom_call" | custom-call | flops 54999998464 | tf_op jit(solution)/shard_map/gather/pallas_call | solution.py:1027
  80.6 8.2 %prepare.1 = (bf16[1056,1024]{1,0:T(8,128)(2,1)}, bf16[1024,1024]{1,0:T(8,128)(2,1)}) custom-call(bf16[4,128,1024]{2,1,0:T(8,128)(2,1)} %prompt_ref.3, bf16[4,128,1024]{2,1,0:T(8,128)(2,1)} %piece_ref.3, bf16[4,128,1024]{2,1,0:T(8,128)(2,1)} %prompt_cot_ref.3, bf16[4,128,1024]{2,1,0:T(8,128)(2,1)} %piece_cot_ref.3, f32[32,1024]{1,0:T(8,128)} %bitcast_convert_fusion.halo_ref, ...), custom_call_target="tpu_custom_call" | custom-call | flops 5000000000 | tf_op jit(solution)/shard_map/prepare/pallas_call | solution.py:79
  88.8 9.7 %fusion.15.mix_ref = bf16[132,8,2048]{2,1,0:T(8,128)(2,1)} fusion(bf16[1056,1024]{1,0:T(8,128)(2,1)} %get-tuple-element.100, bf16[1024,4096]{1,0:T(8,128)(2,1)} %get-tuple-element.101), kind=kOutput, calls=%fused_computation.23 | convolution fusion | flops 4431347712 | bytes 10682368 | tf_op jit(solution)/shard_map/dot_general | solution.py:1335
  98.5 9.2 %convolution_bitcast_fusion.gate_ref = f32[132,8,2048]{2,1,0:T(8,128)} fusion(bf16[1056,1024]{1,0:T(8,128)(2,1)S(1)} %copy-done.21, bf16[1024,4096]{1,0:T(8,128)(2,1)} %get-tuple-element.101), kind=kOutput, calls=%fused_computation.2 | convolution fusion | flops 4429185024 | bytes 15007744 | tf_op jit(solution)/shard_map/dot_general | solution.py:1336
  111.8 10.7 %convolution_bitcast_fusion.1.gg_ref = f32[128,8,2048]{2,1,0:T(8,128)} fusion(bf16[1024,1024]{1,0:T(8,128)(2,1)} %get-tuple-element.105, bf16[2048,1024]{1,0:T(8,128)(2,1)} %get-tuple-element.106), kind=kOutput, calls=%fused_computation.7 | convolution fusion | flops 4294967296 | bytes 14680064 | tf_op jit(solution)/shard_map/dot_general | solution.py:1231
  122.5 15.6 %front.1 = (f32[128,8,2048]{2,1,0:T(8,128)}, f32[1024,128]{1,0:T(8,128)}) custom-call(bf16[132,8,2048]{2,1,0:T(8,128)(2,1)} %fusion.15.mix_ref, f32[4,2048]{1,0:T(4,128)} %bitcast.132, f32[1,2048]{1,0:T(1,128)} %bitcast.135, bf16[2048,128]{1,0:T(8,128)(2,1)} %get-tuple-element.102.sel_ref), custom_call_target="tpu_custom_call" | custom-call | flops 16000000000 | tf_op jit(solution)/shard_map/front/pallas_call | solution.py:199
  138.1 65.4 %piece.1 = (f32[128,8,2048]{2,1,0:T(8,128)}, bf16[128,8,2048]{2,1,0:T(8,128)(2,1)}, f32[128,8,2048]{2,1,0:T(8,128)}, bf16[128,8,2048]{2,1,0:T(8,128)(2,1)}, bf16...) custom-call(f32[1024,128]{1,0:T(8,128)} %get-tuple-element.104.proj_ref, ...), custom_call_target="tpu_custom_call" | custom-call | flops 60000002048 | tf_op jit(solution)/shard_map/piece/pallas_call | solution.py:397
  203.5 2.3 fusion.34
  206.4 24.8 %chain.1 = (f32[8,16,2048]{2,1,0:T(8,128)}, f32[8,16,2048]{2,1,0:T(8,128)}) custom-call(f32[4,4]{1,0:T(4,128)} %fusion.29.one_hot_ref, f32[4,16,2048]{2,1,0:T(8,128)} %get-tuple-element.110.ahead_ref, f32[4,16,2048]{2,1,0:T(8,128)} %get-tuple-element.186.behind_ref, f32[4,16,2048]{2,1,0:T(8,128)} %get-tuple-element.185.branch_ref, ...), custom_call_target="tpu_custom_call" | custom-call | flops 24999999488 | tf_op jit(solution)/shard_map/chain/pallas_call | solution.py:544
  231.2 51.5 %forward_scan.1 = (bf16[128,8,2048]{2,1,0:T(8,128)(2,1)}, bf16[8,2,129,8,16,128]{5,4,3,2,1,0:T(8,128)(2,1)}, bf16[132,8,2048]{2,1,0:T(8,128)(2,1)}, f32[1,2048]{1,0:T(1,128)}) custom-call(f32[1024,128]{1,0:T(8,128)} %get-tuple-element.104.proj_ref, f32[128,8,2048]{2,1,0:T(8,128)} %get-tuple-element.107.dt_ref, f32[128,8,2048]{2,1,0:T(8,128)} %get-tuple-element.103.act_ref, ...), custom_call_target="tpu_custom_call" | custom-call | flops 49999998976 | tf_op jit(solution)/shard_map/forward_scan/pallas_call | solution.py:622
  282.6 9.5 %convolution_convert_fusion.2 = bf16[2048,1024]{1,0:T(8,128)(2,1)} fusion(bf16[1024,1024]{1,0:T(8,128)(2,1)} %get-tuple-element.105, bf16[128,8,2048]{2,1,0:T(8,128)(2,1)} %get-tuple-element.117), kind=kOutput, calls=%fused_computation.17 | convolution fusion | flops 4297064448 | bytes 10485760 | tf_op jit(solution)/shard_map/dot_general | solution.py:1225
  292.1 3.2 dynamic-slice_bitcast_fusion.2
  296.4 8.3 %fusion.7 = bf16[1024,2048]{1,0:T(8,128)(2,1)S(1)} fusion(bf16[1056,1024]{1,0:T(8,128)(2,1)S(1)} %copy-done.22, bf16[132,8,2048]{2,1,0:T(8,128)(2,1)} %get-tuple-element.118), kind=kOutput, calls=%fused_computation.15 | convolution fusion | flops 4431282176 | bytes 10682368 | tf_op jit(solution)/shard_map/dot_general | solution.py:1225
  304.7 1.9 copy-done.3
  311.0 3.4 fusion.6
  316.0 1.7 dynamic-slice_bitcast_fusion.3
  321.3 90.8 %backward_scan.1 = (f32[128,8,2048]{2,1,0:T(8,128)}, f32[64,2048]{1,0:T(8,128)}, f32[1,2048]{1,0:T(1,128)}, f32[16,2048]{1,0:T(8,128)}, bf16[1024,128]{1,0:T(8,128)(2,1)}) custom-call(f32[1024,128]{1,0:T(8,128)} %get-tuple-element.104.proj_ref, f32[128,8,2048]{2,1,0:T(8,128)} %get-tuple-element.107.dt_ref, bf16[128,8,2048]{2,1,0:T(8,128)(2,1)} %get-tuple-element.108.sig_ref, ...), custom_call_target="tpu_custom_call" | custom-call | flops 89999998976 | tf_op jit(solution)/shard_map/backward_scan/pallas_call | solution.py:778
  412.1 2.5 convert_add_fusion.3
  416.3 1.6 collective-permute-start.5
  417.9 2.6 collective-permute-start.6
  420.7 21.6 %filter_back.1 = (bf16[132,8,2048]{2,1,0:T(8,128)(2,1)}, f32[128,2048]{1,0:T(8,128)}, f32[4,2048]{1,0:T(4,128)}, f32[1,2048]{1,0:T(1,128)}) custom-call(bf16[132,8,2048]{2,1,0:T(8,128)(2,1)} %fusion.15.mix_ref, f32[128,8,2048]{2,1,0:T(8,128)} %get-tuple-element.103.act_ref, f32[128,8,2048]{2,1,0:T(8,128)} %get-tuple-element.121.act_grad_ref, ...), custom_call_target="tpu_custom_call" | custom-call | flops 20000000000 | tf_op jit(solution)/shard_map/filter_back/pallas_call | solution.py:886
  443.5 8.3 %convolution_convert_fusion.1 = bf16[1024,2048]{1,0:T(8,128)(2,1)S(1)} fusion(bf16[1056,1024]{1,0:T(8,128)(2,1)} %get-tuple-element.100, bf16[132,8,2048]{2,1,0:T(8,128)(2,1)} %get-tuple-element.132), kind=kOutput, calls=%fused_computation.16 | convolution fusion | flops 4431282176 | bytes 10682368 | tf_op jit(solution)/shard_map/dot_general | solution.py:1225
  452.4 6.6 %fusion.more_ref.more_halo_ref = f32[1056,1024]{1,0:T(8,128)} fusion(bf16[132,8,2048]{2,1,0:T(8,128)(2,1)S(1)} %bitcast.150, bf16[1024,4096]{1,0:T(8,128)(2,1)S(1)} %bitcast.152), kind=kOutput, calls=%fused_computation.3 | convolution fusion | flops 4429185024 | bytes 12845056 | tf_op jit(solution)/shard_map/dot_general | solution.py:1231
  459.7 3.5 collective-permute-start.13
  464.4 6.3 %fusion.12.grad_ref.grad_halo_ref = f32[1056,1024]{1,0:T(8,128)} fusion(bf16[1056,2048]{1,0:T(8,128)(2,1)S(1)} %bitcast.145, bf16[1024,4096]{1,0:T(8,128)(2,1)S(1)} %bitcast.152), kind=kOutput, calls=%fused_computation.20 | convolution fusion | flops 4429185024 | bytes 12845056 | tf_op jit(solution)/shard_map/dot_general | solution.py:1231
  473.1 6.1 %fusion.36.mixed_ref = f32[1024,1024]{1,0:T(8,128)} fusion(bf16[1024,2048]{1,0:T(8,128)(2,1)S(1)} %bitcast.146, bf16[2048,1024]{1,0:T(8,128)(2,1)S(1)} %copy-done.23), kind=kOutput, calls=%fused_computation.88 | convolution fusion | flops 4294967296 | bytes 12582912 | tf_op jit(solution)/shard_map/dot_general | solution.py:1406
  479.1 1.8 collective-permute-start.11
  481.0 15.4 %collective-permute-done.10.b2 = bf16[128,2048]{1,0:T(8,128)(2,1)S(1)} collective-permute-done((bf16[128,2048]{1,0:T(8,128)(2,1)S(1)}, bf16[128,2048]{1,0:T(8,128)(2,1)S(1)}, u32[]{:S(2)}, u32[]{:S(2)}) %collective-permute-start.10) | collective-permute-done | bytes 524320 | tf_op jit(solution)/shard_map/ppermute | solution.py:1237
  497.7 12.5 %finish.1 = (bf16[4,128,1024]{2,1,0:T(8,128)(2,1)}, bf16[4,128,1024]{2,1,0:T(8,128)(2,1)}, f32[4,128,1024]{2,1,0:T(8,128)}, f32[4,128,1024]{2,1,0:T(8,128)}, f32[32,1024]{1,0:T(8,128)}, /*index=5*/f32[1,1024]{1,0:T(1,128)}) custom-call(f32[1024,1024]{1,0:T(8,128)} %fusion.36.mixed_ref, f32[1056,1024]{1,0:T(8,128)} %fusion.12.grad_ref.grad_halo_ref, ...), custom_call_target="tpu_custom_call" | custom-call | flops 8000000000 | tf_op jit(solution)/shard_map/finish/pallas_call | solution.py:145
  510.2 36.4 %tail.1 = (f32[128,4096]{1,0:T(8,128)}, f32[256,1024]{1,0:T(8,128)}, f32[4,256]{1,0:T(4,128)}, f32[1,256]{1,0:T(1,128)}, f32[1,256]{1,0:T(1,128)}, /*index=5*/f3...) custom-call(f32[4,4]{1,0:T(4,128)} %fusion.29.one_hot_ref, ...), custom_call_target="tpu_custom_call" | custom-call | flops 30000001024 | tf_op jit(solution)/shard_map/tail/pallas_call | solution.py:1199
  547.7 1.6 fusion.23
  550.3 3.1 copy.83
  (154 shorter events, 45.0 us)
Async XLA Ops:
  8.8 70.5 %copy-start.18 = (s32[4]{0:T(128)S(1)}, s32[4]{0:T(128)}, u32[]{:S(2)}) copy-start(s32[4]{0:T(128)} %param.19) | copy-start | bytes 52
  88.8 9.7 %copy-start.21 = (bf16[1056,1024]{1,0:T(8,128)(2,1)S(1)}, bf16[1056,1024]{1,0:T(8,128)(2,1)}, u32[]{:S(2)}) copy-start(bf16[1056,1024]{1,0:T(8,128)(2,1)} %get-tuple-element.100) | copy-start | bytes 6488068
  98.5 9.2 %copy-start.8 = (bf16[1024,256]{1,0:T(8,128)(2,1)S(1)}, bf16[1024,256]{1,0:T(8,128)(2,1)}, u32[]{:S(2)}) copy-start(bf16[1024,256]{1,0:T(8,128)(2,1)} %get-tuple-element.99) | copy-start | bytes 1572868
  98.5 9.9 %copy-start.7 = (bf16[2048,128]{1,0:T(8,128)(2,1)S(1)}, bf16[2048,128]{1,0:T(8,128)(2,1)}, u32[]{:S(2)}) copy-start(bf16[2048,128]{1,0:T(8,128)(2,1)} %get-tuple-element.102.sel_ref) | copy-start | bytes 1572868
  109.6 12.9 %copy-start.1 = (bf16[64,8,256]{0,2,1:T(8,128)(2,1)}, bf16[64,8,256]{0,2,1:T(8,128)(2,1)S(1)}, u32[]{:S(2)}) copy-start(bf16[64,8,256]{0,2,1:T(8,128)(2,1)S(1)} %copy.55) | copy-start | bytes 786436
  295.3 15.7 %collective-permute-start = (bf16[4,256,1024]{2,1,0:T(8,128)(2,1)}, bf16[4,256,1024]{2,1,0:T(8,128)(2,1)}, u32[]{:S(2)}, u32[]{:S(2)}) collective-permute-start(bf16[4,256,1024]{2,1,0:T(8,128)(2,1)} %dynamic-slice_bitcast_fusion.2), channel_id=1, source_target_pairs={{0,1},{1,0},{2,3},{3,2},{4,5},{5,4},{6,7},{7,6},{8,9},{9,8},{10,11... | collective-permute-start | bytes 6291464 | tf_op jit(solution)/shard_map/ppermute | solution.py:1237
  308.1 6.5 %collective-permute-start.1 = (bf16[4,128,2048]{2,1,0:T(8,128)(2,1)}, bf16[4,128,2048]{2,1,0:T(8,128)(2,1)S(1)}, u32[]{:S(2)}, u32[]{:S(2)}) collective-permute-start(bf16[4,128,2048]{2,1,0:T(8,128)(2,1)} %dynamic-slice_bitcast_fusion.1), channel_id=1, source_target_pairs={{0,1},{1,0},{2,3},{3,2},{4,5},{5,4},{6,7},{7,6},{8,9},{9,8},{10,11... | collective-permute-start | bytes 6291464 | tf_op jit(solution)/shard_map/ppermute | solution.py:1237
  317.8 94.3 %collective-permute-start.2 = (bf16[256,2048]{1,0:T(8,128)(2,1)}, bf16[256,2048]{1,0:T(8,128)(2,1)}, u32[]{:S(2)}, u32[]{:S(2)}) collective-permute-start(bf16[256,2048]{1,0:T(8,128)(2,1)} %get-tuple-element.174), channel_id=1, source_target_pairs={{0,2},{1,3},{2,0},{3,1},{4,6},{5,7},{6,4},{7,5},{8,10},{9,11},{10,... | collective-permute-start | bytes 3145736 | tf_op jit(solution)/shard_map/ppermute | solution.py:1237
  319.1 93.0 %collective-permute-start.3 = (bf16[256,2048]{1,0:T(8,128)(2,1)}, bf16[256,2048]{1,0:T(8,128)(2,1)}, u32[]{:S(2)}, u32[]{:S(2)}) collective-permute-start(bf16[256,2048]{1,0:T(8,128)(2,1)} %get-tuple-element.173), channel_id=1, source_target_pairs={{0,4},{1,5},{2,6},{3,7},{4,0},{5,1},{6,2},{7,3},{8,12},{9,13},{10,... | collective-permute-start | bytes 3145736 | tf_op jit(solution)/shard_map/ppermute | solution.py:1237
  320.2 91.9 %collective-permute-start.4 = (bf16[256,2048]{1,0:T(8,128)(2,1)}, bf16[256,2048]{1,0:T(8,128)(2,1)}, u32[]{:S(2)}, u32[]{:S(2)}) collective-permute-start(bf16[256,2048]{1,0:T(8,128)(2,1)} %get-tuple-element.172), channel_id=1, source_target_pairs={{0,6},{1,7},{2,4},{3,5},{4,2},{5,3},{6,0},{7,1},{8,14},{9,15},{10,... | collective-permute-start | bytes 3145736 | tf_op jit(solution)/shard_map/ppermute | solution.py:1237
  416.3 27.2 %collective-permute-start.5 = (bf16[64,2048]{1,0:T(8,128)(2,1)S(1)}, bf16[64,2048]{1,0:T(8,128)(2,1)S(1)}, u32[]{:S(2)}, u32[]{:S(2)}) collective-permute-start(bf16[64,2048]{1,0:T(8,128)(2,1)S(1)} %get-tuple-element.184), channel_id=1, source_target_pairs={{0,8},{8,0},{16,24},{24,16},{1,9},{9,1},{17,25},{25,17},{2,10},{10... | collective-permute-start | bytes 786440 | tf_op jit(solution)/shard_map/ppermute | solution.py:1237
  417.9 25.5 %collective-permute-start.6 = (bf16[64,2048]{1,0:T(8,128)(2,1)S(1)}, bf16[64,2048]{1,0:T(8,128)(2,1)S(1)}, u32[]{:S(2)}, u32[]{:S(2)}) collective-permute-start(bf16[64,2048]{1,0:T(8,128)(2,1)S(1)} %get-tuple-element.183), channel_id=1, source_target_pairs={{0,16},{8,24},{16,0},{24,8},{1,17},{9,25},{17,1},{25,9},{2,18},{10... | collective-permute-start | bytes 786440 | tf_op jit(solution)/shard_map/ppermute | solution.py:1237
  420.5 22.9 %collective-permute-start.7 = (bf16[64,2048]{1,0:T(8,128)(2,1)S(1)}, bf16[64,2048]{1,0:T(8,128)(2,1)S(1)}, u32[]{:S(2)}, u32[]{:S(2)}) collective-permute-start(bf16[64,2048]{1,0:T(8,128)(2,1)S(1)} %get-tuple-element.182), channel_id=1, source_target_pairs={{0,24},{8,16},{16,8},{24,0},{1,25},{9,17},{17,9},{25,1},{2,26},{10... | collective-permute-start | bytes 786440 | tf_op jit(solution)/shard_map/ppermute | solution.py:1237
  443.5 8.9 %slice-start.2 = ((s8[4325376]{0:T(1024)(128)(4,1)}), s8[4194304]{0:T(1024)(128)(4,1)S(1)}, s32[]{:S(2)}) async-start(s8[4325376]{0:T(1024)(128)(4,1)} %bitcast.149), calls=%async_computation.2 | async-start | bytes 8388608
  443.5 8.9 %slice-start.4 = ((s8[8388608]{0:T(1024)(128)(4,1)}), s8[4194304]{0:T(1024)(128)(4,1)S(1)}, s32[]{:S(2)}) async-start(s8[8388608]{0:T(1024)(128)(4,1)} %bitcast.151), calls=%async_computation.4 | async-start | bytes 8388608
  443.5 8.9 %slice-start.3 = ((s8[4325376]{0:T(1024)(128)(4,1)}), s8[131072]{0:T(1024)(128)(4,1)S(1)}, s32[]{:S(2)}) async-start(s8[4325376]{0:T(1024)(128)(4,1)} %bitcast.149), calls=%async_computation.3 | async-start | bytes 262144
  443.5 8.9 %slice-start.5 = ((s8[8388608]{0:T(1024)(128)(4,1)}), s8[4194304]{0:T(1024)(128)(4,1)S(1)}, s32[]{:S(2)}) async-start(s8[8388608]{0:T(1024)(128)(4,1)} %bitcast.151), calls=%async_computation.5 | async-start | bytes 8388608
  452.0 11.2 %copy-start.10 = (bf16[64,2048]{1,0:T(8,128)(2,1)}, bf16[64,2048]{1,0:T(8,128)(2,1)S(1)}, u32[]{:S(2)}) copy-start(bf16[64,2048]{1,0:T(8,128)(2,1)S(1)} %add_convert_fusion.rest_0_) | copy-start | bytes 786436
  452.0 12.3 %slice-start = ((s8[4325376]{0:T(1024)(128)(4,1)}), s8[4194304]{0:T(1024)(128)(4,1)S(1)}, s32[]{:S(2)}) async-start(s8[4325376]{0:T(1024)(128)(4,1)} %bitcast.143), calls=%async_computation | async-start | bytes 8388608
  452.2 12.1 %slice-start.1 = ((s8[4325376]{0:T(1024)(128)(4,1)}), s8[131072]{0:T(1024)(128)(4,1)S(1)}, s32[]{:S(2)}) async-start(s8[4325376]{0:T(1024)(128)(4,1)} %bitcast.143), calls=%async_computation.1 | async-start | bytes 262144
  452.3 11.1 %collective-permute-start.8 = (bf16[4,128,2048]{2,1,0:T(8,128)(2,1)S(1)}, bf16[4,128,2048]{2,1,0:T(8,128)(2,1)S(1)}, u32[]{:S(2)}, u32[]{:S(2)}) collective-permute-start(bf16[4,128,2048]{2,1,0:T(8,128)(2,1)S(1)} %dynamic-slice_bitcast_fusion), channel_id=1, source_target_pairs={{0,1},{1,0},{2,3},{3,2},{4,5},{5,4},{6,7},{7,6},{8,9},{9,8},{10,11... | collective-permute-start | bytes 6291464 | tf_op jit(solution)/shard_map/ppermute | solution.py:1237
  459.0 51.2 %collective-permute-start.12 = (bf16[64,2048]{1,0:T(8,128)(2,1)S(1)}, bf16[64,2048]{1,0:T(8,128)(2,1)}, u32[]{:S(2)}, u32[]{:S(2)}) collective-permute-start(bf16[64,2048]{1,0:T(8,128)(2,1)S(1)} %add_convert_fusion.rest_0_), channel_id=1, source_target_pairs={{0,8},{8,0},{16,24},{24,16},{1,9},{9,1},{17,25},{25,17},{2,10},{10... | collective-permute-start | bytes 786440 | tf_op jit(solution)/shard_map/ppermute | solution.py:1237
  459.7 50.5 %collective-permute-start.13 = (bf16[64,2048]{1,0:T(8,128)(2,1)S(1)}, bf16[64,2048]{1,0:T(8,128)(2,1)}, u32[]{:S(2)}, u32[]{:S(2)}) collective-permute-start(bf16[64,2048]{1,0:T(8,128)(2,1)S(1)} %add_convert_fusion.rest_0_), channel_id=1, source_target_pairs={{0,16},{8,24},{16,0},{24,8},{1,17},{9,25},{17,1},{25,9},{2,18},{10... | collective-permute-start | bytes 786440 | tf_op jit(solution)/shard_map/ppermute | solution.py:1237
  463.2 47.1 %collective-permute-start.14 = (bf16[64,2048]{1,0:T(8,128)(2,1)S(1)}, bf16[64,2048]{1,0:T(8,128)(2,1)}, u32[]{:S(2)}, u32[]{:S(2)}) collective-permute-start(bf16[64,2048]{1,0:T(8,128)(2,1)S(1)} %add_convert_fusion.rest_0_), channel_id=1, source_target_pairs={{0,24},{8,16},{16,8},{24,0},{1,25},{9,17},{17,9},{25,1},{2,26},{10... | collective-permute-start | bytes 786440 | tf_op jit(solution)/shard_map/ppermute | solution.py:1237
  471.6 24.8 %collective-permute-start.10 = (bf16[128,2048]{1,0:T(8,128)(2,1)S(1)}, bf16[128,2048]{1,0:T(8,128)(2,1)S(1)}, u32[]{:S(2)}, u32[]{:S(2)}) collective-permute-start(bf16[128,2048]{1,0:T(8,128)(2,1)S(1)} %get-tuple-element.177), channel_id=1, source_target_pairs={{0,4},{1,5},{2,6},{3,7},{4,0},{5,1},{6,2},{7,3},{8,12},{9,13},{10,... | collective-permute-start | bytes 1572872 | tf_op jit(solution)/shard_map/ppermute | solution.py:1237
  479.1 31.0 %collective-permute-start.11 = (bf16[128,2048]{1,0:T(8,128)(2,1)S(1)}, bf16[128,2048]{1,0:T(8,128)(2,1)}, u32[]{:S(2)}, u32[]{:S(2)}) collective-permute-start(bf16[128,2048]{1,0:T(8,128)(2,1)S(1)} %get-tuple-element.176), channel_id=1, source_target_pairs={{0,6},{1,7},{2,4},{3,5},{4,2},{5,3},{6,0},{7,1},{8,14},{9,15},{10,... | collective-permute-start | bytes 1572872 | tf_op jit(solution)/shard_map/ppermute | solution.py:1237
  496.4 13.8 %copy-start.19 = (bf16[128,2048]{1,0:T(8,128)(2,1)}, bf16[128,2048]{1,0:T(8,128)(2,1)S(1)}, u32[]{:S(2)}) copy-start(bf16[128,2048]{1,0:T(8,128)(2,1)S(1)} %collective-permute-done.10.b2) | copy-start | bytes 1572868
  496.4 13.8 %collective-permute-start.9 = (bf16[128,2048]{1,0:T(8,128)(2,1)S(1)}, bf16[128,2048]{1,0:T(8,128)(2,1)}, u32[]{:S(2)}, u32[]{:S(2)}) collective-permute-start(bf16[128,2048]{1,0:T(8,128)(2,1)S(1)} %get-tuple-element.178), channel_id=1, source_target_pairs={{0,2},{1,3},{2,0},{3,1},{4,6},{5,7},{6,4},{7,5},{8,10},{9,11},{10,... | collective-permute-start | bytes 1572872 | tf_op jit(solution)/shard_map/ppermute | solution.py:1237
  546.7 9.2 %copy-start.16 = (f32[1,256]{1,0:T(1,128)S(1)}, f32[1,256]{1,0:T(1,128)}, u32[]{:S(2)}) copy-start(f32[1,256]{1,0:T(1,128)} %get-tuple-element.168) | copy-start | bytes 3076
  546.7 9.8 %copy-start.13 = (f32[16,256]{1,0:T(8,128)S(1)}, f32[16,256]{1,0:T(8,128)}, u32[]{:S(2)}) copy-start(f32[16,256]{1,0:T(8,128)} %get-tuple-element.169) | copy-start | bytes 49156
  546.7 10.4 %copy-start.15 = (f32[1,256]{1,0:T(1,128)S(1)}, f32[1,256]{1,0:T(1,128)}, u32[]{:S(2)}) copy-start(f32[1,256]{1,0:T(1,128)} %get-tuple-element.170) | copy-start | bytes 3076
  546.7 10.9 %copy-start.5 = (f32[256,1024]{1,0:T(8,128)S(1)}, f32[256,1024]{1,0:T(8,128)}, u32[]{:S(2)}) copy-start(f32[256,1024]{1,0:T(8,128)} %get-tuple-element.219) | copy-start | bytes 3145732
  (13 other events, 63.1 us)

commit v2 on v1

--- a/solution.py
+++ b/solution.py
@@ -41,6 +41,42 @@
 
 def softplus(x):
     return jnp.maximum(x, 0.0) + jnp.log1p(jnp.exp(-jnp.abs(x)))
+
+
+def product_kernel(across, *refs):
+    lefts, rhs_ref, out_ref = refs[:-2], refs[-2], refs[-1]
+    total = None
+    at = 0
+    for left in lefts:
+        depth = left.shape[1]
+        rhs = rhs_ref[:, at : at + depth] if across else rhs_ref[at : at + depth]
+        dims = (((1,), (1 if across else 0,)), ((), ()))
+        term = lax.dot_general(left[...], rhs, dims, preferred_element_type=f32)
+        total = term if total is None else total + term
+        at += depth
+    out_ref[...] = total.astype(out_ref.dtype)
+
+
+def product(lefts, rhs, kind, across=False, part=0, parts=1):
+    rows = lefts[0].shape[0]
+    depth = sum(left.shape[1] for left in lefts)
+    if across:
+        columns = rhs.shape[0]
+        rhs_spec = pl.BlockSpec((WIDE, depth), lambda j: (j, 0))
+    else:
+        columns = rhs.shape[1] // parts
+        first = part * columns // WIDE
+        rhs_spec = pl.BlockSpec((depth, WIDE), lambda j: (0, first + j))
+    return pl.pallas_call(
+        functools.partial(product_kernel, across),
+        grid=(columns // WIDE,),
+        in_specs=[pl.BlockSpec(left.shape, lambda j: (0, 0)) for left in lefts] + [rhs_spec],
+        out_specs=pl.BlockSpec((rows, WIDE), lambda j: (0, j)),
+        out_shape=jax.ShapeDtypeStruct((rows, columns), kind),
+        compiler_params=params(),
+        cost_estimate=cost(0.01),
+        name="product",
+    )(*lefts, rhs)
 
 
 def scale_of(rows):
@@ -107,7 +143,7 @@
 
 
 def finish_kernel(
-    mixed_ref, grad_ref, more_ref, grad_halo_ref, more_halo_ref,
+    mixed_ref, grad_ref, grad_halo_ref,
     prompt_ref, piece_ref, prompt_cot_ref, piece_cot_ref, halo_ref, gain_ref,
     prompt_out, piece_out, prompt_grad, piece_grad, halo_grad, gain_grad,
 ):
@@ -116,7 +152,7 @@
 
     @pl.when(i == 0)
     def _():
-        back, sums = norm_back(halo_ref[...], grad_halo_ref[...] + more_halo_ref[...], gain)
+        back, sums = norm_back(halo_ref[...], grad_halo_ref[...], gain)
         halo_grad[...] = back
         gain_grad[...] = jnp.sum(sums, axis=0, keepdims=True)
 
@@ -124,7 +160,7 @@
     rows = by_time(prompt_ref, piece_ref)
     shape = rows.shape
     rows = rows.reshape(-1, D)
-    back, sums = norm_back(rows, grad_ref[...] + more_ref[...], gain)
+    back, sums = norm_back(rows, grad_ref[...], gain)
     gain_grad[...] += jnp.sum(sums, axis=0, keepdims=True)
     back = jnp.swapaxes(back.reshape(shape), 0, 1)
     prompt_grad[...] = back[:half] + prompt_cot_ref[...].astype(f32)
@@ -134,7 +170,7 @@
     piece_out[...] = mixed[half:].astype(bf16)
 
 
-def finish(mixed, grad, more, prompt, piece, prompt_cot, piece_cot, halo, gain):
+def finish(mixed, grad, prompt, piece, prompt_cot, piece_cot, halo, gain):
     steps = prompt.shape[1]
     part = pl.BlockSpec((SEQS // 2, CHUNK, D), lambda i: (0, i, 0))
     first = pl.BlockSpec((HALO * SEQS, D), lambda i: (0, 0))
@@ -147,7 +183,7 @@
         grid=(steps // CHUNK,),
         in_specs=[
             pl.BlockSpec((CHUNK * SEQS, D), lambda i: (i, 0)),
-            shifted, shifted, first, first,
+            shifted, first,
             part, part, part, part,
             first,
             pl.BlockSpec((1, D), lambda i: (0, 0)),
@@ -162,9 +198,9 @@
             jax.ShapeDtypeStruct((1, D), f32),
         ],
         compiler_params=params(),
-        cost_estimate=cost(8),
+        cost_estimate=cost(0.01),
         name="finish",
-    )(mixed, grad, more, grad, more, prompt, piece, prompt_cot, piece_cot, halo, gain)
+    )(mixed, grad, grad, prompt, piece, prompt_cot, piece_cot, halo, gain)
 
 
 def front_kernel(mix_ref, fw_ref, fb_ref, sel_ref, act_ref, proj_ref):
@@ -324,26 +360,7 @@
     total = lax.fori_loop(0, steps // chunk, prep, jnp.zeros((SEQS, WIDE), f32))
     tot_ref[...] = total
 
-    def weighted(rates, vectors, map_at, out):
-        acc_scr[...] = jnp.zeros_like(acc_scr)
-
-        def run(i, _):
-            sums = [None] * PAIRS
-            for k in range(RUN):
-                t = i * RUN + k
-                time, drive = vectors(t)
-                for p in range(PAIRS):
-                    term = jnp.exp2(time * rates[p]) * drive * map_at(t, p)
-                    sums[p] = term if k == 0 else sums[p] + term
-            for p in range(PAIRS):
-                a, b = halves(sums[p])
-                acc_scr[2 * p] += a
-                acc_scr[2 * p + 1] += b
-            return 0
-
-        lax.fori_loop(0, steps // RUN, run, 0)
-        for n in range(STATES):
-            out(n, acc_scr[n])
+    units = []
 
     low = lax.broadcasted_iota(jnp.int32, (SEQS, LANES), 0) < half
     packed = [
@@ -351,7 +368,8 @@
         for n in range(STATES)
     ]
     packed = [pair(packed[2 * p], packed[2 * p + 1]) for p in range(PAIRS)]
-    for group in range(groups):
+
+    def forward_unit(group):
         rows = slice(group * half, (group + 1) * half)
 
         def pack(v):
@@ -361,31 +379,50 @@
 
         def vectors(t):
             return both(whole - pack(time_scr[t])), both(pack(dt_ref[t] * act_ref[t]))
-
-        def map_at(t, p):
-            return b_scr[group, t, p]
 
         def out(n, value):
             fwd_ref[rows, n, :LANES] = value[:half]
             fwd_ref[rows, n, LANES:] = value[half:]
 
-        weighted(packed, vectors, map_at, out)
-
-    for part in range(WIDE // LANES):
-        cols = slice(part * LANES, (part + 1) * LANES)
+        return packed, vectors, lambda t, p: b_scr[group, t, p], out
+
+    def backward_unit(cols):
         mine = [jnp.broadcast_to(rate_ref[n : n + 1, cols], (SEQS, LANES)) for n in range(STATES)]
         mine = [pair(mine[2 * p], mine[2 * p + 1]) for p in range(PAIRS)]
 
         def vectors(t):
             return both(time_scr[t, :, cols]), both(yg_ref[t, :, cols])
 
-        def map_at(t, p):
-            return c_scr[t, p]
-
         def out(n, value):
             bwd_ref[:, n, cols] = value
 
-        weighted(mine, vectors, map_at, out)
+        return mine, vectors, lambda t, p: c_scr[t, p], out
+
+    for group in range(groups):
+        units.append(forward_unit(group))
+    for part in range(WIDE // LANES):
+        units.append(backward_unit(slice(part * LANES, (part + 1) * LANES)))
+    acc_scr[...] = jnp.zeros_like(acc_scr)
+
+    def run(i, _):
+        for k, (rates, vectors, map_at, _) in enumerate(units):
+            sums = [None] * PAIRS
+            for m in range(RUN):
+                t = i * RUN + m
+                time, drive = vectors(t)
+                for p in range(PAIRS):
+                    term = jnp.exp2(time * rates[p]) * drive * map_at(t, p)
+                    sums[p] = term if m == 0 else sums[p] + term
+            for p in range(PAIRS):
+                a, b = halves(sums[p])
+                acc_scr[k, 2 * p] += a
+                acc_scr[k, 2 * p + 1] += b
+        return 0
+
+    lax.fori_loop(0, steps // RUN, run, 0)
+    for k, (_, _, _, out) in enumerate(units):
+        for n in range(STATES):
+            out(n, acc_scr[k, n])
 
 
 def piece(proj, act, gate, gated_grad, step_pad, sbias, rate, select, groups):
@@ -427,7 +464,7 @@
             pltpu.VMEM((groups, steps, PAIRS, 2 * SEQS, LANES), bf16),
             pltpu.VMEM((steps, PAIRS, 2 * SEQS, LANES), bf16),
             pltpu.VMEM((steps, SEQS, WIDE), f32),
-            pltpu.VMEM((STATES, SEQS, LANES), f32),
+            pltpu.VMEM((groups + WIDE // LANES, STATES, SEQS, LANES), f32),
         ],
         compiler_params=params(),
         cost_estimate=cost(60),
@@ -1052,17 +1089,12 @@
 
 def tail_kernel(
     one_hot_ref, b0, b1, b2, b3, filter_ref, fbias_ref, sbias_ref, skip_ref, decay_ref, step_ref, select_ref,
-    gain_ref, halo_ref, *rest,
+    gain_ref, halo_ref, block_out, small_out, rim_out,
+    total, to_z, from_z, part, parts, small_f, small_ref, got_small, small_z, small_from_z, small_part,
+    small_parts, rim, child, got_rim, got_child,
+    sems_s, sems_z, sems_p, sems_sz, sems_sp, sems_r, sems_cs, sems_cr,
 ):
     depth = lax.axis_size("replica")
-    early_refs, rest = rest[:depth], rest[depth:]
-    (
-        in_out, out_out, filter_out, fbias_out, sbias_out, skip_out, decay_out, step_out, select_out, gain_out,
-        rim_out,
-        total, to_z, from_z, part, parts, small_f, small_ref, got_small, small_z, small_from_z, small_part,
-        small_parts, rim, child, got_rim, got_child, early,
-        sems_s, sems_z, sems_p, sems_sz, sems_sp, sems_r, sems_cs, sems_cr,
-    ) = rest
     me, size = lax.axis_index("fsdp"), lax.axis_size("fsdp")
     mz = lax.axis_index("replica")
     last = size - 1
@@ -1148,24 +1180,8 @@
         q_copies.append(copy)
     for copy in p_copies + q_copies:
         copy.wait()
-    half = in_out.shape[1] // 2
-    in_out[:, 0:half] = parts[...].reshape(in_out.shape[0], half).astype(f32)
-    small = small_parts[...].reshape(SMALL_ROWS, width).astype(f32)
-    at = 0
-    for out, count in zip(
-        (filter_out, fbias_out, sbias_out, skip_out, decay_out, step_out, select_out, gain_out), SMALL
-    ):
-        out[...] = small[at : at + count, 0 : out.shape[1]]
-        at += count
-    for d, ref in enumerate(early_refs):
-        count = ref.shape[0]
-        total_rows = pl.ds(pl.multiple_of(xor(mz, d) * count, count), count)
-        early[total_rows, :] = ref[...].astype(f32)
-    rows = out_out.shape[0] // 2
-    features = out_out.shape[1]
-    out_out[0:rows, :] = early[0:rows, 0:features]
-    out_out[rows:, :] = early[0:rows, features:]
-    in_out[:, half:] = early[rows:, :]
+    block_out[...] = parts[...].reshape(block_out.shape)
+    small_out[...] = small_parts[...].reshape(small_out.shape)
     to_left.wait()
 
     @pl.when(me != last)
@@ -1182,7 +1198,7 @@
         rim_out[...] = sums
 
 
-def tail(one_hot, blocks, small, halo_grad, early):
+def tail(one_hot, blocks, small, halo_grad):
     size, depth = lax.axis_size("fsdp"), lax.axis_size("replica")
     vmem = pl.BlockSpec(memory_space=pltpu.VMEM)
     dma = pltpu.SemaphoreType.DMA
@@ -1195,14 +1211,14 @@
     by_owner = (size, SMALL_ROWS, width)
     small_cut = (depth, SMALL_ROWS // depth, width)
     rim = (HALO * PROMPTS, features)
-    counts = [(count, width) for count in SMALL[:-1]] + [(1, features // size)]
     return pl.pallas_call(
         tail_kernel,
-        in_specs=[pl.BlockSpec(memory_space=pltpu.SMEM)] + [vmem] * (4 + len(small) + 1 + depth),
-        out_specs=[vmem] * (3 + len(counts)),
+        in_specs=[pl.BlockSpec(memory_space=pltpu.SMEM)] + [vmem] * (4 + len(small) + 1),
+        out_specs=[vmem] * 3,
         out_shape=[
-            jax.ShapeDtypeStruct(shape, f32)
-            for shape in [(rows, 2 * channels), (2 * rows, features)] + counts + [rim]
+            jax.ShapeDtypeStruct((rows, channels), bf16),
+            jax.ShapeDtypeStruct((SMALL_ROWS, width), bf16),
+            jax.ShapeDtypeStruct(rim, f32),
         ],
         scratch_shapes=[
             pltpu.VMEM(cut, f32), pltpu.VMEM(cut, bf16), pltpu.VMEM(cut, bf16),
@@ -1211,14 +1227,73 @@
             pltpu.VMEM(small_cut, f32), pltpu.VMEM(small_cut, bf16),
             pltpu.VMEM(small_cut, bf16), pltpu.VMEM(small_cut, bf16),
             pltpu.VMEM(rim, f32), pltpu.VMEM(rim, f32), pltpu.VMEM(rim, f32), pltpu.VMEM((size,) + rim, f32),
-            pltpu.VMEM((2 * rows, channels), f32),
             dma((2, size)), dma((2, depth)), dma((2, depth)), dma((2, depth)), dma((2, depth)),
             dma((2,)), dma((size,)), dma((size,)),
         ],
         compiler_params=params(collective_id=4, has_side_effects=True),
         cost_estimate=cost(30),
         name="tail",
-    )(one_hot, *blocks, *small, halo_grad, *early)
+    )(one_hot, *blocks, *small, halo_grad)
+
+
+def deliver_kernel(block_ref, small_ref, rim_ref, prompt_ref, *rest):
+    depth = lax.axis_size("replica")
+    early_refs, outs = rest[:depth], rest[depth:-1]
+    early = rest[-1]
+    in_out, out_out, prompt_out = outs[:3]
+    mz = lax.axis_index("replica")
+    half = in_out.shape[1] // 2
+    in_out[:, 0:half] = block_ref[...].astype(f32)
+    small = small_ref[...].astype(f32)
+    at = 0
+    for k, (out, count) in enumerate(zip(outs[3:], SMALL)):
+        rows = small[at : at + count]
+        if k in (4, 6):
+            rows = jnp.concatenate([rows, jnp.zeros((-count % LANES, rows.shape[1]), f32)], axis=0)
+            out[...] = rows.T[:, :count]
+        else:
+            out[...] = rows[:, 0 : out.shape[1]]
+        at += count
+    for d, ref in enumerate(early_refs):
+        count = ref.shape[0]
+        early[pl.ds(pl.multiple_of(xor(mz, d) * count, count), count), :] = ref[...].astype(f32)
+    rows = out_out.shape[0] // 2
+    features = out_out.shape[1]
+    out_out[0:rows, :] = early[0:rows, 0:features]
+    out_out[rows:, :] = early[0:rows, features:]
+    in_out[:, half:] = early[rows:, :]
+    for p in range(PROMPTS):
+        prompt_out[p, 0 : SEQS - HALO] = prompt_ref[p, 0 : SEQS - HALO]
+        for t in range(HALO):
+            row = SEQS - HALO + t
+            prompt_out[p, row : row + 1] = (
+                prompt_ref[p, row : row + 1] + rim_ref[t * PROMPTS + p : t * PROMPTS + p + 1]
+            )
+
+
+def deliver(block, small, rim, prompt_grad, early):
+    size = lax.axis_size("fsdp")
+    rows, channels = block.shape
+    width = small.shape[1]
+    features = prompt_grad.shape[2]
+    vmem = pl.BlockSpec(memory_space=pltpu.VMEM)
+    end = prompt_grad.shape[1] // SEQS - 1
+    last = pl.BlockSpec((PROMPTS, SEQS, features), lambda i: (0, end, 0))
+    shapes = [(count, width) for count in SMALL[:-1]] + [(1, features // size)]
+    shapes[4], shapes[6] = shapes[4][::-1], shapes[6][::-1]
+    shapes = [(rows, 2 * channels), (2 * rows, features), prompt_grad.shape] + shapes
+    return pl.pallas_call(
+        deliver_kernel,
+        grid=(1,),
+        in_specs=[vmem, vmem, vmem, last] + [vmem] * len(early),
+        out_specs=[vmem, vmem, last] + [vmem] * len(SMALL),
+        out_shape=[jax.ShapeDtypeStruct(shape, f32) for shape in shapes],
+        scratch_shapes=[pltpu.VMEM((2 * rows, channels), f32)],
+        input_output_aliases={3: 2},
+        compiler_params=params(),
+        cost_estimate=cost(4),
+        name="deliver",
+    )(block, small, rim, prompt_grad, *early)
 
 
 def contract_rows(left_side, right_side):
@@ -1270,12 +1345,6 @@
 
 def from_replicas(part):
     return [part] + [exchanged(part, "replica", d) for d in range(1, lax.axis_size("replica"))]
-
-
-def joined(parts):
-    here = lax.axis_index("replica")
-    parts = jnp.stack(parts)
-    return jnp.concatenate([pick_row(parts, here ^ i) for i in range(parts.shape[0])]).astype(f32)
 
 
 def body(
@@ -1332,11 +1401,11 @@
     piece_cot = sequel_cotangent.reshape(-1, steps, D)
     scaled, cotangent = prepare(prompt_hidden, pieces, prompt_cotangent, piece_cot, halo, gain)
 
-    mixture = jnp.dot(scaled, full_input[:, :INNER], preferred_element_type=f32).astype(bf16)
-    gate = jnp.dot(scaled, full_input[:, INNER:], preferred_element_type=f32)
+    mixture = product([scaled], full_input, bf16, part=0, parts=2)
+    gate = product([scaled], full_input, f32, part=1, parts=2)
     mixture = mixture.reshape(steps + HALO, SEQS, INNER)
     gate = gate.reshape(steps + HALO, SEQS, INNER)
-    gated_grad = contract_cols(cotangent, full_output).reshape(steps, SEQS, INNER)
+    gated_grad = product([cotangent], full_output, f32, across=True).reshape(steps, SEQS, INNER)
     act, proj = front(mixture, fw, fb, select_pad, steps)
     groups = 1 if split == 1 else 2
     lane = jnp.arange(2 * STATES * LANES)[None, :]
@@ -1399,24 +1468,22 @@
     filter_weight_grad, early = after((filter_weight_grad, early))
     late = over_cores(filter_weight_grad.reshape(size, -1, INNER))
     early = from_replicas(early)
-    more = contract_cols(gate_grad, full_input[:, INNER:])
-    late, more, filter_in_grad, gated = after((late, more, filter_in_grad, gated))
+    mixed = jnp.dot(gated, full_output, preferred_element_type=f32)
+    late, mixed, filter_in_grad = after((late, mixed, filter_in_grad))
     own_block, late = to_chips(late)
-    scaled_grad = contract_cols(filter_in_grad, full_input[:, :INNER])
-    mixed = jnp.dot(gated, full_output, preferred_element_type=f32)
+    scaled_grad = product([filter_in_grad, gate_grad], full_input, f32, across=True)
     prompt_out, piece_out, prompt_grad, piece_grad, halo_grad, gain_grad = finish(
-        mixed, scaled_grad, more, prompt_hidden, pieces, prompt_cotangent, piece_cot, halo, gain
+        mixed, scaled_grad, prompt_hidden, pieces, prompt_cotangent, piece_cot, halo, gain
     )
     halo_grad, own_block, late = after((halo_grad, own_block, late))
     halo_grad = halo_grad.reshape(HALO, SEQS, D)
     small = [
         filter_grad, filter_bias_grad, bias_grad, skip_grad, decay_grad, step_grad, select_grad, gain_grad,
     ]
+    block, small, following = tail(one_hot, [own_block] + late, small, halo_grad)
     (
-        input_grad, output_grad, g_filter, g_fbias, g_sbias, g_skip, g_decay, g_step, g_select, g_gain, following,
-    ) = tail(one_hot, [own_block] + late, small, halo_grad, early)
-    following = jnp.swapaxes(following.reshape(HALO, half, D), 0, 1)
-    prompt_grad = prompt_grad.at[:, steps - HALO :].add(following)
+        input_grad, output_grad, prompt_grad, g_filter, g_fbias, g_sbias, g_skip, g_decay, g_step, g_select, g_gain,
+    ) = deliver(block, small, following, prompt_grad, early)
     if split > 1:
         own = jnp.swapaxes(halo_grad[:, half:], 0, 1).reshape(sequels, split, HALO, D)
         own = jnp.pad(own[:, 1:], ((0, 0), (0, 1), (0, 0), (0, 0))).reshape(half, HALO, D)
@@ -1430,10 +1497,10 @@
         input_grad,
         g_filter,
         g_fbias[0],
-        g_select.T,
+        g_select,
         g_step,
         g_sbias[0],
-        g_decay.T,
+        g_decay,
         g_skip[0],
         output_grad,
     )

time: 570 us -> 544 us (0.954); the launches traced: 559 us -> 541 us
  Pallas kernels: 393 us -> 438 us
  matrix products: 74.7 us -> 32.2 us
  waiting for transfers between devices: 15.5 us -> 0.04 us
    pallas_call x0 -> x5, Pallas kernels: none -> 50.6 us  [the longest x4 47.1 us: product(): pl.pallas_call(functools.partial(product_kernel, across), grid=(columns /...]
    dot_general x5 -> x0, matrix products: 42.5 us -> none  [the longest x3 23.6 us: contract_cols(): lax.dot_general(left_side, right_side, (((1,), (1,)), ((), ())), preferre...]
    ppermute x15, waiting for transfers between devices: 15.5 us -> 0.04 us  [exchanged(): lax.ppermute(block, axis, [(i, i ^ distance) for i in range(lax.axis_size...]
    unnamed x73 -> x31, local copies, waits for them, and re-layouts: 14.1 us -> 10.8 us
  transfers between devices with their start and end apart: 15 -> 15, of which waited for: 1 -> 0; matrix products, arithmetic and copies ran while one was open for 7% -> 4% of each run, Pallas kernels for 22% -> 32%
where the time goes in v2:
time: 544 us; the launch traced here: 541 us
  Pallas kernels  438 us (81%)
  local copies, waits for them, and re-layouts  37.5 us (7%)
  matrix products  32.2 us (6%)
  starting transfers between devices  17 us (3%)
  other arithmetic  15.6 us (3%)
    pallas_call x1, Pallas kernels, backward(): pl.pallas_call(backward_kernel, grid=(grid,), in_specs=[pl.BlockSpec((ste...  90.8 us
    pallas_call x1, Pallas kernels, gather(): pl.pallas_call(gather_kernel, in_specs=[vmem] * 4, out_specs=[hbm] * 4, o...  66 us
    pallas_call x1, Pallas kernels, piece(): pl.pallas_call(piece_kernel, grid=(grid,), in_specs=[pl.BlockSpec((steps...  61.7 us
    pallas_call x1, Pallas kernels, forward(): pl.pallas_call(forward_kernel, grid=(grid,), in_specs=[pl.BlockSpec((step...  51.5 us
    pallas_call x4, Pallas kernels, product(): pl.pallas_call(functools.partial(product_kernel, across), grid=(columns /...  47.1 us
    pallas_call x1, Pallas kernels, tail(): pl.pallas_call(tail_kernel, in_specs=[pl.BlockSpec(memory_space=pltpu.SME...  35.8 us
    dot_general x3, matrix products, contract_rows(): lax.dot_general(left_side, right_side, (((0,), (0,)), ((), ())), preferre...  26.1 us
    pallas_call x1, Pallas kernels, chain(): pl.pallas_call(chain_kernel, in_specs=[pl.BlockSpec(memory_space=pltpu.SM...  24.8 us
  transfers between devices with their start and end apart: 15, of which 0 were waited for; matrix products, arithmetic and copies ran while one was open for 4% of the time, Pallas kernels for 32%

profile of v2, /device:TPU:0, one launch (start us, length us, event | category | flops | bytes accessed | tf_op | source)
XLA Modules:
  0.0 541.4 jit_solution(2681869055600036199)
XLA Ops:
  10.7 66.0 %gather.7 = (bf16[1024,256]{1,0:T(8,128)(2,1)}, bf16[2048,128]{1,0:T(8,128)(2,1)}, bf16[2048,1024]{1,0:T(8,128)(2,1)}, bf16[1024,4096]{1,0:T(8,128)(2,1)}) custom-call(bf16[128,256]{1,0:T(8,128)(2,1)} %pad.21.rows_ref, bf16[256,128]{1,0:T(8,128)(2,1)} %fusion.14.select_ref, bf16[256,1024]{1,0:T(8,128)(2,1)} %out_ref.1, bf16[128,4096]{1,0:T(8,128)(2,1)} %in_ref.1), custom_call_target="tpu_custom_call" | custom-call | flops 54999998464 | tf_op jit(solution)/shard_map/gather/pallas_call | solution.py:1064
  83.6 8.2 %prepare.1 = (bf16[1056,1024]{1,0:T(8,128)(2,1)}, bf16[1024,1024]{1,0:T(8,128)(2,1)}) custom-call(bf16[4,128,1024]{2,1,0:T(8,128)(2,1)} %prompt_ref.3, bf16[4,128,1024]{2,1,0:T(8,128)(2,1)} %piece_ref.3, bf16[4,128,1024]{2,1,0:T(8,128)(2,1)} %prompt_cot_ref.3, bf16[4,128,1024]{2,1,0:T(8,128)(2,1)} %piece_cot_ref.3, f32[32,1024]{1,0:T(8,128)} %bitcast_convert_fusion.halo_ref, ...), custom_call_target="tpu_custom_call" | custom-call | flops 5000000000 | tf_op jit(solution)/shard_map/prepare/pallas_call | solution.py:115
  91.7 10.2 %product.4 = bf16[1056,2048]{1,0:T(8,128)(2,1)} custom-call(bf16[1056,1024]{1,0:T(8,128)(2,1)} %get-tuple-element.90.refs_0_, bf16[1024,4096]{1,0:T(8,128)(2,1)} %get-tuple-element.91.refs_1_.refs_2_), custom_call_target="tpu_custom_call" | custom-call | flops 10000000 | tf_op jit(solution)/shard_map/product/pallas_call | solution.py:70
  101.9 11.0 %product.5 = f32[1056,2048]{1,0:T(8,128)} custom-call(bf16[1056,1024]{1,0:T(8,128)(2,1)} %get-tuple-element.90.refs_0_, bf16[1024,4096]{1,0:T(8,128)(2,1)} %get-tuple-element.91.refs_1_.refs_2_), custom_call_target="tpu_custom_call" | custom-call | flops 10000000 | tf_op jit(solution)/shard_map/product/pallas_call | solution.py:70
  117.1 10.9 %product.6 = f32[1024,2048]{1,0:T(8,128)} custom-call(bf16[1024,1024]{1,0:T(8,128)(2,1)} %get-tuple-element.95.refs_0_, bf16[2048,1024]{1,0:T(8,128)(2,1)} %get-tuple-element.96.refs_1_), custom_call_target="tpu_custom_call" | custom-call | flops 10000000 | tf_op jit(solution)/shard_map/product/pallas_call | solution.py:70
  128.0 15.6 %front.1 = (f32[128,8,2048]{2,1,0:T(8,128)}, f32[1024,128]{1,0:T(8,128)}) custom-call(bf16[132,8,2048]{2,1,0:T(8,128)(2,1)} %bitcast.106, f32[4,2048]{1,0:T(4,128)} %bitcast.122, f32[1,2048]{1,0:T(1,128)} %bitcast.124, bf16[2048,128]{1,0:T(8,128)(2,1)} %get-tuple-element.92.sel_ref), custom_call_target="tpu_custom_call" | custom-call | flops 16000000000 | tf_op jit(solution)/shard_map/front/pallas_call | solution.py:235
  143.6 61.7 %piece.1 = (f32[128,8,2048]{2,1,0:T(8,128)}, bf16[128,8,2048]{2,1,0:T(8,128)(2,1)}, f32[128,8,2048]{2,1,0:T(8,128)}, bf16[128,8,2048]{2,1,0:T(8,128)(2,1)}, bf16...) custom-call(f32[1024,128]{1,0:T(8,128)} %get-tuple-element.94.proj_ref, ...), custom_call_target="tpu_custom_call" | custom-call | flops 60000002048 | tf_op jit(solution)/shard_map/piece/pallas_call | solution.py:434
  205.3 2.3 fusion.25
  208.2 24.8 %chain.1 = (f32[8,16,2048]{2,1,0:T(8,128)}, f32[8,16,2048]{2,1,0:T(8,128)}) custom-call(f32[4,4]{1,0:T(4,128)} %fusion.20.one_hot_ref, f32[4,16,2048]{2,1,0:T(8,128)} %get-tuple-element.100.ahead_ref, f32[4,16,2048]{2,1,0:T(8,128)} %get-tuple-element.220.behind_ref, f32[4,16,2048]{2,1,0:T(8,128)} %get-tuple-element.219.branch_ref, ...), custom_call_target="tpu_custom_call" | custom-call | flops 24999999488 | tf_op jit(solution)/shard_map/chain/pallas_call | solution.py:581
  232.9 51.5 %forward_scan.1 = (bf16[128,8,2048]{2,1,0:T(8,128)(2,1)}, bf16[8,2,129,8,16,128]{5,4,3,2,1,0:T(8,128)(2,1)}, bf16[132,8,2048]{2,1,0:T(8,128)(2,1)}, f32[1,2048]{1,0:T(1,128)}) custom-call(f32[1024,128]{1,0:T(8,128)} %get-tuple-element.94.proj_ref, f32[128,8,2048]{2,1,0:T(8,128)} %get-tuple-element.97.dt_ref, f32[128,8,2048]{2,1,0:T(8,128)} %get-tuple-element.93.act_ref, ...), custom_call_target="tpu_custom_call" | custom-call | flops 49999998976 | tf_op jit(solution)/shard_map/forward_scan/pallas_call | solution.py:659
  284.4 9.4 %fusion.7 = bf16[2048,1024]{1,0:T(8,128)(2,1)} fusion(bf16[1024,1024]{1,0:T(8,128)(2,1)} %get-tuple-element.95.refs_0_, bf16[128,8,2048]{2,1,0:T(8,128)(2,1)} %get-tuple-element.107), kind=kOutput, calls=%fused_computation.12 | convolution fusion | flops 4297064448 | bytes 10485760 | tf_op jit(solution)/shard_map/dot_general | solution.py:1300
  293.9 3.2 dynamic-slice_bitcast_fusion.2
  298.1 8.1 %convolution_convert_fusion.1 = bf16[1024,2048]{1,0:T(8,128)(2,1)S(1)} fusion(bf16[1056,1024]{1,0:T(8,128)(2,1)S(1)} %copy-done.1, bf16[132,8,2048]{2,1,0:T(8,128)(2,1)} %get-tuple-element.108), kind=kOutput, calls=%fused_computation.14 | convolution fusion | flops 4431282176 | bytes 10682368 | tf_op jit(solution)/shard_map/dot_general | solution.py:1300
  306.3 2.0 copy-done.5
  312.7 3.4 fusion.2
  317.7 1.7 dynamic-slice_bitcast_fusion.3
  319.4 1.8 collective-permute-start.4
  322.9 90.8 %backward_scan.1 = (f32[128,8,2048]{2,1,0:T(8,128)}, f32[64,2048]{1,0:T(8,128)}, f32[1,2048]{1,0:T(1,128)}, f32[16,2048]{1,0:T(8,128)}, bf16[1024,128]{1,0:T(8,128)(2,1)}) custom-call(f32[1024,128]{1,0:T(8,128)} %get-tuple-element.94.proj_ref, f32[128,8,2048]{2,1,0:T(8,128)} %get-tuple-element.97.dt_ref, bf16[128,8,2048]{2,1,0:T(8,128)(2,1)} %get-tuple-element.98.sig_ref, ...), custom_call_target="tpu_custom_call" | custom-call | flops 89999998976 | tf_op jit(solution)/shard_map/backward_scan/pallas_call | solution.py:815
  413.8 2.5 convert_add_fusion.3
  417.9 3.7 collective-permute-start.7
  422.4 21.6 %filter_back.1 = (bf16[132,8,2048]{2,1,0:T(8,128)(2,1)}, f32[128,2048]{1,0:T(8,128)}, f32[4,2048]{1,0:T(4,128)}, f32[1,2048]{1,0:T(1,128)}) custom-call(bf16[132,8,2048]{2,1,0:T(8,128)(2,1)} %bitcast.107, f32[128,8,2048]{2,1,0:T(8,128)} %get-tuple-element.93.act_ref, f32[128,8,2048]{2,1,0:T(8,128)} %get-tuple-element.111.act_grad_ref, ...), custom_call_target="tpu_custom_call" | custom-call | flops 20000000000 | tf_op jit(solution)/shard_map/filter_back/pallas_call | solution.py:923
  445.1 8.6 %convolution_convert_fusion = bf16[1024,2048]{1,0:T(8,128)(2,1)S(1)} fusion(bf16[1056,1024]{1,0:T(8,128)(2,1)} %get-tuple-element.90.refs_0_, bf16[132,8,2048]{2,1,0:T(8,128)(2,1)} %get-tuple-element.122), kind=kOutput, calls=%fused_computation.13 | convolution fusion | flops 4431282176 | bytes 10682368 | tf_op jit(solution)/shard_map/dot_general | solution.py:1300
  454.1 1.8 copy-done.4
  455.9 6.0 %fusion.3.mixed_ref = f32[1024,1024]{1,0:T(8,128)} fusion(bf16[2048,1024]{1,0:T(8,128)(2,1)S(1)} %copy-done.4, bf16[128,8,2048]{2,1,0:T(8,128)(2,1)S(1)} %copy-done.12), kind=kOutput, calls=%fused_computation.8 | convolution fusion | flops 4294967296 | bytes 12582912 | tf_op jit(solution)/shard_map/dot_general | solution.py:1471
  463.7 1.8 collective-permute-start.11
  467.2 3.6 collective-permute-start.14
  470.8 15.1 %product.7.grad_ref.grad_halo_ref = f32[1056,1024]{1,0:T(8,128)} custom-call(bf16[1056,2048]{1,0:T(8,128)(2,1)} %bitcast.109, bf16[1056,2048]{1,0:T(8,128)(2,1)} %bitcast.108, bf16[1024,4096]{1,0:T(8,128)(2,1)} %get-tuple-element.91.refs_1_.refs_2_), custom_call_target="tpu_custom_call" | custom-call | flops 10000000 | tf_op jit(solution)/shard_map/product/pallas_call | solution.py:70
  485.9 11.3 %finish.1 = (bf16[4,128,1024]{2,1,0:T(8,128)(2,1)}, bf16[4,128,1024]{2,1,0:T(8,128)(2,1)}, f32[4,128,1024]{2,1,0:T(8,128)}, f32[4,128,1024]{2,1,0:T(8,128)}, f32[32,1024]{1,0:T(8,128)}, /*index=5*/f32[1,1024]{1,0:T(1,128)}) custom-call(f32[1024,1024]{1,0:T(8,128)} %fusion.3.mixed_ref, f32[1056,1024]{1,0:T(8,128)} %product.7.grad_ref.grad_halo_ref, ...), custom_call_target="tpu_custom_call" | custom-call | flops 10000000 | tf_op jit(solution)/shard_map/finish/pallas_call | solution.py:181
  498.0 35.8 %tail.1 = (bf16[128,2048]{1,0:T(8,128)(2,1)}, bf16[192,256]{1,0:T(8,128)(2,1)}, f32[16,1024]{1,0:T(8,128)}) custom-call(f32[4,4]{1,0:T(4,128)} %fusion.20.one_hot_ref, bf16[128,2048]{1,0:T(8,128)(2,1)} %get-tuple-element.134.b0, bf16[128,2048]{1,0:T(8,128)(2,1)} %collective-permute-done.9.b1, bf16[128,2048]{1,0:T(8,128)(2,1)} %collective-permute-done.10.b2, ...), custom_call_target="tpu_custom_call" | custom-call | flops 30000001024 | tf_op jit(solution)/shard_map/tail/pallas_call | solution.py:1214
  534.6 3.5 deliver.1
  538.1 1.6 copy.66
  539.7 1.6 copy.65
  (107 shorter events, 39.0 us)
Async XLA Ops:
  101.9 14.3 %copy-start.8 = (bf16[2048,128]{1,0:T(8,128)(2,1)S(1)}, bf16[2048,128]{1,0:T(8,128)(2,1)}, u32[]{:S(2)}) copy-start(bf16[2048,128]{1,0:T(8,128)(2,1)} %get-tuple-element.92.sel_ref) | copy-start | bytes 1572868
  114.4 0.8 copy-start.2
  293.9 4.3 copy-start.1
  297.1 15.6 %collective-permute-start = (bf16[4,256,1024]{2,1,0:T(8,128)(2,1)}, bf16[4,256,1024]{2,1,0:T(8,128)(2,1)}, u32[]{:S(2)}, u32[]{:S(2)}) collective-permute-start(bf16[4,256,1024]{2,1,0:T(8,128)(2,1)} %dynamic-slice_bitcast_fusion.2), channel_id=1, source_target_pairs={{0,1},{1,0},{2,3},{3,2},{4,5},{5,4},{6,7},{7,6},{8,9},{9,8},{10,11... | collective-permute-start | bytes 6291464 | tf_op jit(solution)/shard_map/ppermute | solution.py:1312
  306.3 2.0 copy-start.5
  306.3 3.4 copy-start.7
  306.3 4.3 copy-start.3
  309.7 6.5 %collective-permute-start.1 = (bf16[4,128,2048]{2,1,0:T(8,128)(2,1)}, bf16[4,128,2048]{2,1,0:T(8,128)(2,1)S(1)}, u32[]{:S(2)}, u32[]{:S(2)}) collective-permute-start(bf16[4,128,2048]{2,1,0:T(8,128)(2,1)} %dynamic-slice_bitcast_fusion.1), channel_id=1, source_target_pairs={{0,1},{1,0},{2,3},{3,2},{4,5},{5,4},{6,7},{7,6},{8,9},{9,8},{10,11... | collective-permute-start | bytes 6291464 | tf_op jit(solution)/shard_map/ppermute | solution.py:1312
  312.7 3.6 copy-start.6
  319.4 94.3 %collective-permute-start.4 = (bf16[256,2048]{1,0:T(8,128)(2,1)}, bf16[256,2048]{1,0:T(8,128)(2,1)}, u32[]{:S(2)}, u32[]{:S(2)}) collective-permute-start(bf16[256,2048]{1,0:T(8,128)(2,1)} %get-tuple-element.206), channel_id=1, source_target_pairs={{0,6},{1,7},{2,4},{3,5},{4,2},{5,3},{6,0},{7,1},{8,14},{9,15},{10,... | collective-permute-start | bytes 3145736 | tf_op jit(solution)/shard_map/ppermute | solution.py:1312
  321.2 92.5 %collective-permute-start.3 = (bf16[256,2048]{1,0:T(8,128)(2,1)}, bf16[256,2048]{1,0:T(8,128)(2,1)}, u32[]{:S(2)}, u32[]{:S(2)}) collective-permute-start(bf16[256,2048]{1,0:T(8,128)(2,1)} %get-tuple-element.207), channel_id=1, source_target_pairs={{0,4},{1,5},{2,6},{3,7},{4,0},{5,1},{6,2},{7,3},{8,12},{9,13},{10,... | collective-permute-start | bytes 3145736 | tf_op jit(solution)/shard_map/ppermute | solution.py:1312
  322.2 91.6 %collective-permute-start.2 = (bf16[256,2048]{1,0:T(8,128)(2,1)}, bf16[256,2048]{1,0:T(8,128)(2,1)}, u32[]{:S(2)}, u32[]{:S(2)}) collective-permute-start(bf16[256,2048]{1,0:T(8,128)(2,1)} %get-tuple-element.208), channel_id=1, source_target_pairs={{0,2},{1,3},{2,0},{3,1},{4,6},{5,7},{6,4},{7,5},{8,10},{9,11},{10,... | collective-permute-start | bytes 3145736 | tf_op jit(solution)/shard_map/ppermute | solution.py:1312
  413.7 2.6 copy-start.9
  416.3 1.4 copy-start
  417.9 27.1 %collective-permute-start.7 = (bf16[64,2048]{1,0:T(8,128)(2,1)S(1)}, bf16[64,2048]{1,0:T(8,128)(2,1)S(1)}, u32[]{:S(2)}, u32[]{:S(2)}) collective-permute-start(bf16[64,2048]{1,0:T(8,128)(2,1)S(1)} %get-tuple-element.216), channel_id=1, source_target_pairs={{0,24},{8,16},{16,8},{24,0},{1,25},{9,17},{17,9},{25,1},{2,26},{10... | collective-permute-start | bytes 786440 | tf_op jit(solution)/shard_map/ppermute | solution.py:1312
  421.6 23.4 %collective-permute-start.6 = (bf16[64,2048]{1,0:T(8,128)(2,1)S(1)}, bf16[64,2048]{1,0:T(8,128)(2,1)S(1)}, u32[]{:S(2)}, u32[]{:S(2)}) collective-permute-start(bf16[64,2048]{1,0:T(8,128)(2,1)S(1)} %get-tuple-element.217), channel_id=1, source_target_pairs={{0,16},{8,24},{16,0},{24,8},{1,17},{9,25},{17,1},{25,9},{2,18},{10... | collective-permute-start | bytes 786440 | tf_op jit(solution)/shard_map/ppermute | solution.py:1312
  421.6 23.4 %collective-permute-start.5 = (bf16[64,2048]{1,0:T(8,128)(2,1)S(1)}, bf16[64,2048]{1,0:T(8,128)(2,1)S(1)}, u32[]{:S(2)}, u32[]{:S(2)}) collective-permute-start(bf16[64,2048]{1,0:T(8,128)(2,1)S(1)} %get-tuple-element.218), channel_id=1, source_target_pairs={{0,8},{8,0},{16,24},{24,16},{1,9},{9,1},{17,25},{25,17},{2,10},{10... | collective-permute-start | bytes 786440 | tf_op jit(solution)/shard_map/ppermute | solution.py:1312
  445.1 9.1 %copy-start.12 = (bf16[128,8,2048]{2,1,0:T(8,128)(2,1)S(1)}, bf16[128,8,2048]{2,1,0:T(8,128)(2,1)}, u32[]{:S(2)}) copy-start(bf16[128,8,2048]{2,1,0:T(8,128)(2,1)} %get-tuple-element.107) | copy-start | bytes 12582916
  453.6 2.3 copy-start.4
  453.8 43.4 %copy-start.10 = (bf16[64,2048]{1,0:T(8,128)(2,1)}, bf16[64,2048]{1,0:T(8,128)(2,1)S(1)}, u32[]{:S(2)}) copy-start(bf16[64,2048]{1,0:T(8,128)(2,1)S(1)} %add_convert_fusion.rest_0_) | copy-start | bytes 786436
  454.1 7.9 %collective-permute-start.8 = (bf16[4,128,2048]{2,1,0:T(8,128)(2,1)S(1)}, bf16[4,128,2048]{2,1,0:T(8,128)(2,1)S(1)}, u32[]{:S(2)}, u32[]{:S(2)}) collective-permute-start(bf16[4,128,2048]{2,1,0:T(8,128)(2,1)S(1)} %dynamic-slice_bitcast_fusion), channel_id=1, source_target_pairs={{0,1},{1,0},{2,3},{3,2},{4,5},{5,4},{6,7},{7,6},{8,9},{9,8},{10,11... | collective-permute-start | bytes 6291464 | tf_op jit(solution)/shard_map/ppermute | solution.py:1312
  463.7 33.5 %collective-permute-start.11 = (bf16[128,2048]{1,0:T(8,128)(2,1)S(1)}, bf16[128,2048]{1,0:T(8,128)(2,1)}, u32[]{:S(2)}, u32[]{:S(2)}) collective-permute-start(bf16[128,2048]{1,0:T(8,128)(2,1)S(1)} %get-tuple-element.210), channel_id=1, source_target_pairs={{0,6},{1,7},{2,4},{3,5},{4,2},{5,3},{6,0},{7,1},{8,14},{9,15},{10,... | collective-permute-start | bytes 1572872 | tf_op jit(solution)/shard_map/ppermute | solution.py:1312
  465.6 32.5 %collective-permute-start.10 = (bf16[128,2048]{1,0:T(8,128)(2,1)S(1)}, bf16[128,2048]{1,0:T(8,128)(2,1)}, u32[]{:S(2)}, u32[]{:S(2)}) collective-permute-start(bf16[128,2048]{1,0:T(8,128)(2,1)S(1)} %get-tuple-element.211), channel_id=1, source_target_pairs={{0,4},{1,5},{2,6},{3,7},{4,0},{5,1},{6,2},{7,3},{8,12},{9,13},{10,... | collective-permute-start | bytes 1572872 | tf_op jit(solution)/shard_map/ppermute | solution.py:1312
  466.5 31.6 %collective-permute-start.9 = (bf16[128,2048]{1,0:T(8,128)(2,1)S(1)}, bf16[128,2048]{1,0:T(8,128)(2,1)}, u32[]{:S(2)}, u32[]{:S(2)}) collective-permute-start(bf16[128,2048]{1,0:T(8,128)(2,1)S(1)} %get-tuple-element.212), channel_id=1, source_target_pairs={{0,2},{1,3},{2,0},{3,1},{4,6},{5,7},{6,4},{7,5},{8,10},{9,11},{10,... | collective-permute-start | bytes 1572872 | tf_op jit(solution)/shard_map/ppermute | solution.py:1312
  467.2 66.7 %collective-permute-start.14 = (bf16[64,2048]{1,0:T(8,128)(2,1)S(1)}, bf16[64,2048]{1,0:T(8,128)(2,1)}, u32[]{:S(2)}, u32[]{:S(2)}) collective-permute-start(bf16[64,2048]{1,0:T(8,128)(2,1)S(1)} %add_convert_fusion.rest_0_), channel_id=1, source_target_pairs={{0,24},{8,16},{16,8},{24,0},{1,25},{9,17},{17,9},{25,1},{2,26},{10... | collective-permute-start | bytes 786440 | tf_op jit(solution)/shard_map/ppermute | solution.py:1312
  470.8 63.1 %collective-permute-start.13 = (bf16[64,2048]{1,0:T(8,128)(2,1)S(1)}, bf16[64,2048]{1,0:T(8,128)(2,1)}, u32[]{:S(2)}, u32[]{:S(2)}) collective-permute-start(bf16[64,2048]{1,0:T(8,128)(2,1)S(1)} %add_convert_fusion.rest_0_), channel_id=1, source_target_pairs={{0,16},{8,24},{16,0},{24,8},{1,17},{9,25},{17,1},{25,9},{2,18},{10... | collective-permute-start | bytes 786440 | tf_op jit(solution)/shard_map/ppermute | solution.py:1312
  497.2 36.7 %collective-permute-start.12 = (bf16[64,2048]{1,0:T(8,128)(2,1)S(1)}, bf16[64,2048]{1,0:T(8,128)(2,1)S(1)}, u32[]{:S(2)}, u32[]{:S(2)}) collective-permute-start(bf16[64,2048]{1,0:T(8,128)(2,1)S(1)} %add_convert_fusion.rest_0_), channel_id=1, source_target_pairs={{0,8},{8,0},{16,24},{24,16},{1,9},{9,1},{17,25},{25,17},{2,10},{10... | collective-permute-start | bytes 786440 | tf_op jit(solution)/shard_map/ppermute | solution.py:1312
  533.9 0.7 copy-start.11

commit v3 on v2

--- a/solution.py
+++ b/solution.py
@@ -60,18 +60,19 @@
 def product(lefts, rhs, kind, across=False, part=0, parts=1):
     rows = lefts[0].shape[0]
     depth = sum(left.shape[1] for left in lefts)
+    tile = 2 * WIDE if len(lefts) == 1 else WIDE
     if across:
         columns = rhs.shape[0]
-        rhs_spec = pl.BlockSpec((WIDE, depth), lambda j: (j, 0))
+        rhs_spec = pl.BlockSpec((tile, depth), lambda j: (j, 0))
     else:
         columns = rhs.shape[1] // parts
-        first = part * columns // WIDE
-        rhs_spec = pl.BlockSpec((depth, WIDE), lambda j: (0, first + j))
+        first = part * columns // tile
+        rhs_spec = pl.BlockSpec((depth, tile), lambda j: (0, first + j))
     return pl.pallas_call(
         functools.partial(product_kernel, across),
-        grid=(columns // WIDE,),
+        grid=(columns // tile,),
         in_specs=[pl.BlockSpec(left.shape, lambda j: (0, 0)) for left in lefts] + [rhs_spec],
-        out_specs=pl.BlockSpec((rows, WIDE), lambda j: (0, j)),
+        out_specs=pl.BlockSpec((rows, tile), lambda j: (0, j)),
         out_shape=jax.ShapeDtypeStruct((rows, columns), kind),
         compiler_params=params(),
         cost_estimate=cost(0.01),
@@ -975,31 +976,40 @@
 
 
 FIRST, SECOND = (0, 1, 2, 3), (4, 5)
+TRADED = (2, 3, 4, 5)
 
 
 def gather_kernel(
     rows_ref, select_ref, out_ref, in_ref, all_rows, all_select, all_out, all_in,
-    local_sems, own_send, own_recv, pass_send, pass_recv, core_send, core_recv,
+    local_sems, own_send, own_recv, pass_send, pass_recv, core_send, core_recv, trade_send, trade_recv,
 ):
     me = lax.axis_index("fsdp")
+    mz = lax.axis_index("replica")
     a, b = flipped(me, 2), flipped(me, 4)
     corner = flipped(a, 4)
     twin = flipped(me, 1)
-    greet([("fsdp", a), ("fsdp", b), ("fsdp", twin)])
+    mate = flipped(mz, 1)
+    greet([("fsdp", a), ("fsdp", b), ("fsdp", twin), ("replica", mate)])
     kinds = ((rows_ref, all_rows), (select_ref, all_select), (out_ref, all_out), (in_ref, all_in))
-    table = [(0, 0, 1), (1, 0, 1), (2, 0, 2), (3, 0, 2), (2, 1, 2), (3, 1, 2)]
-
-    def place(owner, piece):
-        kind, part, parts = table[piece]
-        count = kinds[kind][0].shape[0]
-        step = count // parts
-        return kinds[kind][1].at[pl.ds(pl.multiple_of(owner * count + part * step, step), step)]
-
-    def mine(piece):
-        kind, part, parts = table[piece]
-        step = kinds[kind][0].shape[0] // parts
-        return kinds[kind][0].at[pl.ds(part * step, step)]
-
+
+    def span(piece, side):
+        if piece < 2:
+            return piece, 0, kinds[piece][0].shape[0]
+        kind = 2 + piece % 2
+        quarter = kinds[kind][0].shape[0] // 4
+        return kind, side * (2 * quarter) + (quarter if piece in SECOND else 0), quarter
+
+    def place(owner, piece, side):
+        kind, start, count = span(piece, side)
+        first = owner * kinds[kind][0].shape[0] + start
+        return kinds[kind][1].at[pl.ds(pl.multiple_of(first, 16), count)]
+
+    def mine(piece, side):
+        kind, start, count = span(piece, side)
+        return kinds[kind][0].at[pl.ds(pl.multiple_of(start, 16), count) if piece in TRADED else pl.ds(0, count)]
+
+    side = mz % 2
+    other = 1 - side
     started = []
 
     def start(copy):
@@ -1007,28 +1017,48 @@
         started.append(copy)
 
     def own_copy(piece, k, peer, owner):
-        return send(mine(piece), place(owner, piece), own_send.at[k, piece], own_recv.at[k, piece], peer)
-
-    def pass_copy(piece, peer, owner):
-        return send(place(owner, piece), place(owner, piece), pass_send.at[piece], pass_recv.at[piece], peer)
-
-    def core_copy(piece, k, owner):
-        src = mine(piece) if k == 0 else place(owner, piece)
-        return send(src, place(owner, piece), core_send.at[k, piece], core_recv.at[k, piece], twin)
+        return send(mine(piece, side), place(owner, piece, side), own_send.at[k, piece], own_recv.at[k, piece], peer)
+
+    def pass_copy(piece, peer, owner, far=False):
+        ref = place(owner, piece, other if far else side)
+        at = piece + len(FIRST + SECOND) * far
+        return send(ref, ref, pass_send.at[at], pass_recv.at[at], peer)
+
+    def trade_copy(piece, k, owner, whose):
+        ref = place(owner, piece, whose)
+        return send(ref, ref, trade_send.at[k, piece], trade_recv.at[k, piece], mate, "replica")
+
+    def core_copy(piece, k, owner, whose=None):
+        if whose is None:
+            return send(
+                place(owner, piece, side), place(owner, piece, side), core_send.at[k, piece], core_recv.at[k, piece], twin
+            )
+        at = len(FIRST + SECOND) + piece
+        ref = place(owner, piece, whose)
+        return send(ref, ref, core_send.at[k, at], core_recv.at[k, at], twin)
+
+    def whole_copy(kind, owner):
+        src, dst = kinds[kind]
+        count = src.shape[0]
+        rows = dst.at[pl.ds(pl.multiple_of(owner * count, count), count)]
+        return send(src, rows, core_send.at[3, kind], core_recv.at[3, kind], twin)
 
     for piece in FIRST + SECOND:
         start(own_copy(piece, 0, a, me))
-    for piece in SECOND + FIRST:
+    for piece in SECOND + (2, 3, 0, 1):
         start(own_copy(piece, 1, b, me))
     local = []
-    for piece in FIRST + SECOND:
-        start(core_copy(piece, 0, me))
-        copy = pltpu.make_async_copy(mine(piece), place(me, piece), local_sems.at[piece])
+    for kind, (src, dst) in enumerate(kinds):
+        start(whole_copy(kind, me))
+        count = src.shape[0]
+        rows = dst.at[pl.ds(pl.multiple_of(me * count, count), count)]
+        copy = pltpu.make_async_copy(src, rows, local_sems.at[kind])
         copy.start()
         local.append(copy)
+    owners = (a, b, corner)
 
     def arrived(piece, k):
-        owner = (a, b, corner)[k]
+        owner = owners[k]
         if k == 2:
             pass_copy(piece, a, owner).wait_recv()
         else:
@@ -1037,16 +1067,41 @@
                 start(pass_copy(piece, b, owner))
             if k == 1 and piece in SECOND:
                 start(pass_copy(piece, a, owner))
-        start(core_copy(piece, k + 1, owner))
-
-    for piece, k in (
-        (0, 0), (1, 0), (2, 0), (4, 1), (3, 0), (5, 1), (4, 0), (0, 1), (1, 1), (2, 1), (0, 2), (1, 2), (2, 2),
-        (4, 2), (5, 0), (3, 1), (3, 2), (5, 2),
-    ):
+        if piece in TRADED and k < 2:
+            start(trade_copy(piece, k, owner, side))
+        start(core_copy(piece, k, owner))
+
+    def traded(piece, k):
+        owner = owners[k]
+        trade_copy(piece, k, owner, other).wait_recv()
+        if k == 0 and piece in FIRST:
+            start(pass_copy(piece, b, owner, True))
+        if k == 1 and piece in SECOND:
+            start(pass_copy(piece, a, owner, True))
+        start(core_copy(piece, k, owner, other))
+
+    for piece, k in ((0, 0), (4, 1), (1, 0), (2, 0), (5, 1), (3, 0)):
         arrived(piece, k)
-    for k, owner in enumerate((twin, flipped(twin, 2), flipped(twin, 4), flipped(corner, 1))):
+    traded(2, 0)
+    traded(4, 1)
+    arrived(4, 0)
+    arrived(2, 1)
+    traded(3, 0)
+    traded(5, 1)
+    for piece, k in ((5, 0), (3, 1), (0, 1), (1, 1), (0, 2), (1, 2), (2, 2), (4, 2), (3, 2), (5, 2)):
+        arrived(piece, k)
+    for piece, k in ((4, 0), (2, 1), (5, 0), (3, 1)):
+        traded(piece, k)
+    for piece in (2, 4, 3, 5):
+        pass_copy(piece, a, corner, True).wait_recv()
+        start(core_copy(piece, 2, corner, other))
+    for kind in range(len(kinds)):
+        whole_copy(kind, twin).wait_recv()
+    for k, owner in enumerate((flipped(twin, 2), flipped(twin, 4), flipped(corner, 1))):
         for piece in FIRST + SECOND:
             core_copy(piece, k, owner).wait_recv()
+        for piece in TRADED:
+            core_copy(piece, k, owner, other).wait_recv()
     for copy in started:
         copy.wait_send()
     for copy in local:
@@ -1055,7 +1110,7 @@
 
 def gather(*shards):
     size = lax.axis_size("fsdp")
-    if size != 8:
+    if size != 8 or lax.axis_size("replica") % 2:
         return [lax.all_gather(shard, "fsdp", axis=0, tiled=True) for shard in shards]
     vmem = pl.BlockSpec(memory_space=pltpu.VMEM)
     hbm = pl.BlockSpec(memory_space=pl.ANY)
@@ -1067,8 +1122,8 @@
         out_specs=[hbm] * 4,
         out_shape=[jax.ShapeDtypeStruct((size * shard.shape[0], shard.shape[1]), bf16) for shard in shards],
         scratch_shapes=[
-            dma((pieces,)), dma((2, pieces)), dma((2, pieces)), dma((pieces,)), dma((pieces,)),
-            dma((4, pieces)), dma((4, pieces)),
+            dma((len(shards),)), dma((2, pieces)), dma((2, pieces)), dma((2 * pieces,)), dma((2 * pieces,)),
+            dma((4, 2 * pieces)), dma((4, 2 * pieces)), dma((3, pieces)), dma((3, pieces)),
         ],
         compiler_params=params(collective_id=2, has_side_effects=True),
         cost_estimate=cost(55),
@@ -1246,13 +1301,9 @@
     in_out[:, 0:half] = block_ref[...].astype(f32)
     small = small_ref[...].astype(f32)
     at = 0
-    for k, (out, count) in enumerate(zip(outs[3:], SMALL)):
+    for out, count in zip(outs[3:], SMALL):
         rows = small[at : at + count]
-        if k in (4, 6):
-            rows = jnp.concatenate([rows, jnp.zeros((-count % LANES, rows.shape[1]), f32)], axis=0)
-            out[...] = rows.T[:, :count]
-        else:
-            out[...] = rows[:, 0 : out.shape[1]]
+        out[...] = rows[:, 0 : out.shape[1]]
         at += count
     for d, ref in enumerate(early_refs):
         count = ref.shape[0]
@@ -1280,7 +1331,6 @@
     end = prompt_grad.shape[1] // SEQS - 1
     last = pl.BlockSpec((PROMPTS, SEQS, features), lambda i: (0, end, 0))
     shapes = [(count, width) for count in SMALL[:-1]] + [(1, features // size)]
-    shapes[4], shapes[6] = shapes[4][::-1], shapes[6][::-1]
     shapes = [(rows, 2 * channels), (2 * rows, features), prompt_grad.shape] + shapes
     return pl.pallas_call(
         deliver_kernel,
@@ -1497,10 +1547,10 @@
         input_grad,
         g_filter,
         g_fbias[0],
-        g_select,
+        g_select.T,
         g_step,
         g_sbias[0],
-        g_decay,
+        g_decay.T,
         g_skip[0],
         output_grad,
     )

time: 544 us -> 519 us (0.954)
  Pallas kernels: 438 us -> 416 us
    pallas_call x1, Pallas kernels: 66 us -> 50.4 us  [gather(): pl.pallas_call(gather_kernel, in_specs=[vmem] * 4, out_specs=[hbm] * 4, o...]
  transfers between devices with their start and end apart: 15 -> 15, of which waited for: 0 -> 0; matrix products, arithmetic and copies ran while one was open for 4% -> 4% of each run, Pallas kernels for 32% -> 34%
where the time goes in v3:
time: 519 us; the launch traced here: 517 us
  Pallas kernels  416 us (80%)
  local copies, waits for them, and re-layouts  34.3 us (7%)
  matrix products  32.2 us (6%)
  starting transfers between devices  17 us (3%)
  other arithmetic  15.6 us (3%)
    pallas_call x1, Pallas kernels, backward(): pl.pallas_call(backward_kernel, grid=(grid,), in_specs=[pl.BlockSpec((ste...  90.8 us
    pallas_call x1, Pallas kernels, piece(): pl.pallas_call(piece_kernel, grid=(grid,), in_specs=[pl.BlockSpec((steps...  61.7 us
    pallas_call x1, Pallas kernels, forward(): pl.pallas_call(forward_kernel, grid=(grid,), in_specs=[pl.BlockSpec((step...  51.5 us
    pallas_call x1, Pallas kernels, gather(): pl.pallas_call(gather_kernel, in_specs=[vmem] * 4, out_specs=[hbm] * 4, o...  50.4 us
    pallas_call x4, Pallas kernels, product(): pl.pallas_call(functools.partial(product_kernel, across), grid=(columns /...  42.3 us
    pallas_call x1, Pallas kernels, tail(): pl.pallas_call(tail_kernel, in_specs=[pl.BlockSpec(memory_space=pltpu.SME...  35.2 us
    dot_general x3, matrix products, contract_rows(): lax.dot_general(left_side, right_side, (((0,), (0,)), ((), ())), preferre...  26.1 us
    pallas_call x1, Pallas kernels, chain(): pl.pallas_call(chain_kernel, in_specs=[pl.BlockSpec(memory_space=pltpu.SM...  24.4 us
  transfers between devices with their start and end apart: 15, of which 0 were waited for; matrix products, arithmetic and copies ran while one was open for 4% of the time, Pallas kernels for 34%

profile of v3, /device:TPU:0, one launch (start us, length us, event | category | flops | bytes accessed | tf_op | source)
XLA Modules:
  0.0 516.8 jit_solution(14673418796189878988)
XLA Ops:
  10.7 50.4 %gather.7 = (bf16[1024,256]{1,0:T(8,128)(2,1)}, bf16[2048,128]{1,0:T(8,128)(2,1)}, bf16[2048,1024]{1,0:T(8,128)(2,1)}, bf16[1024,4096]{1,0:T(8,128)(2,1)}) custom-call(bf16[128,256]{1,0:T(8,128)(2,1)} %pad.21.rows_ref, bf16[256,128]{1,0:T(8,128)(2,1)} %fusion.14.select_ref, bf16[256,1024]{1,0:T(8,128)(2,1)} %out_ref.1, bf16[128,4096]{1,0:T(8,128)(2,1)} %in_ref.1), custom_call_target="tpu_custom_call" | custom-call | flops 54999998464 | tf_op jit(solution)/shard_map/gather/pallas_call | solution.py:1119
  67.9 8.2 %prepare.1 = (bf16[1056,1024]{1,0:T(8,128)(2,1)}, bf16[1024,1024]{1,0:T(8,128)(2,1)}) custom-call(bf16[4,128,1024]{2,1,0:T(8,128)(2,1)} %prompt_ref.3, bf16[4,128,1024]{2,1,0:T(8,128)(2,1)} %piece_ref.3, bf16[4,128,1024]{2,1,0:T(8,128)(2,1)} %prompt_cot_ref.3, bf16[4,128,1024]{2,1,0:T(8,128)(2,1)} %piece_cot_ref.3, f32[32,1024]{1,0:T(8,128)} %bitcast_convert_fusion.halo_ref, ...), custom_call_target="tpu_custom_call" | custom-call | flops 5000000000 | tf_op jit(solution)/shard_map/prepare/pallas_call | solution.py:116
  76.1 8.6 %product.4 = bf16[1056,2048]{1,0:T(8,128)(2,1)} custom-call(bf16[1056,1024]{1,0:T(8,128)(2,1)} %get-tuple-element.90.refs_0_, bf16[1024,4096]{1,0:T(8,128)(2,1)} %get-tuple-element.91.refs_1_.refs_2_), custom_call_target="tpu_custom_call" | custom-call | flops 10000000 | tf_op jit(solution)/shard_map/product/pallas_call | solution.py:71
  84.6 9.4 %product.5 = f32[1056,2048]{1,0:T(8,128)} custom-call(bf16[1056,1024]{1,0:T(8,128)(2,1)} %get-tuple-element.90.refs_0_, bf16[1024,4096]{1,0:T(8,128)(2,1)} %get-tuple-element.91.refs_1_.refs_2_), custom_call_target="tpu_custom_call" | custom-call | flops 10000000 | tf_op jit(solution)/shard_map/product/pallas_call | solution.py:71
  98.2 9.3 %product.6 = f32[1024,2048]{1,0:T(8,128)} custom-call(bf16[1024,1024]{1,0:T(8,128)(2,1)} %get-tuple-element.95.refs_0_, bf16[2048,1024]{1,0:T(8,128)(2,1)} %get-tuple-element.96.refs_1_), custom_call_target="tpu_custom_call" | custom-call | flops 10000000 | tf_op jit(solution)/shard_map/product/pallas_call | solution.py:71
  107.5 15.6 %front.1 = (f32[128,8,2048]{2,1,0:T(8,128)}, f32[1024,128]{1,0:T(8,128)}) custom-call(bf16[132,8,2048]{2,1,0:T(8,128)(2,1)} %bitcast.108, f32[4,2048]{1,0:T(4,128)} %bitcast.124, f32[1,2048]{1,0:T(1,128)} %bitcast.126, bf16[2048,128]{1,0:T(8,128)(2,1)} %get-tuple-element.92.sel_ref), custom_call_target="tpu_custom_call" | custom-call | flops 16000000000 | tf_op jit(solution)/shard_map/front/pallas_call | solution.py:236
  123.1 61.7 %piece.1 = (f32[128,8,2048]{2,1,0:T(8,128)}, bf16[128,8,2048]{2,1,0:T(8,128)(2,1)}, f32[128,8,2048]{2,1,0:T(8,128)}, bf16[128,8,2048]{2,1,0:T(8,128)(2,1)}, bf16...) custom-call(f32[1024,128]{1,0:T(8,128)} %get-tuple-element.94.proj_ref, ...), custom_call_target="tpu_custom_call" | custom-call | flops 60000002048 | tf_op jit(solution)/shard_map/piece/pallas_call | solution.py:435
  184.8 2.3 fusion.25
  187.7 24.4 %chain.1 = (f32[8,16,2048]{2,1,0:T(8,128)}, f32[8,16,2048]{2,1,0:T(8,128)}) custom-call(f32[4,4]{1,0:T(4,128)} %fusion.20.one_hot_ref, f32[4,16,2048]{2,1,0:T(8,128)} %get-tuple-element.100.ahead_ref, f32[4,16,2048]{2,1,0:T(8,128)} %get-tuple-element.178.behind_ref, f32[4,16,2048]{2,1,0:T(8,128)} %get-tuple-element.177.branch_ref, ...), custom_call_target="tpu_custom_call" | custom-call | flops 24999999488 | tf_op jit(solution)/shard_map/chain/pallas_call | solution.py:582
  212.1 51.5 %forward_scan.1 = (bf16[128,8,2048]{2,1,0:T(8,128)(2,1)}, bf16[8,2,129,8,16,128]{5,4,3,2,1,0:T(8,128)(2,1)}, bf16[132,8,2048]{2,1,0:T(8,128)(2,1)}, f32[1,2048]{1,0:T(1,128)}) custom-call(f32[1024,128]{1,0:T(8,128)} %get-tuple-element.94.proj_ref, f32[128,8,2048]{2,1,0:T(8,128)} %get-tuple-element.97.dt_ref, f32[128,8,2048]{2,1,0:T(8,128)} %get-tuple-element.93.act_ref, ...), custom_call_target="tpu_custom_call" | custom-call | flops 49999998976 | tf_op jit(solution)/shard_map/forward_scan/pallas_call | solution.py:660
  263.6 9.4 %fusion.7 = bf16[2048,1024]{1,0:T(8,128)(2,1)} fusion(bf16[1024,1024]{1,0:T(8,128)(2,1)} %get-tuple-element.95.refs_0_, bf16[128,8,2048]{2,1,0:T(8,128)(2,1)} %get-tuple-element.107), kind=kOutput, calls=%fused_computation.12 | convolution fusion | flops 4297064448 | bytes 10485760 | tf_op jit(solution)/shard_map/dot_general | solution.py:1350
  273.1 3.2 dynamic-slice_bitcast_fusion.2
  277.3 8.1 %convolution_convert_fusion.1 = bf16[1024,2048]{1,0:T(8,128)(2,1)S(1)} fusion(bf16[1056,1024]{1,0:T(8,128)(2,1)S(1)} %copy-done.1, bf16[132,8,2048]{2,1,0:T(8,128)(2,1)} %get-tuple-element.108), kind=kOutput, calls=%fused_computation.14 | convolution fusion | flops 4431282176 | bytes 10682368 | tf_op jit(solution)/shard_map/dot_general | solution.py:1350
  285.5 2.0 copy-done.5
  291.8 3.4 fusion.2
  296.8 1.7 dynamic-slice_bitcast_fusion.3
  298.6 2.2 collective-permute-start.4
  302.1 90.8 %backward_scan.1 = (f32[128,8,2048]{2,1,0:T(8,128)}, f32[64,2048]{1,0:T(8,128)}, f32[1,2048]{1,0:T(1,128)}, f32[16,2048]{1,0:T(8,128)}, bf16[1024,128]{1,0:T(8,128)(2,1)}) custom-call(f32[1024,128]{1,0:T(8,128)} %get-tuple-element.94.proj_ref, f32[128,8,2048]{2,1,0:T(8,128)} %get-tuple-element.97.dt_ref, bf16[128,8,2048]{2,1,0:T(8,128)(2,1)} %get-tuple-element.98.sig_ref, ...), custom_call_target="tpu_custom_call" | custom-call | flops 89999998976 | tf_op jit(solution)/shard_map/backward_scan/pallas_call | solution.py:816
  392.9 2.5 convert_add_fusion.3
  397.1 2.9 collective-permute-start.7
  400.0 1.5 collective-permute-start.5
  401.5 21.6 %filter_back.1 = (bf16[132,8,2048]{2,1,0:T(8,128)(2,1)}, f32[128,2048]{1,0:T(8,128)}, f32[4,2048]{1,0:T(4,128)}, f32[1,2048]{1,0:T(1,128)}) custom-call(bf16[132,8,2048]{2,1,0:T(8,128)(2,1)} %bitcast.109, f32[128,8,2048]{2,1,0:T(8,128)} %get-tuple-element.93.act_ref, f32[128,8,2048]{2,1,0:T(8,128)} %get-tuple-element.111.act_grad_ref, ...), custom_call_target="tpu_custom_call" | custom-call | flops 20000000000 | tf_op jit(solution)/shard_map/filter_back/pallas_call | solution.py:924
  424.2 8.6 %convolution_convert_fusion = bf16[1024,2048]{1,0:T(8,128)(2,1)S(1)} fusion(bf16[1056,1024]{1,0:T(8,128)(2,1)} %get-tuple-element.90.refs_0_, bf16[132,8,2048]{2,1,0:T(8,128)(2,1)} %get-tuple-element.122), kind=kOutput, calls=%fused_computation.13 | convolution fusion | flops 4431282176 | bytes 10682368 | tf_op jit(solution)/shard_map/dot_general | solution.py:1350
  433.3 1.8 copy-done.4
  435.1 6.0 %fusion.3.mixed_ref = f32[1024,1024]{1,0:T(8,128)} fusion(bf16[2048,1024]{1,0:T(8,128)(2,1)S(1)} %copy-done.4, bf16[128,8,2048]{2,1,0:T(8,128)(2,1)S(1)} %copy-done.12), kind=kOutput, calls=%fused_computation.8 | convolution fusion | flops 4294967296 | bytes 12582912 | tf_op jit(solution)/shard_map/dot_general | solution.py:1521
  442.9 2.2 collective-permute-start.11
  446.4 2.9 collective-permute-start.14
  449.2 15.1 %product.7.grad_ref.grad_halo_ref = f32[1056,1024]{1,0:T(8,128)} custom-call(bf16[1056,2048]{1,0:T(8,128)(2,1)} %bitcast.111, bf16[1056,2048]{1,0:T(8,128)(2,1)} %bitcast.110, bf16[1024,4096]{1,0:T(8,128)(2,1)} %get-tuple-element.91.refs_1_.refs_2_), custom_call_target="tpu_custom_call" | custom-call | flops 10000000 | tf_op jit(solution)/shard_map/product/pallas_call | solution.py:71
  464.3 11.3 %finish.1 = (bf16[4,128,1024]{2,1,0:T(8,128)(2,1)}, bf16[4,128,1024]{2,1,0:T(8,128)(2,1)}, f32[4,128,1024]{2,1,0:T(8,128)}, f32[4,128,1024]{2,1,0:T(8,128)}, f32[32,1024]{1,0:T(8,128)}, /*index=5*/f32[1,1024]{1,0:T(1,128)}) custom-call(f32[1024,1024]{1,0:T(8,128)} %fusion.3.mixed_ref, f32[1056,1024]{1,0:T(8,128)} %product.7.grad_ref.grad_halo_ref, ...), custom_call_target="tpu_custom_call" | custom-call | flops 10000000 | tf_op jit(solution)/shard_map/finish/pallas_call | solution.py:182
  475.6 1.6 collective-permute-start.12
  477.2 35.2 %tail.1 = (bf16[128,2048]{1,0:T(8,128)(2,1)}, bf16[192,256]{1,0:T(8,128)(2,1)}, f32[16,1024]{1,0:T(8,128)}) custom-call(f32[4,4]{1,0:T(4,128)} %fusion.20.one_hot_ref, bf16[128,2048]{1,0:T(8,128)(2,1)} %get-tuple-element.134.b0, bf16[128,2048]{1,0:T(8,128)(2,1)} %collective-permute-done.9.b1, bf16[128,2048]{1,0:T(8,128)(2,1)} %collective-permute-done.10.b2, ...), custom_call_target="tpu_custom_call" | custom-call | flops 30000001024 | tf_op jit(solution)/shard_map/tail/pallas_call | solution.py:1269
  513.1 3.5 deliver.1
  (105 shorter events, 36.7 us)
Async XLA Ops:
  84.6 12.7 %copy-start.8 = (bf16[2048,128]{1,0:T(8,128)(2,1)S(1)}, bf16[2048,128]{1,0:T(8,128)(2,1)}, u32[]{:S(2)}) copy-start(bf16[2048,128]{1,0:T(8,128)(2,1)} %get-tuple-element.92.sel_ref) | copy-start | bytes 1572868
  95.5 0.8 copy-start.2
  273.1 4.2 copy-start.1
  276.3 15.5 %collective-permute-start = (bf16[4,256,1024]{2,1,0:T(8,128)(2,1)}, bf16[4,256,1024]{2,1,0:T(8,128)(2,1)}, u32[]{:S(2)}, u32[]{:S(2)}) collective-permute-start(bf16[4,256,1024]{2,1,0:T(8,128)(2,1)} %dynamic-slice_bitcast_fusion.2), channel_id=1, source_target_pairs={{0,1},{1,0},{2,3},{3,2},{4,5},{5,4},{6,7},{7,6},{8,9},{9,8},{10,11... | collective-permute-start | bytes 6291464 | tf_op jit(solution)/shard_map/ppermute | solution.py:1362
  285.4 2.0 copy-start.5
  285.5 3.4 copy-start.7
  285.5 4.3 copy-start.3
  288.9 6.5 %collective-permute-start.1 = (bf16[4,128,2048]{2,1,0:T(8,128)(2,1)}, bf16[4,128,2048]{2,1,0:T(8,128)(2,1)S(1)}, u32[]{:S(2)}, u32[]{:S(2)}) collective-permute-start(bf16[4,128,2048]{2,1,0:T(8,128)(2,1)} %dynamic-slice_bitcast_fusion.1), channel_id=1, source_target_pairs={{0,1},{1,0},{2,3},{3,2},{4,5},{5,4},{6,7},{7,6},{8,9},{9,8},{10,11... | collective-permute-start | bytes 6291464 | tf_op jit(solution)/shard_map/ppermute | solution.py:1362
  291.8 3.6 copy-start.6
  298.6 94.3 %collective-permute-start.4 = (bf16[256,2048]{1,0:T(8,128)(2,1)}, bf16[256,2048]{1,0:T(8,128)(2,1)}, u32[]{:S(2)}, u32[]{:S(2)}) collective-permute-start(bf16[256,2048]{1,0:T(8,128)(2,1)} %get-tuple-element.164), channel_id=1, source_target_pairs={{0,6},{1,7},{2,4},{3,5},{4,2},{5,3},{6,0},{7,1},{8,14},{9,15},{10,... | collective-permute-start | bytes 3145736 | tf_op jit(solution)/shard_map/ppermute | solution.py:1362
  300.7 92.2 %collective-permute-start.3 = (bf16[256,2048]{1,0:T(8,128)(2,1)}, bf16[256,2048]{1,0:T(8,128)(2,1)}, u32[]{:S(2)}, u32[]{:S(2)}) collective-permute-start(bf16[256,2048]{1,0:T(8,128)(2,1)} %get-tuple-element.165), channel_id=1, source_target_pairs={{0,4},{1,5},{2,6},{3,7},{4,0},{5,1},{6,2},{7,3},{8,12},{9,13},{10,... | collective-permute-start | bytes 3145736 | tf_op jit(solution)/shard_map/ppermute | solution.py:1362
  301.5 91.4 %collective-permute-start.2 = (bf16[256,2048]{1,0:T(8,128)(2,1)}, bf16[256,2048]{1,0:T(8,128)(2,1)}, u32[]{:S(2)}, u32[]{:S(2)}) collective-permute-start(bf16[256,2048]{1,0:T(8,128)(2,1)} %get-tuple-element.166), channel_id=1, source_target_pairs={{0,2},{1,3},{2,0},{3,1},{4,6},{5,7},{6,4},{7,5},{8,10},{9,11},{10,... | collective-permute-start | bytes 3145736 | tf_op jit(solution)/shard_map/ppermute | solution.py:1362
  392.9 2.6 copy-start.9
  395.5 1.4 copy-start
  397.1 27.1 %collective-permute-start.7 = (bf16[64,2048]{1,0:T(8,128)(2,1)S(1)}, bf16[64,2048]{1,0:T(8,128)(2,1)S(1)}, u32[]{:S(2)}, u32[]{:S(2)}) collective-permute-start(bf16[64,2048]{1,0:T(8,128)(2,1)S(1)} %get-tuple-element.174), channel_id=1, source_target_pairs={{0,24},{8,16},{16,8},{24,0},{1,25},{9,17},{17,9},{25,1},{2,26},{10... | collective-permute-start | bytes 786440 | tf_op jit(solution)/shard_map/ppermute | solution.py:1362
  400.0 24.2 %collective-permute-start.6 = (bf16[64,2048]{1,0:T(8,128)(2,1)S(1)}, bf16[64,2048]{1,0:T(8,128)(2,1)S(1)}, u32[]{:S(2)}, u32[]{:S(2)}) collective-permute-start(bf16[64,2048]{1,0:T(8,128)(2,1)S(1)} %get-tuple-element.175), channel_id=1, source_target_pairs={{0,16},{8,24},{16,0},{24,8},{1,17},{9,25},{17,1},{25,9},{2,18},{10... | collective-permute-start | bytes 786440 | tf_op jit(solution)/shard_map/ppermute | solution.py:1362
  400.0 24.2 %collective-permute-start.5 = (bf16[64,2048]{1,0:T(8,128)(2,1)S(1)}, bf16[64,2048]{1,0:T(8,128)(2,1)S(1)}, u32[]{:S(2)}, u32[]{:S(2)}) collective-permute-start(bf16[64,2048]{1,0:T(8,128)(2,1)S(1)} %get-tuple-element.176), channel_id=1, source_target_pairs={{0,8},{8,0},{16,24},{24,16},{1,9},{9,1},{17,25},{25,17},{2,10},{10... | collective-permute-start | bytes 786440 | tf_op jit(solution)/shard_map/ppermute | solution.py:1362
  424.2 9.1 %copy-start.12 = (bf16[128,8,2048]{2,1,0:T(8,128)(2,1)S(1)}, bf16[128,8,2048]{2,1,0:T(8,128)(2,1)}, u32[]{:S(2)}) copy-start(bf16[128,8,2048]{2,1,0:T(8,128)(2,1)} %get-tuple-element.107) | copy-start | bytes 12582916
  432.8 2.3 copy-start.4
  433.0 42.6 %copy-start.10 = (bf16[64,2048]{1,0:T(8,128)(2,1)}, bf16[64,2048]{1,0:T(8,128)(2,1)S(1)}, u32[]{:S(2)}) copy-start(bf16[64,2048]{1,0:T(8,128)(2,1)S(1)} %add_convert_fusion.rest_0_) | copy-start | bytes 786436
  433.2 7.9 %collective-permute-start.8 = (bf16[4,128,2048]{2,1,0:T(8,128)(2,1)S(1)}, bf16[4,128,2048]{2,1,0:T(8,128)(2,1)S(1)}, u32[]{:S(2)}, u32[]{:S(2)}) collective-permute-start(bf16[4,128,2048]{2,1,0:T(8,128)(2,1)S(1)} %dynamic-slice_bitcast_fusion), channel_id=1, source_target_pairs={{0,1},{1,0},{2,3},{3,2},{4,5},{5,4},{6,7},{7,6},{8,9},{9,8},{10,11... | collective-permute-start | bytes 6291464 | tf_op jit(solution)/shard_map/ppermute | solution.py:1362
  442.9 32.7 %collective-permute-start.11 = (bf16[128,2048]{1,0:T(8,128)(2,1)S(1)}, bf16[128,2048]{1,0:T(8,128)(2,1)}, u32[]{:S(2)}, u32[]{:S(2)}) collective-permute-start(bf16[128,2048]{1,0:T(8,128)(2,1)S(1)} %get-tuple-element.168), channel_id=1, source_target_pairs={{0,6},{1,7},{2,4},{3,5},{4,2},{5,3},{6,0},{7,1},{8,14},{9,15},{10,... | collective-permute-start | bytes 1572872 | tf_op jit(solution)/shard_map/ppermute | solution.py:1362
  445.1 32.1 %collective-permute-start.10 = (bf16[128,2048]{1,0:T(8,128)(2,1)S(1)}, bf16[128,2048]{1,0:T(8,128)(2,1)}, u32[]{:S(2)}, u32[]{:S(2)}) collective-permute-start(bf16[128,2048]{1,0:T(8,128)(2,1)S(1)} %get-tuple-element.169), channel_id=1, source_target_pairs={{0,4},{1,5},{2,6},{3,7},{4,0},{5,1},{6,2},{7,3},{8,12},{9,13},{10,... | collective-permute-start | bytes 1572872 | tf_op jit(solution)/shard_map/ppermute | solution.py:1362
  445.8 31.4 %collective-permute-start.9 = (bf16[128,2048]{1,0:T(8,128)(2,1)S(1)}, bf16[128,2048]{1,0:T(8,128)(2,1)}, u32[]{:S(2)}, u32[]{:S(2)}) collective-permute-start(bf16[128,2048]{1,0:T(8,128)(2,1)S(1)} %get-tuple-element.170), channel_id=1, source_target_pairs={{0,2},{1,3},{2,0},{3,1},{4,6},{5,7},{6,4},{7,5},{8,10},{9,11},{10,... | collective-permute-start | bytes 1572872 | tf_op jit(solution)/shard_map/ppermute | solution.py:1362
  446.4 66.0 %collective-permute-start.14 = (bf16[64,2048]{1,0:T(8,128)(2,1)S(1)}, bf16[64,2048]{1,0:T(8,128)(2,1)}, u32[]{:S(2)}, u32[]{:S(2)}) collective-permute-start(bf16[64,2048]{1,0:T(8,128)(2,1)S(1)} %add_convert_fusion.rest_0_), channel_id=1, source_target_pairs={{0,24},{8,16},{16,8},{24,0},{1,25},{9,17},{17,9},{25,1},{2,26},{10... | collective-permute-start | bytes 786440 | tf_op jit(solution)/shard_map/ppermute | solution.py:1362
  449.2 63.2 %collective-permute-start.13 = (bf16[64,2048]{1,0:T(8,128)(2,1)S(1)}, bf16[64,2048]{1,0:T(8,128)(2,1)}, u32[]{:S(2)}, u32[]{:S(2)}) collective-permute-start(bf16[64,2048]{1,0:T(8,128)(2,1)S(1)} %add_convert_fusion.rest_0_), channel_id=1, source_target_pairs={{0,16},{8,24},{16,0},{24,8},{1,17},{9,25},{17,1},{25,9},{2,18},{10... | collective-permute-start | bytes 786440 | tf_op jit(solution)/shard_map/ppermute | solution.py:1362
  475.6 36.8 %collective-permute-start.12 = (bf16[64,2048]{1,0:T(8,128)(2,1)S(1)}, bf16[64,2048]{1,0:T(8,128)(2,1)S(1)}, u32[]{:S(2)}, u32[]{:S(2)}) collective-permute-start(bf16[64,2048]{1,0:T(8,128)(2,1)S(1)} %add_convert_fusion.rest_0_), channel_id=1, source_target_pairs={{0,8},{8,0},{16,24},{24,16},{1,9},{9,1},{17,25},{25,17},{2,10},{10... | collective-permute-start | bytes 786440 | tf_op jit(solution)/shard_map/ppermute | solution.py:1362
  512.4 0.7 copy-start.11

commit v4 on v3

--- a/solution.py
+++ b/solution.py
@@ -54,10 +54,14 @@
         term = lax.dot_general(left[...], rhs, dims, preferred_element_type=f32)
         total = term if total is None else total + term
         at += depth
-    out_ref[...] = total.astype(out_ref.dtype)
-
-
-def product(lefts, rhs, kind, across=False, part=0, parts=1):
+    if len(out_ref.shape) == 2:
+        out_ref[...] = total.astype(out_ref.dtype)
+    else:
+        for k in range(out_ref.shape[0]):
+            out_ref[k] = total[:, k * WIDE : (k + 1) * WIDE].astype(out_ref.dtype)
+
+
+def product(lefts, rhs, kind, across=False, part=0, parts=1, tiled=False):
     rows = lefts[0].shape[0]
     depth = sum(left.shape[1] for left in lefts)
     tile = 2 * WIDE if len(lefts) == 1 else WIDE
@@ -72,8 +76,10 @@
         functools.partial(product_kernel, across),
         grid=(columns // tile,),
         in_specs=[pl.BlockSpec(left.shape, lambda j: (0, 0)) for left in lefts] + [rhs_spec],
-        out_specs=pl.BlockSpec((rows, tile), lambda j: (0, j)),
-        out_shape=jax.ShapeDtypeStruct((rows, columns), kind),
+        out_specs=pl.BlockSpec((tile // WIDE, rows, WIDE), lambda j: (j, 0, 0))
+        if tiled
+        else pl.BlockSpec((rows, tile), lambda j: (0, j)),
+        out_shape=jax.ShapeDtypeStruct((columns // WIDE, rows, WIDE) if tiled else (rows, columns), kind),
         compiler_params=params(),
         cost_estimate=cost(0.01),
         name="product",
@@ -204,7 +210,7 @@
     )(mixed, grad, grad, prompt, piece, prompt_cot, piece_cot, halo, gain)
 
 
-def front_kernel(mix_ref, fw_ref, fb_ref, sel_ref, act_ref, proj_ref):
+def front_kernel(mix_ref, fw_ref, fb_ref, sel_ref, act_ref, bend_ref, proj_ref):
     j = pl.program_id(0)
     steps = act_ref.shape[0]
     chunk = 16
@@ -221,8 +227,10 @@
         v = bias[None] + taps[0][None] * x[1 : 1 + chunk]
         for k in range(1, KERNEL):
             v = v + taps[k][None] * x[1 + k : 1 + k + chunk]
-        act = v * sigmoid(v)
+        sig = sigmoid(v)
+        act = v * sig
         act_ref[pl.ds(t, chunk)] = act
+        bend_ref[pl.ds(t, chunk)] = (sig + act * (1.0 - sig)).astype(bf16)
         low = act.reshape(chunk * SEQS, act.shape[-1]).astype(bf16)
         r = pl.multiple_of(t * SEQS, chunk * SEQS)
         proj_ref[pl.ds(r, chunk * SEQS), :] += jnp.dot(low, sel_ref[...], preferred_element_type=f32)
@@ -237,17 +245,19 @@
         front_kernel,
         grid=(channels // WIDE,),
         in_specs=[
-            pl.BlockSpec((steps + HALO, SEQS, WIDE), lambda j: (0, 0, j)),
+            pl.BlockSpec((None, steps + HALO, SEQS, WIDE), lambda j: (j, 0, 0, 0)),
             pl.BlockSpec((KERNEL, WIDE), lambda j: (0, j)),
             pl.BlockSpec((1, WIDE), lambda j: (0, j)),
             pl.BlockSpec((WIDE, LANES), lambda j: (j, 0)),
         ],
         out_specs=[
-            pl.BlockSpec((steps, SEQS, WIDE), lambda j: (0, 0, j)),
+            pl.BlockSpec((None, steps, SEQS, WIDE), lambda j: (j, 0, 0, 0)),
+            pl.BlockSpec((None, steps, SEQS, WIDE), lambda j: (j, 0, 0, 0)),
             pl.BlockSpec((steps * SEQS, LANES), lambda j: (0, 0)),
         ],
         out_shape=[
-            jax.ShapeDtypeStruct((steps, SEQS, channels), f32),
+            jax.ShapeDtypeStruct((channels // WIDE, steps, SEQS, WIDE), f32),
+            jax.ShapeDtypeStruct((channels // WIDE, steps, SEQS, WIDE), bf16),
             jax.ShapeDtypeStruct((steps * SEQS, LANES), f32),
         ],
         compiler_params=params(),
@@ -427,18 +437,18 @@
 
 
 def piece(proj, act, gate, gated_grad, step_pad, sbias, rate, select, groups):
-    steps, _, channels = act.shape
-    grid = channels // WIDE
+    grid, steps, _, _ = act.shape
+    channels = grid * WIDE
     wide = lambda j: (0, 0, j)
-    flat = pl.BlockSpec((steps, SEQS, WIDE), wide)
-    shape = (steps, SEQS, channels)
+    flat = pl.BlockSpec((None, steps, SEQS, WIDE), lambda j: (j, 0, 0, 0))
+    shape = act.shape
     return pl.pallas_call(
         piece_kernel,
         grid=(grid,),
         in_specs=[
             pl.BlockSpec((steps * SEQS, LANES), lambda j: (0, 0)),
             flat,
-            pl.BlockSpec((steps + HALO, SEQS, WIDE), wide),
+            pl.BlockSpec((None, steps + HALO, SEQS, WIDE), lambda j: (j, 0, 0, 0)),
             flat,
             pl.BlockSpec((LANES, WIDE), lambda j: (0, j)),
             pl.BlockSpec((1, WIDE), lambda j: (0, j)),
@@ -474,19 +484,19 @@
 
 
 def chain_kernel(
-    one_hot_ref, ahead_ref, behind_ref, branch_ref, time_ref, rate_ref, start_out, end_out,
+    one_hot_ref, ahead_ref, behind_ref, time_ref, rate_ref, start_out, end_out,
     moved_ref, got, got_time, back, done, sems, time_sems, back_sems,
 ):
     size = got.shape[0]
     width = got.shape[2]
     count = PROMPTS * STATES
-    sequels = branch_ref.shape[0]
+    sequels = one_hot_ref.shape[0]
     me = lax.axis_index("fsdp")
     for p in range(PROMPTS):
         rows = slice(p * STATES, (p + 1) * STATES)
-        total = one_hot_ref[0, p] * branch_ref[0]
+        total = one_hot_ref[0, p] * behind_ref[PROMPTS]
         for k in range(1, sequels):
-            total = total + one_hot_ref[k, p] * branch_ref[k]
+            total = total + one_hot_ref[k, p] * behind_ref[PROMPTS + k]
         moved_ref[0 * count + p * STATES : 0 * count + (p + 1) * STATES] = ahead_ref[p].astype(bf16)
         moved_ref[1 * count + p * STATES : 1 * count + (p + 1) * STATES] = behind_ref[p].astype(bf16)
         moved_ref[2 * count + p * STATES : 2 * count + (p + 1) * STATES] = total.astype(bf16)
@@ -571,17 +581,17 @@
             end_out[PROMPTS + q, :, columns_k] = jnp.zeros_like(total)
 
 
-def chain(one_hot, ahead, behind, branch, time, rate):
+def chain(one_hot, ahead, behind, time, rate):
     size = lax.axis_size("fsdp")
     channels = ahead.shape[2]
     rows = 3 * PROMPTS * STATES
     width = channels // size
     own = lax.dynamic_slice_in_dim(rate, lax.axis_index("fsdp") * width, width, 1)
     whole = pl.BlockSpec(memory_space=pltpu.VMEM)
-    shape = (PROMPTS + branch.shape[0], STATES, channels)
+    shape = (PROMPTS + one_hot.shape[0], STATES, channels)
     return pl.pallas_call(
         chain_kernel,
-        in_specs=[pl.BlockSpec(memory_space=pltpu.SMEM)] + [whole] * 5,
+        in_specs=[pl.BlockSpec(memory_space=pltpu.SMEM)] + [whole] * 4,
         out_specs=[whole] * 2,
         out_shape=[jax.ShapeDtypeStruct(shape, f32)] * 2,
         scratch_shapes=[
@@ -597,7 +607,7 @@
         compiler_params=params(collective_id=1, has_side_effects=True),
         cost_estimate=cost(25),
         name="chain",
-    )(one_hot, ahead, behind, branch, time, own)
+    )(one_hot, ahead, behind, time, own)
 
 
 TILES = [slice(k * LANES, (k + 1) * LANES) for k in range(WIDE // LANES)]
@@ -616,46 +626,48 @@
         spread_maps(proj_ref, select_ref, RANK, STATES, store_plain(b_scr))
         spread_maps(proj_ref, select_ref, RANK + STATES, STATES, store_pairs(c_scr))
 
-    rates = [jnp.broadcast_to(rate_ref[n : n + 1, :], (SEQS, LANES)) for n in range(STATES)]
-    skip = jnp.broadcast_to(skip_ref[0:1, :], (SEQS, LANES))
-    gategrad_ref[0:HALO] = jnp.zeros((HALO, SEQS, LANES), bf16)
+    gategrad_ref[0:HALO] = jnp.zeros((HALO, SEQS, WIDE), bf16)
     unroll = 8
 
-    def run(i, carry):
-        h, skip_sum = carry
-        for k in range(unroll):
-            t = i * unroll + k
-            dt = dt_ref[t]
-            act = act_ref[t]
-            u = dt * act
-            new = []
-            y = None
-            for p in range(PAIRS):
-                for n in (2 * p, 2 * p + 1):
-                    new.append(jnp.exp2(dt * rates[n]) * h[n] + u * b_scr[t, n])
-                low = pair(new[2 * p], new[2 * p + 1])
-                hist_ref[t + 1, p] = low
-                term = low * c_scr[t, p]
-                y = term if p == 0 else y + term
-            h = tuple(new)
-            mixed = folded(y) + skip * act
-            gated_ref[t] = (mixed * silu_ref[t].astype(f32)).astype(bf16)
-            gategrad_ref[t + HALO] = (mixed * slope_ref[t].astype(f32)).astype(bf16)
-            skip_sum = skip_sum + yg_ref[t] * act
-        return h, skip_sum
-
-    start = tuple(start_ref[:, n, :] for n in range(STATES))
-    for p in range(PAIRS):
-        hist_ref[0, p] = pair(start[2 * p], start[2 * p + 1])
-    _, skip_sum = lax.fori_loop(0, steps // unroll, run, (start, jnp.zeros((SEQS, LANES), f32)))
-    skipg_ref[...] = jnp.sum(skip_sum, axis=0, keepdims=True)
+    for part, cols in enumerate(TILES):
+        rates = [jnp.broadcast_to(rate_ref[n : n + 1, cols], (SEQS, LANES)) for n in range(STATES)]
+        skip = jnp.broadcast_to(skip_ref[0:1, cols], (SEQS, LANES))
+
+        def run(i, carry):
+            h, skip_sum = carry
+            for k in range(unroll):
+                t = i * unroll + k
+                dt = dt_ref[t, :, cols]
+                act = act_ref[t, :, cols]
+                u = dt * act
+                new = []
+                y = None
+                for p in range(PAIRS):
+                    for n in (2 * p, 2 * p + 1):
+                        new.append(jnp.exp2(dt * rates[n]) * h[n] + u * b_scr[t, n])
+                    low = pair(new[2 * p], new[2 * p + 1])
+                    hist_ref[part, t + 1, p] = low
+                    term = low * c_scr[t, p]
+                    y = term if p == 0 else y + term
+                h = tuple(new)
+                mixed = folded(y) + skip * act
+                gated_ref[t, :, cols] = (mixed * silu_ref[t, :, cols].astype(f32)).astype(bf16)
+                gategrad_ref[t + HALO, :, cols] = (mixed * slope_ref[t, :, cols].astype(f32)).astype(bf16)
+                skip_sum = skip_sum + yg_ref[t, :, cols] * act
+            return h, skip_sum
+
+        start = tuple(start_ref[:, n, cols] for n in range(STATES))
+        for p in range(PAIRS):
+            hist_ref[part, 0, p] = pair(start[2 * p], start[2 * p + 1])
+        _, skip_sum = lax.fori_loop(0, steps // unroll, run, (start, jnp.zeros((SEQS, LANES), f32)))
+        skipg_ref[:, cols] = jnp.sum(skip_sum, axis=0, keepdims=True)
 
 
 def forward(proj, dt, act, yg, silu, slope, rate, start, skip, select):
-    steps, _, channels = act.shape
-    grid = channels // LANES
+    grid, steps, _, _ = act.shape
+    channels = grid * WIDE
     tile = lambda j: (0, 0, j)
-    flat = pl.BlockSpec((steps, SEQS, LANES), tile)
+    flat = pl.BlockSpec((None, steps, SEQS, WIDE), lambda j: (j, 0, 0, 0))
     parts = len(TILES)
     return pl.pallas_call(
         forward_kernel,
@@ -663,23 +675,20 @@
         in_specs=[
             pl.BlockSpec((steps * SEQS, LANES), lambda j: (0, 0)),
             flat, flat, flat, flat, flat,
-            pl.BlockSpec((STATES, LANES), lambda j: (0, j)),
-            pl.BlockSpec((SEQS, STATES, LANES), tile),
-            pl.BlockSpec((1, LANES), lambda j: (0, j)),
+            pl.BlockSpec((STATES, WIDE), lambda j: (0, j)),
+            pl.BlockSpec((SEQS, STATES, WIDE), tile),
+            pl.BlockSpec((1, WIDE), lambda j: (0, j)),
             pl.BlockSpec(select.shape, lambda j: (0, 0)),
         ],
         out_specs=[
-            flat,
-            pl.BlockSpec(
-                (None, None, steps + 1, PAIRS, 2 * SEQS, LANES),
-                lambda j: (j // parts, j % parts, 0, 0, 0, 0),
-            ),
-            pl.BlockSpec((steps + HALO, SEQS, LANES), tile),
-            pl.BlockSpec((1, LANES), lambda j: (0, j)),
+            pl.BlockSpec((steps, SEQS, WIDE), tile),
+            pl.BlockSpec((None, parts, steps + 1, PAIRS, 2 * SEQS, LANES), lambda j: (j, 0, 0, 0, 0, 0)),
+            pl.BlockSpec((steps + HALO, SEQS, WIDE), tile),
+            pl.BlockSpec((1, WIDE), lambda j: (0, j)),
         ],
         out_shape=[
             jax.ShapeDtypeStruct((steps, SEQS, channels), bf16),
-            jax.ShapeDtypeStruct((grid // parts, parts, steps + 1, PAIRS, 2 * SEQS, LANES), bf16),
+            jax.ShapeDtypeStruct((grid, parts, steps + 1, PAIRS, 2 * SEQS, LANES), bf16),
             jax.ShapeDtypeStruct((steps + HALO, SEQS, channels), bf16),
             jax.ShapeDtypeStruct((1, channels), f32),
         ],
@@ -807,11 +816,11 @@
 
 
 def backward(proj, dt, sig, act, yg, rate, end, skip, hist, rank_t, stepw_t, pick, select):
-    steps, _, channels = act.shape
-    grid = channels // WIDE
+    grid, steps, _, _ = act.shape
+    channels = grid * WIDE
     tile = lambda j: (0, 0, j)
     whole = lambda j: (0, 0)
-    flat = pl.BlockSpec((steps, SEQS, WIDE), tile)
+    flat = pl.BlockSpec((None, steps, SEQS, WIDE), lambda j: (j, 0, 0, 0))
     sums = pltpu.VMEM((steps, PAIRS, 2 * SEQS, LANES), bf16)
     return pl.pallas_call(
         backward_kernel,
@@ -838,7 +847,7 @@
             pl.BlockSpec((steps * SEQS, LANES), whole),
         ],
         out_shape=[
-            jax.ShapeDtypeStruct((steps, SEQS, channels), f32),
+            jax.ShapeDtypeStruct(act.shape, f32),
             jax.ShapeDtypeStruct((RANK, channels), f32),
             jax.ShapeDtypeStruct((1, channels), f32),
             jax.ShapeDtypeStruct((STATES, channels), f32),
@@ -861,14 +870,13 @@
 
 
 def filter_back_kernel(
-    mix_ref, act_ref, act_grad_ref, projg_ref, projg_t_ref, sel_ref, fw_ref, fb_ref,
+    mix_ref, act_ref, bend_ref, act_grad_ref, projg_ref, projg_t_ref, sel_ref, fw_ref,
     mixgrad_ref, selg_ref, fwg_ref, fbg_ref,
     dv_scr,
 ):
     steps = act_ref.shape[0]
     chunk = 16
     taps = [fw_ref[k : k + 1, :] for k in range(KERNEL)]
-    bias = fb_ref[0:1, :]
     zero = jnp.zeros((HALO, SEQS, WIDE), f32)
     dv_scr[0:HALO] = zero
     dv_scr[steps + HALO :] = zero
@@ -876,14 +884,10 @@
     def step(i, sums):
         t = i * chunk
         x = mix_ref[pl.ds(t, chunk + HALO)].astype(f32)
-        v = bias[None] + taps[0][None] * x[1 : 1 + chunk]
-        for k in range(1, KERNEL):
-            v = v + taps[k][None] * x[1 + k : 1 + k + chunk]
-        sig = sigmoid(v)
         r = pl.multiple_of(t * SEQS, chunk * SEQS)
         more = contract_cols(projg_ref[pl.ds(r, chunk * SEQS), :], sel_ref[...])
         total = act_grad_ref[pl.ds(t, chunk)] + more.reshape(chunk, SEQS, WIDE)
-        dv = total * (sig * (1.0 + v * (1.0 - sig)))
+        dv = total * bend_ref[pl.ds(t, chunk)].astype(f32)
         dv_scr[pl.ds(t + HALO, chunk)] = dv
         new = [sums[0] + jnp.sum(dv, axis=0)]
         for k in range(KERNEL):
@@ -915,9 +919,9 @@
     selg_ref[...] = jnp.dot(projg_t_ref[...], low, preferred_element_type=f32)
 
 
-def filter_back(mixture, act, act_grad, projg, projg_t, select_pad, fw, fb):
-    steps, _, channels = act.shape
-    grid = channels // WIDE
+def filter_back(mixture, act, bend, act_grad, projg, projg_t, select_pad, fw):
+    grid, steps, _, _ = act.shape
+    channels = grid * WIDE
     wide = lambda j: (0, 0, j)
     whole = lambda j: (0, 0)
     cols = lambda j: (0, j)
@@ -925,14 +929,14 @@
         filter_back_kernel,
         grid=(grid,),
         in_specs=[
-            pl.BlockSpec((steps + HALO, SEQS, WIDE), wide),
-            pl.BlockSpec((steps, SEQS, WIDE), wide),
-            pl.BlockSpec((steps, SEQS, WIDE), wide),
+            pl.BlockSpec((None, steps + HALO, SEQS, WIDE), lambda j: (j, 0, 0, 0)),
+            pl.BlockSpec((None, steps, SEQS, WIDE), lambda j: (j, 0, 0, 0)),
+            pl.BlockSpec((None, steps, SEQS, WIDE), lambda j: (j, 0, 0, 0)),
+            pl.BlockSpec((None, steps, SEQS, WIDE), lambda j: (j, 0, 0, 0)),
             pl.BlockSpec((steps * SEQS, LANES), whole),
             pl.BlockSpec((LANES, steps * SEQS), whole),
             pl.BlockSpec((WIDE, LANES), lambda j: (j, 0)),
             pl.BlockSpec((KERNEL, WIDE), cols),
-            pl.BlockSpec((1, WIDE), cols),
         ],
         out_specs=[
             pl.BlockSpec((steps + HALO, SEQS, WIDE), wide),
@@ -950,7 +954,7 @@
         compiler_params=params(),
         cost_estimate=cost(20),
         name="filter_back",
-    )(mixture, act, act_grad, projg, projg_t, select_pad, fw, fb)
+    )(mixture, act, bend, act_grad, projg, projg_t, select_pad, fw)
 
 
 def send(src, dst, send_sem, recv_sem, peer, axis="fsdp"):
@@ -1451,12 +1455,13 @@
     piece_cot = sequel_cotangent.reshape(-1, steps, D)
     scaled, cotangent = prepare(prompt_hidden, pieces, prompt_cotangent, piece_cot, halo, gain)
 
-    mixture = product([scaled], full_input, bf16, part=0, parts=2)
-    gate = product([scaled], full_input, f32, part=1, parts=2)
-    mixture = mixture.reshape(steps + HALO, SEQS, INNER)
-    gate = gate.reshape(steps + HALO, SEQS, INNER)
-    gated_grad = product([cotangent], full_output, f32, across=True).reshape(steps, SEQS, INNER)
-    act, proj = front(mixture, fw, fb, select_pad, steps)
+    mixture = product([scaled], full_input, bf16, part=0, parts=2, tiled=True)
+    gate = product([scaled], full_input, f32, part=1, parts=2, tiled=True)
+    mixture = mixture.reshape(-1, steps + HALO, SEQS, WIDE)
+    gate = gate.reshape(-1, steps + HALO, SEQS, WIDE)
+    gated_grad = product([cotangent], full_output, f32, across=True, tiled=True)
+    gated_grad = gated_grad.reshape(-1, steps, SEQS, WIDE)
+    act, bend, proj = front(mixture, fw, fb, select_pad, steps)
     groups = 1 if split == 1 else 2
     lane = jnp.arange(2 * STATES * LANES)[None, :]
     select = (jnp.arange(LANES)[:, None] == RANK + lane // LANES).astype(bf16)
@@ -1472,7 +1477,8 @@
     for p in range(split - 2, -1, -1):
         own_end.insert(0, back)
         back = own_behind[:, p] + jnp.exp2(rate * own[:, p]) * back
-    start, end = chain(one_hot, ahead[:half], behind[:half], back, total, rate)
+    joint = behind if split == 1 else jnp.concatenate([behind[:half], back], axis=0)
+    start, end = chain(one_hot, ahead, joint, total, rate)
     if split > 1:
         state = start[half:]
         own_start = [state]
@@ -1509,7 +1515,7 @@
     projg, early = after((projg, early))
     early = to_replicas(early)
     filter_in_grad, select_grad, filter_grad, filter_bias_grad = filter_back(
-        mixture, act, act_grad, projg, projg.T, select_pad, fw, fb
+        mixture, act, bend, act_grad, projg, projg.T, select_pad, fw
     )
     filter_in_grad, early = after((filter_in_grad, early))
     early = summed(*early).astype(bf16)

time: 519 us -> 514 us (level)
  transfers between devices with their start and end apart: 15 -> 15, of which waited for: 0 -> 0; matrix products, arithmetic and copies ran while one was open for 4% -> 5% of each run, Pallas kernels for 34% -> 34%
where the time goes in v4:
time: 514 us; the launch traced here: 513 us
  Pallas kernels  414 us (81%)
  matrix products  32.2 us (6%)
  local copies, waits for them, and re-layouts  32.1 us (6%)
  starting transfers between devices  17 us (3%)
  other arithmetic  15.6 us (3%)
    pallas_call x1, Pallas kernels, backward(): pl.pallas_call(backward_kernel, grid=(grid,), in_specs=[pl.BlockSpec((ste...  90.7 us
    pallas_call x1, Pallas kernels, piece(): pl.pallas_call(piece_kernel, grid=(grid,), in_specs=[pl.BlockSpec((steps...  61.6 us
    pallas_call x1, Pallas kernels, gather(): pl.pallas_call(gather_kernel, in_specs=[vmem] * 4, out_specs=[hbm] * 4, o...  50.4 us
    pallas_call x1, Pallas kernels, forward(): pl.pallas_call(forward_kernel, grid=(grid,), in_specs=[pl.BlockSpec((step...  49.1 us
    pallas_call x4, Pallas kernels, product(): pl.pallas_call(functools.partial(product_kernel, across), grid=(columns /...  42 us
    pallas_call x1, Pallas kernels, tail(): pl.pallas_call(tail_kernel, in_specs=[pl.BlockSpec(memory_space=pltpu.SME...  35.2 us
    dot_general x3, matrix products, contract_rows(): lax.dot_general(left_side, right_side, (((0,), (0,)), ((), ())), preferre...  26.1 us
    pallas_call x1, Pallas kernels, chain(): pl.pallas_call(chain_kernel, in_specs=[pl.BlockSpec(memory_space=pltpu.SM...  24.4 us
  transfers between devices with their start and end apart: 15, of which 0 were waited for; matrix products, arithmetic and copies ran while one was open for 5% of the time, Pallas kernels for 34%

profile of v4, /device:TPU:0, one launch (start us, length us, event | category | flops | bytes accessed | tf_op | source)
XLA Modules:
  0.0 512.7 jit_solution(9567858500462739429)
XLA Ops:
  6.2 1.5 concatenate.15
  10.7 50.4 %gather.7 = (bf16[1024,256]{1,0:T(8,128)(2,1)}, bf16[2048,128]{1,0:T(8,128)(2,1)}, bf16[2048,1024]{1,0:T(8,128)(2,1)}, bf16[1024,4096]{1,0:T(8,128)(2,1)}) custom-call(bf16[128,256]{1,0:T(8,128)(2,1)} %pad.21.rows_ref, bf16[256,128]{1,0:T(8,128)(2,1)} %fusion.14.select_ref, bf16[256,1024]{1,0:T(8,128)(2,1)} %out_ref.1, bf16[128,4096]{1,0:T(8,128)(2,1)} %in_ref.1), custom_call_target="tpu_custom_call" | custom-call | flops 54999998464 | tf_op jit(solution)/shard_map/gather/pallas_call | solution.py:1123
  67.9 8.2 %prepare.1 = (bf16[1056,1024]{1,0:T(8,128)(2,1)}, bf16[1024,1024]{1,0:T(8,128)(2,1)}) custom-call(bf16[4,128,1024]{2,1,0:T(8,128)(2,1)} %prompt_ref.3, bf16[4,128,1024]{2,1,0:T(8,128)(2,1)} %piece_ref.3, bf16[4,128,1024]{2,1,0:T(8,128)(2,1)} %prompt_cot_ref.3, bf16[4,128,1024]{2,1,0:T(8,128)(2,1)} %piece_cot_ref.3, f32[32,1024]{1,0:T(8,128)} %bitcast_convert_fusion.halo_ref, ...), custom_call_target="tpu_custom_call" | custom-call | flops 5000000000 | tf_op jit(solution)/shard_map/prepare/pallas_call | solution.py:122
  76.1 8.5 %product.4 = bf16[8,1056,256]{2,1,0:T(8,128)(2,1)} custom-call(bf16[1056,1024]{1,0:T(8,128)(2,1)} %get-tuple-element.91.refs_0_, bf16[1024,4096]{1,0:T(8,128)(2,1)} %get-tuple-element.92.refs_1_.refs_2_), custom_call_target="tpu_custom_call" | custom-call | flops 10000000 | tf_op jit(solution)/shard_map/product/pallas_call | solution.py:75
  84.6 9.3 %product.5 = f32[8,1056,256]{2,1,0:T(8,128)} custom-call(bf16[1056,1024]{1,0:T(8,128)(2,1)} %get-tuple-element.91.refs_0_, bf16[1024,4096]{1,0:T(8,128)(2,1)} %get-tuple-element.92.refs_1_.refs_2_), custom_call_target="tpu_custom_call" | custom-call | flops 10000000 | tf_op jit(solution)/shard_map/product/pallas_call | solution.py:75
  98.8 9.2 %product.6 = f32[8,1024,256]{2,1,0:T(8,128)} custom-call(bf16[1024,1024]{1,0:T(8,128)(2,1)} %get-tuple-element.97.refs_0_, bf16[2048,1024]{1,0:T(8,128)(2,1)} %get-tuple-element.98.refs_1_), custom_call_target="tpu_custom_call" | custom-call | flops 10000000 | tf_op jit(solution)/shard_map/product/pallas_call | solution.py:75
  107.9 16.5 %front.1 = (f32[8,128,8,256]{3,2,1,0:T(8,128)}, bf16[8,128,8,256]{3,2,1,0:T(8,128)(2,1)}, f32[1024,128]{1,0:T(8,128)}) custom-call(bf16[8,132,8,256]{3,2,1,0:T(8,128)(2,1)} %bitcast.108, f32[4,2048]{1,0:T(4,128)} %bitcast.124, f32[1,2048]{1,0:T(1,128)} %bitcast.129, bf16[2048,128]{1,0:T(8,128)(2,1)} %get-tuple-element.93.sel_ref), custom_call_target="tpu_custom_call" | custom-call | flops 16000000000 | tf_op jit(solution)/shard_map/front/pallas_call | solution.py:244
  124.5 61.6 %piece.1 = (f32[8,128,8,256]{3,2,1,0:T(8,128)}, bf16[8,128,8,256]{3,2,1,0:T(8,128)(2,1)}, f32[8,128,8,256]{3,2,1,0:T(8,128)}, bf16[8,128,8,256]{3,2,1,0:T(8,128)...) custom-call(f32[1024,128]{1,0:T(8,128)} %get-tuple-element.96.proj_r, ...), custom_call_target="tpu_custom_call" | custom-call | flops 60000002048 | tf_op jit(solution)/shard_map/piece/pallas_call | solution.py:445
  186.1 24.4 %chain.1 = (f32[8,16,2048]{2,1,0:T(8,128)}, f32[8,16,2048]{2,1,0:T(8,128)}) custom-call(f32[4,4]{1,0:T(4,128)} %fusion.20.one_hot_ref, f32[4,16,2048]{2,1,0:T(8,128)} %get-tuple-element.102.ahead_ref, f32[8,16,2048]{2,1,0:T(8,128)} %get-tuple-element.103.behind_ref, f32[8,2048]{1,0:T(8,128)} %get-tuple-element.104.time_ref, ...), custom_call_target="tpu_custom_call" | custom-call | flops 24999999488 | tf_op jit(solution)/shard_map/chain/pallas_call | solution.py:592
  210.5 49.1 %forward_scan.1 = (bf16[128,8,2048]{2,1,0:T(8,128)(2,1)}, bf16[8,2,129,8,16,128]{5,4,3,2,1,0:T(8,128)(2,1)}, bf16[132,8,2048]{2,1,0:T(8,128)(2,1)}, f32[1,2048]{1,0:T(1,128)}) custom-call(f32[1024,128]{1,0:T(8,128)} %get-tuple-element.96.proj_ref, f32[8,128,8,256]{3,2,1,0:T(8,128)} %get-tuple-element.99.dt_ref, ...), custom_call_target="tpu_custom_call" | custom-call | flops 49999998976 | tf_op jit(solution)/shard_map/forward_scan/pallas_call | solution.py:672
  259.6 9.5 %fusion.7 = bf16[2048,1024]{1,0:T(8,128)(2,1)} fusion(bf16[1024,1024]{1,0:T(8,128)(2,1)} %get-tuple-element.97.refs_0_, bf16[128,8,2048]{2,1,0:T(8,128)(2,1)} %get-tuple-element.109), kind=kOutput, calls=%fused_computation.12 | convolution fusion | flops 4297064448 | bytes 10485760 | tf_op jit(solution)/shard_map/dot_general | solution.py:1354
  269.0 3.2 dynamic-slice_bitcast_fusion.2
  273.2 8.1 %convolution_convert_fusion.1 = bf16[1024,2048]{1,0:T(8,128)(2,1)S(1)} fusion(bf16[1056,1024]{1,0:T(8,128)(2,1)S(1)} %copy-done.1, bf16[132,8,2048]{2,1,0:T(8,128)(2,1)} %get-tuple-element.110), kind=kOutput, calls=%fused_computation.14 | convolution fusion | flops 4431282176 | bytes 10682368 | tf_op jit(solution)/shard_map/dot_general | solution.py:1354
  281.4 2.0 copy-done.5
  287.8 3.4 fusion.2
  292.8 1.7 dynamic-slice_bitcast_fusion.3
  294.5 2.2 collective-permute-start.4
  298.0 90.7 %backward_scan.1 = (f32[8,128,8,256]{3,2,1,0:T(8,128)}, f32[64,2048]{1,0:T(8,128)}, f32[1,2048]{1,0:T(1,128)}, f32[16,2048]{1,0:T(8,128)}, bf16[1024,128]{1,0:T(8,128)(2,1)}) custom-call(f32[1024,128]{1,0:T(8,128)} %get-tuple-element.96.proj_ref, f32[8,128,8,256]{3,2,1,0:T(8,128)} %get-tuple-element.99.dt_ref, ...), custom_call_target="tpu_custom_call" | custom-call | flops 89999998976 | tf_op jit(solution)/shard_map/backward_scan/pallas_call | solution.py:825
  388.8 2.5 convert_add_fusion.3
  392.9 2.9 collective-permute-start.7
  395.9 1.5 collective-permute-start.5
  397.4 21.7 %filter_back.1 = (bf16[132,8,2048]{2,1,0:T(8,128)(2,1)}, f32[128,2048]{1,0:T(8,128)}, f32[4,2048]{1,0:T(4,128)}, f32[1,2048]{1,0:T(1,128)}) custom-call(bf16[8,132,8,256]{3,2,1,0:T(8,128)(2,1)} %bitcast.109, f32[8,128,8,256]{3,2,1,0:T(8,128)} %get-tuple-element.94.act_ref, bf16[8,128,8,256]{3,2,1,0:T(8,128)(2,1)} %get-tuple-element.95.bend_ref, ...), custom_call_target="tpu_custom_call" | custom-call | flops 20000000000 | tf_op jit(solution)/shard_map/filter_back/pallas_call | solution.py:928
  420.2 8.6 %convolution_convert_fusion = bf16[1024,2048]{1,0:T(8,128)(2,1)S(1)} fusion(bf16[1056,1024]{1,0:T(8,128)(2,1)} %get-tuple-element.91.refs_0_, bf16[132,8,2048]{2,1,0:T(8,128)(2,1)} %get-tuple-element.124), kind=kOutput, calls=%fused_computation.13 | convolution fusion | flops 4431282176 | bytes 10682368 | tf_op jit(solution)/shard_map/dot_general | solution.py:1354
  429.3 1.8 copy-done.4
  431.0 6.1 %fusion.3.mixed_ref = f32[1024,1024]{1,0:T(8,128)} fusion(bf16[2048,1024]{1,0:T(8,128)(2,1)S(1)} %copy-done.4, bf16[128,8,2048]{2,1,0:T(8,128)(2,1)S(1)} %copy-done.12), kind=kOutput, calls=%fused_computation.8 | convolution fusion | flops 4294967296 | bytes 12582912 | tf_op jit(solution)/shard_map/dot_general | solution.py:1527
  438.9 2.2 collective-permute-start.11
  442.4 2.9 collective-permute-start.14
  445.2 15.0 %product.7.grad_ref.grad_halo_ref = f32[1056,1024]{1,0:T(8,128)} custom-call(bf16[1056,2048]{1,0:T(8,128)(2,1)} %bitcast.111, bf16[1056,2048]{1,0:T(8,128)(2,1)} %bitcast.110, bf16[1024,4096]{1,0:T(8,128)(2,1)} %get-tuple-element.92.refs_1_.refs_2_), custom_call_target="tpu_custom_call" | custom-call | flops 10000000 | tf_op jit(solution)/shard_map/product/pallas_call | solution.py:75
  460.2 11.3 %finish.1 = (bf16[4,128,1024]{2,1,0:T(8,128)(2,1)}, bf16[4,128,1024]{2,1,0:T(8,128)(2,1)}, f32[4,128,1024]{2,1,0:T(8,128)}, f32[4,128,1024]{2,1,0:T(8,128)}, f32[32,1024]{1,0:T(8,128)}, /*index=5*/f32[1,1024]{1,0:T(1,128)}) custom-call(f32[1024,1024]{1,0:T(8,128)} %fusion.3.mixed_ref, f32[1056,1024]{1,0:T(8,128)} %product.7.grad_ref.grad_halo_ref, ...), custom_call_target="tpu_custom_call" | custom-call | flops 10000000 | tf_op jit(solution)/shard_map/finish/pallas_call | solution.py:188
  471.5 1.6 collective-permute-start.12
  473.1 35.2 %tail.1 = (bf16[128,2048]{1,0:T(8,128)(2,1)}, bf16[192,256]{1,0:T(8,128)(2,1)}, f32[16,1024]{1,0:T(8,128)}) custom-call(f32[4,4]{1,0:T(4,128)} %fusion.20.one_hot_ref, bf16[128,2048]{1,0:T(8,128)(2,1)} %get-tuple-element.136.b0, bf16[128,2048]{1,0:T(8,128)(2,1)} %collective-permute-done.9.b1, bf16[128,2048]{1,0:T(8,128)(2,1)} %collective-permute-done.10.b2, ...), custom_call_target="tpu_custom_call" | custom-call | flops 30000001024 | tf_op jit(solution)/shard_map/tail/pallas_call | solution.py:1273
  509.0 3.5 deliver.1
  (104 shorter events, 35.2 us)
Async XLA Ops:
  84.6 12.7 %copy-start.8 = (bf16[2048,128]{1,0:T(8,128)(2,1)S(1)}, bf16[2048,128]{1,0:T(8,128)(2,1)}, u32[]{:S(2)}) copy-start(bf16[2048,128]{1,0:T(8,128)(2,1)} %get-tuple-element.93.sel_ref) | copy-start | bytes 1572868
  95.4 0.8 copy-start.2
  269.0 4.2 copy-start.1
  272.2 15.6 %collective-permute-start = (bf16[4,256,1024]{2,1,0:T(8,128)(2,1)}, bf16[4,256,1024]{2,1,0:T(8,128)(2,1)}, u32[]{:S(2)}, u32[]{:S(2)}) collective-permute-start(bf16[4,256,1024]{2,1,0:T(8,128)(2,1)} %dynamic-slice_bitcast_fusion.2), channel_id=1, source_target_pairs={{0,1},{1,0},{2,3},{3,2},{4,5},{5,4},{6,7},{7,6},{8,9},{9,8},{10,11... | collective-permute-start | bytes 6291464 | tf_op jit(solution)/shard_map/ppermute | solution.py:1366
  281.4 2.0 copy-start.5
  281.4 3.4 copy-start.7
  281.4 4.3 copy-start.3
  284.8 6.6 %collective-permute-start.1 = (bf16[4,128,2048]{2,1,0:T(8,128)(2,1)}, bf16[4,128,2048]{2,1,0:T(8,128)(2,1)S(1)}, u32[]{:S(2)}, u32[]{:S(2)}) collective-permute-start(bf16[4,128,2048]{2,1,0:T(8,128)(2,1)} %dynamic-slice_bitcast_fusion.1), channel_id=1, source_target_pairs={{0,1},{1,0},{2,3},{3,2},{4,5},{5,4},{6,7},{7,6},{8,9},{9,8},{10,11... | collective-permute-start | bytes 6291464 | tf_op jit(solution)/shard_map/ppermute | solution.py:1366
  287.8 3.6 copy-start.6
  294.5 94.2 %collective-permute-start.4 = (bf16[256,2048]{1,0:T(8,128)(2,1)}, bf16[256,2048]{1,0:T(8,128)(2,1)}, u32[]{:S(2)}, u32[]{:S(2)}) collective-permute-start(bf16[256,2048]{1,0:T(8,128)(2,1)} %get-tuple-element.166), channel_id=1, source_target_pairs={{0,6},{1,7},{2,4},{3,5},{4,2},{5,3},{6,0},{7,1},{8,14},{9,15},{10,... | collective-permute-start | bytes 3145736 | tf_op jit(solution)/shard_map/ppermute | solution.py:1366
  296.7 92.0 %collective-permute-start.3 = (bf16[256,2048]{1,0:T(8,128)(2,1)}, bf16[256,2048]{1,0:T(8,128)(2,1)}, u32[]{:S(2)}, u32[]{:S(2)}) collective-permute-start(bf16[256,2048]{1,0:T(8,128)(2,1)} %get-tuple-element.167), channel_id=1, source_target_pairs={{0,4},{1,5},{2,6},{3,7},{4,0},{5,1},{6,2},{7,3},{8,12},{9,13},{10,... | collective-permute-start | bytes 3145736 | tf_op jit(solution)/shard_map/ppermute | solution.py:1366
  297.5 91.3 %collective-permute-start.2 = (bf16[256,2048]{1,0:T(8,128)(2,1)}, bf16[256,2048]{1,0:T(8,128)(2,1)}, u32[]{:S(2)}, u32[]{:S(2)}) collective-permute-start(bf16[256,2048]{1,0:T(8,128)(2,1)} %get-tuple-element.168), channel_id=1, source_target_pairs={{0,2},{1,3},{2,0},{3,1},{4,6},{5,7},{6,4},{7,5},{8,10},{9,11},{10,... | collective-permute-start | bytes 3145736 | tf_op jit(solution)/shard_map/ppermute | solution.py:1366
  388.7 2.6 copy-start.9
  391.3 1.4 copy-start
  392.9 27.2 %collective-permute-start.7 = (bf16[64,2048]{1,0:T(8,128)(2,1)S(1)}, bf16[64,2048]{1,0:T(8,128)(2,1)S(1)}, u32[]{:S(2)}, u32[]{:S(2)}) collective-permute-start(bf16[64,2048]{1,0:T(8,128)(2,1)S(1)} %get-tuple-element.176), channel_id=1, source_target_pairs={{0,24},{8,16},{16,8},{24,0},{1,25},{9,17},{17,9},{25,1},{2,26},{10... | collective-permute-start | bytes 786440 | tf_op jit(solution)/shard_map/ppermute | solution.py:1366
  395.9 24.3 %collective-permute-start.6 = (bf16[64,2048]{1,0:T(8,128)(2,1)S(1)}, bf16[64,2048]{1,0:T(8,128)(2,1)S(1)}, u32[]{:S(2)}, u32[]{:S(2)}) collective-permute-start(bf16[64,2048]{1,0:T(8,128)(2,1)S(1)} %get-tuple-element.177), channel_id=1, source_target_pairs={{0,16},{8,24},{16,0},{24,8},{1,17},{9,25},{17,1},{25,9},{2,18},{10... | collective-permute-start | bytes 786440 | tf_op jit(solution)/shard_map/ppermute | solution.py:1366
  395.9 24.3 %collective-permute-start.5 = (bf16[64,2048]{1,0:T(8,128)(2,1)S(1)}, bf16[64,2048]{1,0:T(8,128)(2,1)S(1)}, u32[]{:S(2)}, u32[]{:S(2)}) collective-permute-start(bf16[64,2048]{1,0:T(8,128)(2,1)S(1)} %get-tuple-element.178), channel_id=1, source_target_pairs={{0,8},{8,0},{16,24},{24,16},{1,9},{9,1},{17,25},{25,17},{2,10},{10... | collective-permute-start | bytes 786440 | tf_op jit(solution)/shard_map/ppermute | solution.py:1366
  420.2 9.1 %copy-start.12 = (bf16[128,8,2048]{2,1,0:T(8,128)(2,1)S(1)}, bf16[128,8,2048]{2,1,0:T(8,128)(2,1)}, u32[]{:S(2)}) copy-start(bf16[128,8,2048]{2,1,0:T(8,128)(2,1)} %get-tuple-element.109) | copy-start | bytes 12582916
  428.8 2.3 copy-start.4
  428.9 42.6 %copy-start.10 = (bf16[64,2048]{1,0:T(8,128)(2,1)}, bf16[64,2048]{1,0:T(8,128)(2,1)S(1)}, u32[]{:S(2)}) copy-start(bf16[64,2048]{1,0:T(8,128)(2,1)S(1)} %add_convert_fusion.rest_0_) | copy-start | bytes 786436
  429.2 7.9 %collective-permute-start.8 = (bf16[4,128,2048]{2,1,0:T(8,128)(2,1)S(1)}, bf16[4,128,2048]{2,1,0:T(8,128)(2,1)S(1)}, u32[]{:S(2)}, u32[]{:S(2)}) collective-permute-start(bf16[4,128,2048]{2,1,0:T(8,128)(2,1)S(1)} %dynamic-slice_bitcast_fusion), channel_id=1, source_target_pairs={{0,1},{1,0},{2,3},{3,2},{4,5},{5,4},{6,7},{7,6},{8,9},{9,8},{10,11... | collective-permute-start | bytes 6291464 | tf_op jit(solution)/shard_map/ppermute | solution.py:1366
  438.9 32.6 %collective-permute-start.11 = (bf16[128,2048]{1,0:T(8,128)(2,1)S(1)}, bf16[128,2048]{1,0:T(8,128)(2,1)}, u32[]{:S(2)}, u32[]{:S(2)}) collective-permute-start(bf16[128,2048]{1,0:T(8,128)(2,1)S(1)} %get-tuple-element.170), channel_id=1, source_target_pairs={{0,6},{1,7},{2,4},{3,5},{4,2},{5,3},{6,0},{7,1},{8,14},{9,15},{10,... | collective-permute-start | bytes 1572872 | tf_op jit(solution)/shard_map/ppermute | solution.py:1366
  441.1 32.0 %collective-permute-start.10 = (bf16[128,2048]{1,0:T(8,128)(2,1)S(1)}, bf16[128,2048]{1,0:T(8,128)(2,1)}, u32[]{:S(2)}, u32[]{:S(2)}) collective-permute-start(bf16[128,2048]{1,0:T(8,128)(2,1)S(1)} %get-tuple-element.171), channel_id=1, source_target_pairs={{0,4},{1,5},{2,6},{3,7},{4,0},{5,1},{6,2},{7,3},{8,12},{9,13},{10,... | collective-permute-start | bytes 1572872 | tf_op jit(solution)/shard_map/ppermute | solution.py:1366
  441.8 31.3 %collective-permute-start.9 = (bf16[128,2048]{1,0:T(8,128)(2,1)S(1)}, bf16[128,2048]{1,0:T(8,128)(2,1)}, u32[]{:S(2)}, u32[]{:S(2)}) collective-permute-start(bf16[128,2048]{1,0:T(8,128)(2,1)S(1)} %get-tuple-element.172), channel_id=1, source_target_pairs={{0,2},{1,3},{2,0},{3,1},{4,6},{5,7},{6,4},{7,5},{8,10},{9,11},{10,... | collective-permute-start | bytes 1572872 | tf_op jit(solution)/shard_map/ppermute | solution.py:1366
  442.4 66.0 %collective-permute-start.14 = (bf16[64,2048]{1,0:T(8,128)(2,1)S(1)}, bf16[64,2048]{1,0:T(8,128)(2,1)}, u32[]{:S(2)}, u32[]{:S(2)}) collective-permute-start(bf16[64,2048]{1,0:T(8,128)(2,1)S(1)} %add_convert_fusion.rest_0_), channel_id=1, source_target_pairs={{0,24},{8,16},{16,8},{24,0},{1,25},{9,17},{17,9},{25,1},{2,26},{10... | collective-permute-start | bytes 786440 | tf_op jit(solution)/shard_map/ppermute | solution.py:1366
  445.2 63.1 %collective-permute-start.13 = (bf16[64,2048]{1,0:T(8,128)(2,1)S(1)}, bf16[64,2048]{1,0:T(8,128)(2,1)}, u32[]{:S(2)}, u32[]{:S(2)}) collective-permute-start(bf16[64,2048]{1,0:T(8,128)(2,1)S(1)} %add_convert_fusion.rest_0_), channel_id=1, source_target_pairs={{0,16},{8,24},{16,0},{24,8},{1,17},{9,25},{17,1},{25,9},{2,18},{10... | collective-permute-start | bytes 786440 | tf_op jit(solution)/shard_map/ppermute | solution.py:1366
  471.5 36.8 %collective-permute-start.12 = (bf16[64,2048]{1,0:T(8,128)(2,1)S(1)}, bf16[64,2048]{1,0:T(8,128)(2,1)S(1)}, u32[]{:S(2)}, u32[]{:S(2)}) collective-permute-start(bf16[64,2048]{1,0:T(8,128)(2,1)S(1)} %add_convert_fusion.rest_0_), channel_id=1, source_target_pairs={{0,8},{8,0},{16,24},{24,16},{1,9},{9,1},{17,25},{25,17},{2,10},{10... | collective-permute-start | bytes 786440 | tf_op jit(solution)/shard_map/ppermute | solution.py:1366
  508.3 0.7 copy-start.11

commit v5 on v4

--- a/solution.py
+++ b/solution.py
@@ -210,7 +210,7 @@
     )(mixed, grad, grad, prompt, piece, prompt_cot, piece_cot, halo, gain)
 
 
-def front_kernel(mix_ref, fw_ref, fb_ref, sel_ref, act_ref, bend_ref, proj_ref):
+def front_kernel(mix_ref, fw_ref, fb_ref, sel_ref, act_ref, bend_ref, proj_ref, low_scr):
     j = pl.program_id(0)
     steps = act_ref.shape[0]
     chunk = 16
@@ -231,12 +231,12 @@
         act = v * sig
         act_ref[pl.ds(t, chunk)] = act
         bend_ref[pl.ds(t, chunk)] = (sig + act * (1.0 - sig)).astype(bf16)
-        low = act.reshape(chunk * SEQS, act.shape[-1]).astype(bf16)
         r = pl.multiple_of(t * SEQS, chunk * SEQS)
-        proj_ref[pl.ds(r, chunk * SEQS), :] += jnp.dot(low, sel_ref[...], preferred_element_type=f32)
+        low_scr[pl.ds(r, chunk * SEQS), :] = act.reshape(chunk * SEQS, act.shape[-1]).astype(bf16)
         return 0
 
     lax.fori_loop(0, steps // chunk, step, 0)
+    proj_ref[...] += jnp.dot(low_scr[...], sel_ref[...], preferred_element_type=f32)
 
 
 def front(mixture, fw, fb, select_pad, steps):
@@ -260,6 +260,7 @@
             jax.ShapeDtypeStruct((channels // WIDE, steps, SEQS, WIDE), bf16),
             jax.ShapeDtypeStruct((steps * SEQS, LANES), f32),
         ],
+        scratch_shapes=[pltpu.VMEM((steps * SEQS, WIDE), bf16)],
         compiler_params=params(),
         cost_estimate=cost(16),
         name="front",
@@ -343,13 +344,12 @@
 
     chunk = 8
     sbias = sbias_ref[0:1, :]
+    pre = jnp.dot(proj_ref[...].astype(bf16), stepw_ref[...], preferred_element_type=f32)
+    time_scr[...] = pre.reshape(steps, SEQS, WIDE)
 
     def prep(i, total):
         t = i * chunk
-        r = pl.multiple_of(t * SEQS, chunk * SEQS)
-        rank = proj_ref[pl.ds(r, chunk * SEQS), :].astype(bf16)
-        pre = jnp.dot(rank, stepw_ref[...], preferred_element_type=f32).reshape(chunk, SEQS, WIDE)
-        pre = pre + sbias[None]
+        pre = time_scr[pl.ds(t, chunk)] + sbias[None]
         small = jnp.exp2(jnp.abs(pre) * -LOG2E)
         one = 1.0 + small
         inverse = 1.0 / one
@@ -872,7 +872,7 @@
 def filter_back_kernel(
     mix_ref, act_ref, bend_ref, act_grad_ref, projg_ref, projg_t_ref, sel_ref, fw_ref,
     mixgrad_ref, selg_ref, fwg_ref, fbg_ref,
-    dv_scr,
+    dv_scr, more_scr,
 ):
     steps = act_ref.shape[0]
     chunk = 16
@@ -881,12 +881,13 @@
     dv_scr[0:HALO] = zero
     dv_scr[steps + HALO :] = zero
 
+    more = contract_cols(projg_ref[...], sel_ref[...])
+    more_scr[...] = more.reshape(steps, SEQS, WIDE)
+
     def step(i, sums):
         t = i * chunk
         x = mix_ref[pl.ds(t, chunk + HALO)].astype(f32)
-        r = pl.multiple_of(t * SEQS, chunk * SEQS)
-        more = contract_cols(projg_ref[pl.ds(r, chunk * SEQS), :], sel_ref[...])
-        total = act_grad_ref[pl.ds(t, chunk)] + more.reshape(chunk, SEQS, WIDE)
+        total = act_grad_ref[pl.ds(t, chunk)] + more_scr[pl.ds(t, chunk)]
         dv = total * bend_ref[pl.ds(t, chunk)].astype(f32)
         dv_scr[pl.ds(t + HALO, chunk)] = dv
         new = [sums[0] + jnp.sum(dv, axis=0)]
@@ -950,7 +951,10 @@
             jax.ShapeDtypeStruct((KERNEL, channels), f32),
             jax.ShapeDtypeStruct((1, channels), f32),
         ],
-        scratch_shapes=[pltpu.VMEM((steps + 2 * HALO, SEQS, WIDE), f32)],
+        scratch_shapes=[
+            pltpu.VMEM((steps + 2 * HALO, SEQS, WIDE), f32),
+            pltpu.VMEM((steps, SEQS, WIDE), f32),
+        ],
         compiler_params=params(),
         cost_estimate=cost(20),
         name="filter_back",

time: 514 us -> 497 us (0.967)
  Pallas kernels: 414 us -> 394 us
    pallas_call x1, Pallas kernels: 61.6 us -> 50.4 us  [piece(): pl.pallas_call(piece_kernel, grid=(grid,), in_specs=[pl.BlockSpec((steps...]
    pallas_call x1, Pallas kernels: 16.5 us -> 11.3 us  [front(): pl.pallas_call(front_kernel, grid=(channels // WIDE,), in_specs=[pl.Block...]
  transfers between devices with their start and end apart: 15 -> 15, of which waited for: 0 -> 1; matrix products, arithmetic and copies ran while one was open for 5% -> 5% of each run, Pallas kernels for 34% -> 34%
where the time goes in v5:
time: 497 us; the launch traced here: 495 us
  Pallas kernels  394 us (79%)
  local copies, waits for them, and re-layouts  32.1 us (6%)
  matrix products  32 us (6%)
  starting transfers between devices  17 us (3%)
  other arithmetic  15.6 us (3%)
    pallas_call x1, Pallas kernels, backward(): pl.pallas_call(backward_kernel, grid=(grid,), in_specs=[pl.BlockSpec((ste...  90.9 us
    pallas_call x1, Pallas kernels, piece(): pl.pallas_call(piece_kernel, grid=(grid,), in_specs=[pl.BlockSpec((steps...  50.4 us
    pallas_call x1, Pallas kernels, gather(): pl.pallas_call(gather_kernel, in_specs=[vmem] * 4, out_specs=[hbm] * 4, o...  50.4 us
    pallas_call x1, Pallas kernels, forward(): pl.pallas_call(forward_kernel, grid=(grid,), in_specs=[pl.BlockSpec((step...  49.1 us
    pallas_call x4, Pallas kernels, product(): pl.pallas_call(functools.partial(product_kernel, across), grid=(columns /...  42 us
    pallas_call x1, Pallas kernels, tail(): pl.pallas_call(tail_kernel, in_specs=[pl.BlockSpec(memory_space=pltpu.SME...  35.3 us
    dot_general x3, matrix products, contract_rows(): lax.dot_general(left_side, right_side, (((0,), (0,)), ((), ())), preferre...  25.9 us
    pallas_call x1, Pallas kernels, chain(): pl.pallas_call(chain_kernel, in_specs=[pl.BlockSpec(memory_space=pltpu.SM...  24.4 us
  transfers between devices with their start and end apart: 15, of which 1 were waited for; matrix products, arithmetic and copies ran while one was open for 5% of the time, Pallas kernels for 34%

profile of v5, /device:TPU:0, one launch (start us, length us, event | category | flops | bytes accessed | tf_op | source)
XLA Modules:
  0.0 495.0 jit_solution(3515287538360897727)
XLA Ops:
  10.7 50.4 %gather.7 = (bf16[1024,256]{1,0:T(8,128)(2,1)}, bf16[2048,128]{1,0:T(8,128)(2,1)}, bf16[2048,1024]{1,0:T(8,128)(2,1)}, bf16[1024,4096]{1,0:T(8,128)(2,1)}) custom-call(bf16[128,256]{1,0:T(8,128)(2,1)} %pad.21.rows_ref, bf16[256,128]{1,0:T(8,128)(2,1)} %fusion.14.select_ref, bf16[256,1024]{1,0:T(8,128)(2,1)} %out_ref.1, bf16[128,4096]{1,0:T(8,128)(2,1)} %in_ref.1), custom_call_target="tpu_custom_call" | custom-call | flops 54999998464 | tf_op jit(solution)/shard_map/gather/pallas_call | solution.py:1127
  67.9 8.2 %prepare.1 = (bf16[1056,1024]{1,0:T(8,128)(2,1)}, bf16[1024,1024]{1,0:T(8,128)(2,1)}) custom-call(bf16[4,128,1024]{2,1,0:T(8,128)(2,1)} %prompt_ref.3, bf16[4,128,1024]{2,1,0:T(8,128)(2,1)} %piece_ref.3, bf16[4,128,1024]{2,1,0:T(8,128)(2,1)} %prompt_cot_ref.3, bf16[4,128,1024]{2,1,0:T(8,128)(2,1)} %piece_cot_ref.3, f32[32,1024]{1,0:T(8,128)} %bitcast_convert_fusion.halo_ref, ...), custom_call_target="tpu_custom_call" | custom-call | flops 5000000000 | tf_op jit(solution)/shard_map/prepare/pallas_call | solution.py:122
  76.1 8.5 %product.4 = bf16[8,1056,256]{2,1,0:T(8,128)(2,1)} custom-call(bf16[1056,1024]{1,0:T(8,128)(2,1)} %get-tuple-element.91.refs_0_, bf16[1024,4096]{1,0:T(8,128)(2,1)} %get-tuple-element.92.refs_1_.refs_2_), custom_call_target="tpu_custom_call" | custom-call | flops 10000000 | tf_op jit(solution)/shard_map/product/pallas_call | solution.py:75
  84.6 9.3 %product.5 = f32[8,1056,256]{2,1,0:T(8,128)} custom-call(bf16[1056,1024]{1,0:T(8,128)(2,1)} %get-tuple-element.91.refs_0_, bf16[1024,4096]{1,0:T(8,128)(2,1)} %get-tuple-element.92.refs_1_.refs_2_), custom_call_target="tpu_custom_call" | custom-call | flops 10000000 | tf_op jit(solution)/shard_map/product/pallas_call | solution.py:75
  98.8 9.2 %product.6 = f32[8,1024,256]{2,1,0:T(8,128)} custom-call(bf16[1024,1024]{1,0:T(8,128)(2,1)} %get-tuple-element.97.refs_0_, bf16[2048,1024]{1,0:T(8,128)(2,1)} %get-tuple-element.98.refs_1_), custom_call_target="tpu_custom_call" | custom-call | flops 10000000 | tf_op jit(solution)/shard_map/product/pallas_call | solution.py:75
  107.9 11.3 %front.1 = (f32[8,128,8,256]{3,2,1,0:T(8,128)}, bf16[8,128,8,256]{3,2,1,0:T(8,128)(2,1)}, f32[1024,128]{1,0:T(8,128)}) custom-call(bf16[8,132,8,256]{3,2,1,0:T(8,128)(2,1)} %bitcast.108, f32[4,2048]{1,0:T(4,128)} %bitcast.124, f32[1,2048]{1,0:T(1,128)} %bitcast.129, bf16[2048,128]{1,0:T(8,128)(2,1)} %get-tuple-element.93.sel_ref), custom_call_target="tpu_custom_call" | custom-call | flops 16000000000 | tf_op jit(solution)/shard_map/front/pallas_call | solution.py:244
  119.2 50.4 %piece.1 = (f32[8,128,8,256]{3,2,1,0:T(8,128)}, bf16[8,128,8,256]{3,2,1,0:T(8,128)(2,1)}, f32[8,128,8,256]{3,2,1,0:T(8,128)}, bf16[8,128,8,256]{3,2,1,0:T(8,128)...) custom-call(f32[1024,128]{1,0:T(8,128)} %get-tuple-element.96.proj_r, ...), custom_call_target="tpu_custom_call" | custom-call | flops 60000002048 | tf_op jit(solution)/shard_map/piece/pallas_call | solution.py:445
  169.6 24.4 %chain.1 = (f32[8,16,2048]{2,1,0:T(8,128)}, f32[8,16,2048]{2,1,0:T(8,128)}) custom-call(f32[4,4]{1,0:T(4,128)} %fusion.20.one_hot_ref, f32[4,16,2048]{2,1,0:T(8,128)} %get-tuple-element.102.ahead_ref, f32[8,16,2048]{2,1,0:T(8,128)} %get-tuple-element.103.behind_ref, f32[8,2048]{1,0:T(8,128)} %get-tuple-element.104.time_ref, ...), custom_call_target="tpu_custom_call" | custom-call | flops 24999999488 | tf_op jit(solution)/shard_map/chain/pallas_call | solution.py:592
  194.0 49.1 %forward_scan.1 = (bf16[128,8,2048]{2,1,0:T(8,128)(2,1)}, bf16[8,2,129,8,16,128]{5,4,3,2,1,0:T(8,128)(2,1)}, bf16[132,8,2048]{2,1,0:T(8,128)(2,1)}, f32[1,2048]{1,0:T(1,128)}) custom-call(f32[1024,128]{1,0:T(8,128)} %get-tuple-element.96.proj_ref, f32[8,128,8,256]{3,2,1,0:T(8,128)} %get-tuple-element.99.dt_ref, ...), custom_call_target="tpu_custom_call" | custom-call | flops 49999998976 | tf_op jit(solution)/shard_map/forward_scan/pallas_call | solution.py:672
  243.1 9.5 %fusion.7 = bf16[2048,1024]{1,0:T(8,128)(2,1)} fusion(bf16[1024,1024]{1,0:T(8,128)(2,1)} %get-tuple-element.97.refs_0_, bf16[128,8,2048]{2,1,0:T(8,128)(2,1)} %get-tuple-element.109), kind=kOutput, calls=%fused_computation.12 | convolution fusion | flops 4297064448 | bytes 10485760 | tf_op jit(solution)/shard_map/dot_general | solution.py:1358
  252.6 3.2 dynamic-slice_bitcast_fusion.2
  256.8 8.1 %convolution_convert_fusion.1 = bf16[1024,2048]{1,0:T(8,128)(2,1)S(1)} fusion(bf16[1056,1024]{1,0:T(8,128)(2,1)S(1)} %copy-done.1, bf16[132,8,2048]{2,1,0:T(8,128)(2,1)} %get-tuple-element.110), kind=kOutput, calls=%fused_computation.14 | convolution fusion | flops 4431282176 | bytes 10682368 | tf_op jit(solution)/shard_map/dot_general | solution.py:1358
  265.0 2.0 copy-done.5
  271.4 3.4 fusion.2
  276.4 1.7 dynamic-slice_bitcast_fusion.3
  278.1 2.2 collective-permute-start.4
  281.6 90.9 %backward_scan.1 = (f32[8,128,8,256]{3,2,1,0:T(8,128)}, f32[64,2048]{1,0:T(8,128)}, f32[1,2048]{1,0:T(1,128)}, f32[16,2048]{1,0:T(8,128)}, bf16[1024,128]{1,0:T(8,128)(2,1)}) custom-call(f32[1024,128]{1,0:T(8,128)} %get-tuple-element.96.proj_ref, f32[8,128,8,256]{3,2,1,0:T(8,128)} %get-tuple-element.99.dt_ref, ...), custom_call_target="tpu_custom_call" | custom-call | flops 89999998976 | tf_op jit(solution)/shard_map/backward_scan/pallas_call | solution.py:825
  372.6 2.5 convert_add_fusion.3
  376.7 2.9 collective-permute-start.7
  379.7 1.5 collective-permute-start.5
  381.2 17.0 %filter_back.1 = (bf16[132,8,2048]{2,1,0:T(8,128)(2,1)}, f32[128,2048]{1,0:T(8,128)}, f32[4,2048]{1,0:T(4,128)}, f32[1,2048]{1,0:T(1,128)}) custom-call(bf16[8,132,8,256]{3,2,1,0:T(8,128)(2,1)} %bitcast.109, f32[8,128,8,256]{3,2,1,0:T(8,128)} %get-tuple-element.94.act_ref, bf16[8,128,8,256]{3,2,1,0:T(8,128)(2,1)} %get-tuple-element.95.bend_ref, ...), custom_call_target="tpu_custom_call" | custom-call | flops 20000000000 | tf_op jit(solution)/shard_map/filter_back/pallas_call | solution.py:929
  399.3 3.1 collective-permute-done.6
  402.4 8.3 %convolution_convert_fusion = bf16[1024,2048]{1,0:T(8,128)(2,1)S(1)} fusion(bf16[1056,1024]{1,0:T(8,128)(2,1)} %get-tuple-element.91.refs_0_, bf16[132,8,2048]{2,1,0:T(8,128)(2,1)} %get-tuple-element.124), kind=kOutput, calls=%fused_computation.13 | convolution fusion | flops 4431282176 | bytes 10682368 | tf_op jit(solution)/shard_map/dot_general | solution.py:1358
  411.2 1.8 copy-done.4
  413.0 6.1 %fusion.3.mixed_ref = f32[1024,1024]{1,0:T(8,128)} fusion(bf16[2048,1024]{1,0:T(8,128)(2,1)S(1)} %copy-done.4, bf16[128,8,2048]{2,1,0:T(8,128)(2,1)S(1)} %copy-done.12), kind=kOutput, calls=%fused_computation.8 | convolution fusion | flops 4294967296 | bytes 12582912 | tf_op jit(solution)/shard_map/dot_general | solution.py:1531
  420.8 2.2 collective-permute-start.11
  424.3 2.6 collective-permute-start.14
  427.0 15.0 %product.7.grad_ref.grad_halo_ref = f32[1056,1024]{1,0:T(8,128)} custom-call(bf16[1056,2048]{1,0:T(8,128)(2,1)} %bitcast.111, bf16[1056,2048]{1,0:T(8,128)(2,1)} %bitcast.110, bf16[1024,4096]{1,0:T(8,128)(2,1)} %get-tuple-element.92.refs_1_.refs_2_), custom_call_target="tpu_custom_call" | custom-call | flops 10000000 | tf_op jit(solution)/shard_map/product/pallas_call | solution.py:75
  441.9 11.5 %finish.1 = (bf16[4,128,1024]{2,1,0:T(8,128)(2,1)}, bf16[4,128,1024]{2,1,0:T(8,128)(2,1)}, f32[4,128,1024]{2,1,0:T(8,128)}, f32[4,128,1024]{2,1,0:T(8,128)}, f32[32,1024]{1,0:T(8,128)}, /*index=5*/f32[1,1024]{1,0:T(1,128)}) custom-call(f32[1024,1024]{1,0:T(8,128)} %fusion.3.mixed_ref, f32[1056,1024]{1,0:T(8,128)} %product.7.grad_ref.grad_halo_ref, ...), custom_call_target="tpu_custom_call" | custom-call | flops 10000000 | tf_op jit(solution)/shard_map/finish/pallas_call | solution.py:188
  453.5 1.8 collective-permute-start.12
  455.3 35.3 %tail.1 = (bf16[128,2048]{1,0:T(8,128)(2,1)}, bf16[192,256]{1,0:T(8,128)(2,1)}, f32[16,1024]{1,0:T(8,128)}) custom-call(f32[4,4]{1,0:T(4,128)} %fusion.20.one_hot_ref, bf16[128,2048]{1,0:T(8,128)(2,1)} %get-tuple-element.136.b0, bf16[128,2048]{1,0:T(8,128)(2,1)} %collective-permute-done.9.b1, bf16[128,2048]{1,0:T(8,128)(2,1)} %collective-permute-done.10.b2, ...), custom_call_target="tpu_custom_call" | custom-call | flops 30000001024 | tf_op jit(solution)/shard_map/tail/pallas_call | solution.py:1277
  491.3 3.5 deliver.1
  (104 shorter events, 36.7 us)
Async XLA Ops:
  84.6 12.7 %copy-start.8 = (bf16[2048,128]{1,0:T(8,128)(2,1)S(1)}, bf16[2048,128]{1,0:T(8,128)(2,1)}, u32[]{:S(2)}) copy-start(bf16[2048,128]{1,0:T(8,128)(2,1)} %get-tuple-element.93.sel_ref) | copy-start | bytes 1572868
  95.4 0.8 copy-start.2
  252.6 4.2 copy-start.1
  255.8 15.6 %collective-permute-start = (bf16[4,256,1024]{2,1,0:T(8,128)(2,1)}, bf16[4,256,1024]{2,1,0:T(8,128)(2,1)}, u32[]{:S(2)}, u32[]{:S(2)}) collective-permute-start(bf16[4,256,1024]{2,1,0:T(8,128)(2,1)} %dynamic-slice_bitcast_fusion.2), channel_id=1, source_target_pairs={{0,1},{1,0},{2,3},{3,2},{4,5},{5,4},{6,7},{7,6},{8,9},{9,8},{10,11... | collective-permute-start | bytes 6291464 | tf_op jit(solution)/shard_map/ppermute | solution.py:1370
  265.0 2.0 copy-start.5
  265.0 3.4 copy-start.7
  265.0 4.3 copy-start.3
  268.4 6.6 %collective-permute-start.1 = (bf16[4,128,2048]{2,1,0:T(8,128)(2,1)}, bf16[4,128,2048]{2,1,0:T(8,128)(2,1)S(1)}, u32[]{:S(2)}, u32[]{:S(2)}) collective-permute-start(bf16[4,128,2048]{2,1,0:T(8,128)(2,1)} %dynamic-slice_bitcast_fusion.1), channel_id=1, source_target_pairs={{0,1},{1,0},{2,3},{3,2},{4,5},{5,4},{6,7},{7,6},{8,9},{9,8},{10,11... | collective-permute-start | bytes 6291464 | tf_op jit(solution)/shard_map/ppermute | solution.py:1370
  271.4 3.6 copy-start.6
  278.1 94.4 %collective-permute-start.4 = (bf16[256,2048]{1,0:T(8,128)(2,1)}, bf16[256,2048]{1,0:T(8,128)(2,1)}, u32[]{:S(2)}, u32[]{:S(2)}) collective-permute-start(bf16[256,2048]{1,0:T(8,128)(2,1)} %get-tuple-element.166), channel_id=1, source_target_pairs={{0,6},{1,7},{2,4},{3,5},{4,2},{5,3},{6,0},{7,1},{8,14},{9,15},{10,... | collective-permute-start | bytes 3145736 | tf_op jit(solution)/shard_map/ppermute | solution.py:1370
  280.3 92.2 %collective-permute-start.3 = (bf16[256,2048]{1,0:T(8,128)(2,1)}, bf16[256,2048]{1,0:T(8,128)(2,1)}, u32[]{:S(2)}, u32[]{:S(2)}) collective-permute-start(bf16[256,2048]{1,0:T(8,128)(2,1)} %get-tuple-element.167), channel_id=1, source_target_pairs={{0,4},{1,5},{2,6},{3,7},{4,0},{5,1},{6,2},{7,3},{8,12},{9,13},{10,... | collective-permute-start | bytes 3145736 | tf_op jit(solution)/shard_map/ppermute | solution.py:1370
  281.0 91.5 %collective-permute-start.2 = (bf16[256,2048]{1,0:T(8,128)(2,1)}, bf16[256,2048]{1,0:T(8,128)(2,1)}, u32[]{:S(2)}, u32[]{:S(2)}) collective-permute-start(bf16[256,2048]{1,0:T(8,128)(2,1)} %get-tuple-element.168), channel_id=1, source_target_pairs={{0,2},{1,3},{2,0},{3,1},{4,6},{5,7},{6,4},{7,5},{8,10},{9,11},{10,... | collective-permute-start | bytes 3145736 | tf_op jit(solution)/shard_map/ppermute | solution.py:1370
  372.5 2.6 copy-start.9
  375.1 1.4 copy-start
  376.7 22.5 %collective-permute-start.7 = (bf16[64,2048]{1,0:T(8,128)(2,1)S(1)}, bf16[64,2048]{1,0:T(8,128)(2,1)S(1)}, u32[]{:S(2)}, u32[]{:S(2)}) collective-permute-start(bf16[64,2048]{1,0:T(8,128)(2,1)S(1)} %get-tuple-element.176), channel_id=1, source_target_pairs={{0,24},{8,16},{16,8},{24,0},{1,25},{9,17},{17,9},{25,1},{2,26},{10... | collective-permute-start | bytes 786440 | tf_op jit(solution)/shard_map/ppermute | solution.py:1370
  379.7 22.7 %collective-permute-start.6 = (bf16[64,2048]{1,0:T(8,128)(2,1)S(1)}, bf16[64,2048]{1,0:T(8,128)(2,1)S(1)}, u32[]{:S(2)}, u32[]{:S(2)}) collective-permute-start(bf16[64,2048]{1,0:T(8,128)(2,1)S(1)} %get-tuple-element.177), channel_id=1, source_target_pairs={{0,16},{8,24},{16,0},{24,8},{1,17},{9,25},{17,1},{25,9},{2,18},{10... | collective-permute-start | bytes 786440 | tf_op jit(solution)/shard_map/ppermute | solution.py:1370
  379.7 22.7 %collective-permute-start.5 = (bf16[64,2048]{1,0:T(8,128)(2,1)S(1)}, bf16[64,2048]{1,0:T(8,128)(2,1)S(1)}, u32[]{:S(2)}, u32[]{:S(2)}) collective-permute-start(bf16[64,2048]{1,0:T(8,128)(2,1)S(1)} %get-tuple-element.178), channel_id=1, source_target_pairs={{0,8},{8,0},{16,24},{24,16},{1,9},{9,1},{17,25},{25,17},{2,10},{10... | collective-permute-start | bytes 786440 | tf_op jit(solution)/shard_map/ppermute | solution.py:1370
  402.4 8.8 %copy-start.12 = (bf16[128,8,2048]{2,1,0:T(8,128)(2,1)S(1)}, bf16[128,8,2048]{2,1,0:T(8,128)(2,1)}, u32[]{:S(2)}) copy-start(bf16[128,8,2048]{2,1,0:T(8,128)(2,1)} %get-tuple-element.109) | copy-start | bytes 12582916
  410.7 2.3 copy-start.4
  410.9 42.6 %copy-start.10 = (bf16[64,2048]{1,0:T(8,128)(2,1)}, bf16[64,2048]{1,0:T(8,128)(2,1)S(1)}, u32[]{:S(2)}) copy-start(bf16[64,2048]{1,0:T(8,128)(2,1)S(1)} %add_convert_fusion.rest_0_) | copy-start | bytes 786436
  411.1 7.9 %collective-permute-start.8 = (bf16[4,128,2048]{2,1,0:T(8,128)(2,1)S(1)}, bf16[4,128,2048]{2,1,0:T(8,128)(2,1)S(1)}, u32[]{:S(2)}, u32[]{:S(2)}) collective-permute-start(bf16[4,128,2048]{2,1,0:T(8,128)(2,1)S(1)} %dynamic-slice_bitcast_fusion), channel_id=1, source_target_pairs={{0,1},{1,0},{2,3},{3,2},{4,5},{5,4},{6,7},{7,6},{8,9},{9,8},{10,11... | collective-permute-start | bytes 6291464 | tf_op jit(solution)/shard_map/ppermute | solution.py:1370
  420.8 32.7 %collective-permute-start.11 = (bf16[128,2048]{1,0:T(8,128)(2,1)S(1)}, bf16[128,2048]{1,0:T(8,128)(2,1)}, u32[]{:S(2)}, u32[]{:S(2)}) collective-permute-start(bf16[128,2048]{1,0:T(8,128)(2,1)S(1)} %get-tuple-element.170), channel_id=1, source_target_pairs={{0,6},{1,7},{2,4},{3,5},{4,2},{5,3},{6,0},{7,1},{8,14},{9,15},{10,... | collective-permute-start | bytes 1572872 | tf_op jit(solution)/shard_map/ppermute | solution.py:1370
  423.0 32.3 %collective-permute-start.10 = (bf16[128,2048]{1,0:T(8,128)(2,1)S(1)}, bf16[128,2048]{1,0:T(8,128)(2,1)}, u32[]{:S(2)}, u32[]{:S(2)}) collective-permute-start(bf16[128,2048]{1,0:T(8,128)(2,1)S(1)} %get-tuple-element.171), channel_id=1, source_target_pairs={{0,4},{1,5},{2,6},{3,7},{4,0},{5,1},{6,2},{7,3},{8,12},{9,13},{10,... | collective-permute-start | bytes 1572872 | tf_op jit(solution)/shard_map/ppermute | solution.py:1370
  423.8 31.6 %collective-permute-start.9 = (bf16[128,2048]{1,0:T(8,128)(2,1)S(1)}, bf16[128,2048]{1,0:T(8,128)(2,1)}, u32[]{:S(2)}, u32[]{:S(2)}) collective-permute-start(bf16[128,2048]{1,0:T(8,128)(2,1)S(1)} %get-tuple-element.172), channel_id=1, source_target_pairs={{0,2},{1,3},{2,0},{3,1},{4,6},{5,7},{6,4},{7,5},{8,10},{9,11},{10,... | collective-permute-start | bytes 1572872 | tf_op jit(solution)/shard_map/ppermute | solution.py:1370
  424.3 66.3 %collective-permute-start.14 = (bf16[64,2048]{1,0:T(8,128)(2,1)S(1)}, bf16[64,2048]{1,0:T(8,128)(2,1)}, u32[]{:S(2)}, u32[]{:S(2)}) collective-permute-start(bf16[64,2048]{1,0:T(8,128)(2,1)S(1)} %add_convert_fusion.rest_0_), channel_id=1, source_target_pairs={{0,24},{8,16},{16,8},{24,0},{1,25},{9,17},{17,9},{25,1},{2,26},{10... | collective-permute-start | bytes 786440 | tf_op jit(solution)/shard_map/ppermute | solution.py:1370
  427.0 63.6 %collective-permute-start.13 = (bf16[64,2048]{1,0:T(8,128)(2,1)S(1)}, bf16[64,2048]{1,0:T(8,128)(2,1)}, u32[]{:S(2)}, u32[]{:S(2)}) collective-permute-start(bf16[64,2048]{1,0:T(8,128)(2,1)S(1)} %add_convert_fusion.rest_0_), channel_id=1, source_target_pairs={{0,16},{8,24},{16,0},{24,8},{1,17},{9,25},{17,1},{25,9},{2,18},{10... | collective-permute-start | bytes 786440 | tf_op jit(solution)/shard_map/ppermute | solution.py:1370
  453.5 37.1 %collective-permute-start.12 = (bf16[64,2048]{1,0:T(8,128)(2,1)S(1)}, bf16[64,2048]{1,0:T(8,128)(2,1)S(1)}, u32[]{:S(2)}, u32[]{:S(2)}) collective-permute-start(bf16[64,2048]{1,0:T(8,128)(2,1)S(1)} %add_convert_fusion.rest_0_), channel_id=1, source_target_pairs={{0,8},{8,0},{16,24},{24,16},{1,9},{9,1},{17,25},{25,17},{2,10},{10... | collective-permute-start | bytes 786440 | tf_op jit(solution)/shard_map/ppermute | solution.py:1370
  490.6 0.7 copy-start.11

commit v6 on v5

--- a/solution.py
+++ b/solution.py
@@ -113,15 +113,16 @@
 
 
 CHUNK = 16
+PREPARE_CHUNK = 32
 
 
 def prepare(prompt, piece, prompt_cot, piece_cot, halo, gain):
     steps = prompt.shape[1]
-    part = pl.BlockSpec((SEQS // 2, CHUNK, D), lambda i: (0, i, 0))
+    part = pl.BlockSpec((SEQS // 2, PREPARE_CHUNK, D), lambda i: (0, i, 0))
     rows = steps * SEQS
     return pl.pallas_call(
         prepare_kernel,
-        grid=(steps // CHUNK,),
+        grid=(steps // PREPARE_CHUNK,),
         in_specs=[
             part, part, part, part,
             pl.BlockSpec((HALO * SEQS, D), lambda i: (0, 0)),
@@ -129,7 +130,7 @@
         ],
         out_specs=[
             pl.BlockSpec((HALO * SEQS + rows, D), lambda i: (0, 0)),
-            pl.BlockSpec((CHUNK * SEQS, D), lambda i: (i, 0)),
+            pl.BlockSpec((PREPARE_CHUNK * SEQS, D), lambda i: (i, 0)),
         ],
         out_shape=[
             jax.ShapeDtypeStruct((HALO * SEQS + rows, D), bf16),
@@ -356,7 +357,7 @@
         dt = jnp.maximum(pre, 0.0) + (jnp.log(one) + (small - (one - 1.0)) * inverse)
         dt_ref[pl.ds(t, chunk)] = dt
         sig_ref[pl.ds(t, chunk)] = jnp.where(pre >= 0.0, inverse, small * inverse).astype(bf16)
-        gate = gate_ref[pl.ds(t + HALO, chunk)]
+        gate = gate_ref[pl.ds(t + HALO, chunk)].astype(f32)
         gg = gg_ref[pl.ds(t, chunk)]
         sig = sigmoid(gate)
         silu = gate * sig
@@ -448,7 +449,7 @@
         in_specs=[
             pl.BlockSpec((steps * SEQS, LANES), lambda j: (0, 0)),
             flat,
-            pl.BlockSpec((None, steps + HALO, SEQS, WIDE), lambda j: (j, 0, 0, 0)),
+            pl.BlockSpec((None, steps + HALO, SEQS, WIDE), lambda j: (j + grid, 0, 0, 0)),
             flat,
             pl.BlockSpec((LANES, WIDE), lambda j: (0, j)),
             pl.BlockSpec((1, WIDE), lambda j: (0, j)),
@@ -1459,10 +1460,8 @@
     piece_cot = sequel_cotangent.reshape(-1, steps, D)
     scaled, cotangent = prepare(prompt_hidden, pieces, prompt_cotangent, piece_cot, halo, gain)
 
-    mixture = product([scaled], full_input, bf16, part=0, parts=2, tiled=True)
-    gate = product([scaled], full_input, f32, part=1, parts=2, tiled=True)
+    mixture = product([scaled], full_input, bf16, tiled=True)
     mixture = mixture.reshape(-1, steps + HALO, SEQS, WIDE)
-    gate = gate.reshape(-1, steps + HALO, SEQS, WIDE)
     gated_grad = product([cotangent], full_output, f32, across=True, tiled=True)
     gated_grad = gated_grad.reshape(-1, steps, SEQS, WIDE)
     act, bend, proj = front(mixture, fw, fb, select_pad, steps)
@@ -1470,7 +1469,7 @@
     lane = jnp.arange(2 * STATES * LANES)[None, :]
     select = (jnp.arange(LANES)[:, None] == RANK + lane // LANES).astype(bf16)
     dt, sig, yg, silu, slope, ahead, behind, total = piece(
-        proj, act, gate, gated_grad, step_pad, sbias, rate, select, groups
+        proj, act, mixture, gated_grad, step_pad, sbias, rate, select, groups
     )
 
     one_hot = (parents[:, None] == jnp.arange(PROMPTS, dtype=jnp.int32)[None, :]).astype(f32)

time: 497 us -> 491 us (0.988)
  Pallas kernels: 394 us -> 389 us
    pallas_call x4 -> x3, Pallas kernels: 42 us -> 38.8 us  [product(): pl.pallas_call(functools.partial(product_kernel, across), grid=(columns /...]
  transfers between devices with their start and end apart: 15 -> 15, of which waited for: 1 -> 1; matrix products, arithmetic and copies ran while one was open for 5% -> 5% of each run, Pallas kernels for 34% -> 35%
where the time goes in v6:
time: 491 us; the launch traced here: 490 us
  Pallas kernels  389 us (79%)
  local copies, waits for them, and re-layouts  32.1 us (7%)
  matrix products  31.9 us (6%)
  starting transfers between devices  17 us (3%)
  other arithmetic  15.6 us (3%)
    pallas_call x1, Pallas kernels, backward(): pl.pallas_call(backward_kernel, grid=(grid,), in_specs=[pl.BlockSpec((ste...  90.8 us
    pallas_call x1, Pallas kernels, piece(): pl.pallas_call(piece_kernel, grid=(grid,), in_specs=[pl.BlockSpec((steps...  50.4 us
    pallas_call x1, Pallas kernels, gather(): pl.pallas_call(gather_kernel, in_specs=[vmem] * 4, out_specs=[hbm] * 4, o...  50.4 us
    pallas_call x1, Pallas kernels, forward(): pl.pallas_call(forward_kernel, grid=(grid,), in_specs=[pl.BlockSpec((step...  49.1 us
    pallas_call x3, Pallas kernels, product(): pl.pallas_call(functools.partial(product_kernel, across), grid=(columns /...  38.8 us
    pallas_call x1, Pallas kernels, tail(): pl.pallas_call(tail_kernel, in_specs=[pl.BlockSpec(memory_space=pltpu.SME...  35.3 us
    dot_general x3, matrix products, contract_rows(): lax.dot_general(left_side, right_side, (((0,), (0,)), ((), ())), preferre...  25.9 us
    pallas_call x1, Pallas kernels, chain(): pl.pallas_call(chain_kernel, in_specs=[pl.BlockSpec(memory_space=pltpu.SM...  24.5 us
  transfers between devices with their start and end apart: 15, of which 1 were waited for; matrix products, arithmetic and copies ran while one was open for 5% of the time, Pallas kernels for 35%

profile of v6, /device:TPU:0, one launch (start us, length us, event | category | flops | bytes accessed | tf_op | source)
XLA Modules:
  0.0 489.9 jit_solution(15890742369970902172)
XLA Ops:
  6.2 1.5 concatenate.15
  10.7 50.4 %gather.7 = (bf16[1024,256]{1,0:T(8,128)(2,1)}, bf16[2048,128]{1,0:T(8,128)(2,1)}, bf16[2048,1024]{1,0:T(8,128)(2,1)}, bf16[1024,4096]{1,0:T(8,128)(2,1)}) custom-call(bf16[128,256]{1,0:T(8,128)(2,1)} %pad.21.rows_ref, bf16[256,128]{1,0:T(8,128)(2,1)} %fusion.14.select_ref, bf16[256,1024]{1,0:T(8,128)(2,1)} %out_ref.1, bf16[128,4096]{1,0:T(8,128)(2,1)} %in_ref.1), custom_call_target="tpu_custom_call" | custom-call | flops 54999998464 | tf_op jit(solution)/shard_map/gather/pallas_call | solution.py:1128
  72.8 6.5 %prepare.1 = (bf16[1056,1024]{1,0:T(8,128)(2,1)}, bf16[1024,1024]{1,0:T(8,128)(2,1)}) custom-call(bf16[4,128,1024]{2,1,0:T(8,128)(2,1)} %prompt_ref.3, bf16[4,128,1024]{2,1,0:T(8,128)(2,1)} %piece_ref.3, bf16[4,128,1024]{2,1,0:T(8,128)(2,1)} %prompt_cot_ref.3, bf16[4,128,1024]{2,1,0:T(8,128)(2,1)} %piece_cot_ref.3, f32[32,1024]{1,0:T(8,128)} %bitcast_convert_fusion.halo_ref, ...), custom_call_target="tpu_custom_call" | custom-call | flops 5000000000 | tf_op jit(solution)/shard_map/prepare/pallas_call | solution.py:123
  79.2 9.3 %product.4 = f32[8,1024,256]{2,1,0:T(8,128)} custom-call(bf16[1024,1024]{1,0:T(8,128)(2,1)} %get-tuple-element.97.refs_0_, bf16[2048,1024]{1,0:T(8,128)(2,1)} %get-tuple-element.98.refs_1_), custom_call_target="tpu_custom_call" | custom-call | flops 10000000 | tf_op jit(solution)/shard_map/product/pallas_call | solution.py:75
  88.5 14.5 %product.3 = bf16[16,1056,256]{2,1,0:T(8,128)(2,1)} custom-call(bf16[1056,1024]{1,0:T(8,128)(2,1)} %get-tuple-element.91.refs_0_, bf16[1024,4096]{1,0:T(8,128)(2,1)} %get-tuple-element.92.refs_1_.refs_2_), custom_call_target="tpu_custom_call" | custom-call | flops 10000000 | tf_op jit(solution)/shard_map/product/pallas_call | solution.py:75
  103.0 11.3 %front.1 = (f32[8,128,8,256]{3,2,1,0:T(8,128)}, bf16[8,128,8,256]{3,2,1,0:T(8,128)(2,1)}, f32[1024,128]{1,0:T(8,128)}) custom-call(bf16[16,132,8,256]{3,2,1,0:T(8,128)(2,1)} %bitcast.103, f32[4,2048]{1,0:T(4,128)} %bitcast.123, f32[1,2048]{1,0:T(1,128)} %bitcast.128, bf16[2048,128]{1,0:T(8,128)(2,1)} %get-tuple-element.93.sel_ref), custom_call_target="tpu_custom_call" | custom-call | flops 16000000000 | tf_op jit(solution)/shard_map/front/pallas_call | solution.py:245
  114.3 50.4 %piece.1 = (f32[8,128,8,256]{3,2,1,0:T(8,128)}, bf16[8,128,8,256]{3,2,1,0:T(8,128)(2,1)}, f32[8,128,8,256]{3,2,1,0:T(8,128)}, bf16[8,128,8,256]{3,2,1,0:T(8,128)...) custom-call(f32[1024,128]{1,0:T(8,128)} %get-tuple-element.96.proj_r, ...), custom_call_target="tpu_custom_call" | custom-call | flops 60000002048 | tf_op jit(solution)/shard_map/piece/pallas_call | solution.py:446
  164.7 24.5 %chain.1 = (f32[8,16,2048]{2,1,0:T(8,128)}, f32[8,16,2048]{2,1,0:T(8,128)}) custom-call(f32[4,4]{1,0:T(4,128)} %fusion.20.one_hot_ref, f32[4,16,2048]{2,1,0:T(8,128)} %get-tuple-element.102.ahead_ref, f32[8,16,2048]{2,1,0:T(8,128)} %get-tuple-element.103.behind_ref, f32[8,2048]{1,0:T(8,128)} %get-tuple-element.104.time_ref, ...), custom_call_target="tpu_custom_call" | custom-call | flops 24999999488 | tf_op jit(solution)/shard_map/chain/pallas_call | solution.py:593
  189.2 49.1 %forward_scan.1 = (bf16[128,8,2048]{2,1,0:T(8,128)(2,1)}, bf16[8,2,129,8,16,128]{5,4,3,2,1,0:T(8,128)(2,1)}, bf16[132,8,2048]{2,1,0:T(8,128)(2,1)}, f32[1,2048]{1,0:T(1,128)}) custom-call(f32[1024,128]{1,0:T(8,128)} %get-tuple-element.96.proj_ref, f32[8,128,8,256]{3,2,1,0:T(8,128)} %get-tuple-element.99.dt_ref, ...), custom_call_target="tpu_custom_call" | custom-call | flops 49999998976 | tf_op jit(solution)/shard_map/forward_scan/pallas_call | solution.py:673
  238.3 9.4 %fusion.7 = bf16[2048,1024]{1,0:T(8,128)(2,1)} fusion(bf16[1024,1024]{1,0:T(8,128)(2,1)} %get-tuple-element.97.refs_0_, bf16[128,8,2048]{2,1,0:T(8,128)(2,1)} %get-tuple-element.109), kind=kOutput, calls=%fused_computation.12 | convolution fusion | flops 4297064448 | bytes 10485760 | tf_op jit(solution)/shard_map/dot_general | solution.py:1359
  247.7 3.2 dynamic-slice_bitcast_fusion.2
  252.0 8.1 %convolution_convert_fusion.1 = bf16[1024,2048]{1,0:T(8,128)(2,1)S(1)} fusion(bf16[1056,1024]{1,0:T(8,128)(2,1)S(1)} %copy-done.6, bf16[132,8,2048]{2,1,0:T(8,128)(2,1)} %get-tuple-element.110), kind=kOutput, calls=%fused_computation.14 | convolution fusion | flops 4431282176 | bytes 10682368 | tf_op jit(solution)/shard_map/dot_general | solution.py:1359
  260.1 2.0 copy-done.4
  266.6 3.4 fusion.2
  271.6 1.7 dynamic-slice_bitcast_fusion.3
  273.3 2.2 collective-permute-start.4
  276.8 90.8 %backward_scan.1 = (f32[8,128,8,256]{3,2,1,0:T(8,128)}, f32[64,2048]{1,0:T(8,128)}, f32[1,2048]{1,0:T(1,128)}, f32[16,2048]{1,0:T(8,128)}, bf16[1024,128]{1,0:T(8,128)(2,1)}) custom-call(f32[1024,128]{1,0:T(8,128)} %get-tuple-element.96.proj_ref, f32[8,128,8,256]{3,2,1,0:T(8,128)} %get-tuple-element.99.dt_ref, ...), custom_call_target="tpu_custom_call" | custom-call | flops 89999998976 | tf_op jit(solution)/shard_map/backward_scan/pallas_call | solution.py:826
  367.6 2.5 convert_add_fusion.3
  371.8 3.0 collective-permute-start.7
  374.8 1.5 collective-permute-start.5
  376.3 17.0 %filter_back.1 = (bf16[132,8,2048]{2,1,0:T(8,128)(2,1)}, f32[128,2048]{1,0:T(8,128)}, f32[4,2048]{1,0:T(4,128)}, f32[1,2048]{1,0:T(1,128)}) custom-call(bf16[16,132,8,256]{3,2,1,0:T(8,128)(2,1)} %bitcast.105, f32[8,128,8,256]{3,2,1,0:T(8,128)} %get-tuple-element.94.act_ref, bf16[8,128,8,256]{3,2,1,0:T(8,128)(2,1)} %get-tuple-element.95.bend_ref, ...), custom_call_target="tpu_custom_call" | custom-call | flops 20000000000 | tf_op jit(solution)/shard_map/filter_back/pallas_call | solution.py:930
  394.4 3.1 collective-permute-done.6
  397.5 8.3 %convolution_convert_fusion = bf16[1024,2048]{1,0:T(8,128)(2,1)S(1)} fusion(bf16[1056,1024]{1,0:T(8,128)(2,1)} %get-tuple-element.91.refs_0_, bf16[132,8,2048]{2,1,0:T(8,128)(2,1)} %get-tuple-element.124), kind=kOutput, calls=%fused_computation.13 | convolution fusion | flops 4431282176 | bytes 10682368 | tf_op jit(solution)/shard_map/dot_general | solution.py:1359
  406.3 1.8 copy-done.3
  408.1 6.0 %fusion.3.mixed_ref = f32[1024,1024]{1,0:T(8,128)} fusion(bf16[2048,1024]{1,0:T(8,128)(2,1)S(1)} %copy-done.3, bf16[128,8,2048]{2,1,0:T(8,128)(2,1)S(1)} %copy-done.12), kind=kOutput, calls=%fused_computation.8 | convolution fusion | flops 4294967296 | bytes 12582912 | tf_op jit(solution)/shard_map/dot_general | solution.py:1530
  415.9 2.2 collective-permute-start.11
  419.4 2.6 collective-permute-start.14
  422.0 15.1 %product.5.grad_ref.grad_halo_ref = f32[1056,1024]{1,0:T(8,128)} custom-call(bf16[1056,2048]{1,0:T(8,128)(2,1)} %bitcast.110, bf16[1056,2048]{1,0:T(8,128)(2,1)} %bitcast.109, bf16[1024,4096]{1,0:T(8,128)(2,1)} %get-tuple-element.92.refs_1_.refs_2_), custom_call_target="tpu_custom_call" | custom-call | flops 10000000 | tf_op jit(solution)/shard_map/product/pallas_call | solution.py:75
  437.1 11.3 %finish.1 = (bf16[4,128,1024]{2,1,0:T(8,128)(2,1)}, bf16[4,128,1024]{2,1,0:T(8,128)(2,1)}, f32[4,128,1024]{2,1,0:T(8,128)}, f32[4,128,1024]{2,1,0:T(8,128)}, f32[32,1024]{1,0:T(8,128)}, /*index=5*/f32[1,1024]{1,0:T(1,128)}) custom-call(f32[1024,1024]{1,0:T(8,128)} %fusion.3.mixed_ref, f32[1056,1024]{1,0:T(8,128)} %product.5.grad_ref.grad_halo_ref, ...), custom_call_target="tpu_custom_call" | custom-call | flops 10000000 | tf_op jit(solution)/shard_map/finish/pallas_call | solution.py:189
  448.4 1.8 collective-permute-start.12
  450.2 35.3 %tail.1 = (bf16[128,2048]{1,0:T(8,128)(2,1)}, bf16[192,256]{1,0:T(8,128)(2,1)}, f32[16,1024]{1,0:T(8,128)}) custom-call(f32[4,4]{1,0:T(4,128)} %fusion.20.one_hot_ref, bf16[128,2048]{1,0:T(8,128)(2,1)} %get-tuple-element.136.b0, bf16[128,2048]{1,0:T(8,128)(2,1)} %collective-permute-done.9.b1, bf16[128,2048]{1,0:T(8,128)(2,1)} %collective-permute-done.10.b2, ...), custom_call_target="tpu_custom_call" | custom-call | flops 30000001024 | tf_op jit(solution)/shard_map/tail/pallas_call | solution.py:1278
  486.2 3.5 deliver.1
  (103 shorter events, 35.3 us)
Async XLA Ops:
  61.1 10.1 %copy-start.8 = (bf16[2048,128]{1,0:T(8,128)(2,1)S(1)}, bf16[2048,128]{1,0:T(8,128)(2,1)}, u32[]{:S(2)}) copy-start(bf16[2048,128]{1,0:T(8,128)(2,1)} %get-tuple-element.93.sel_ref) | copy-start | bytes 1572868
  69.4 0.8 copy-start.1
  247.7 4.2 copy-start.6
  251.0 15.6 %collective-permute-start = (bf16[4,256,1024]{2,1,0:T(8,128)(2,1)}, bf16[4,256,1024]{2,1,0:T(8,128)(2,1)}, u32[]{:S(2)}, u32[]{:S(2)}) collective-permute-start(bf16[4,256,1024]{2,1,0:T(8,128)(2,1)} %dynamic-slice_bitcast_fusion.2), channel_id=1, source_target_pairs={{0,1},{1,0},{2,3},{3,2},{4,5},{5,4},{6,7},{7,6},{8,9},{9,8},{10,11... | collective-permute-start | bytes 6291464 | tf_op jit(solution)/shard_map/ppermute | solution.py:1371
  260.1 2.0 copy-start.4
  260.1 3.5 copy-start.7
  260.1 4.4 copy-start.2
  263.6 6.6 %collective-permute-start.1 = (bf16[4,128,2048]{2,1,0:T(8,128)(2,1)}, bf16[4,128,2048]{2,1,0:T(8,128)(2,1)S(1)}, u32[]{:S(2)}, u32[]{:S(2)}) collective-permute-start(bf16[4,128,2048]{2,1,0:T(8,128)(2,1)} %dynamic-slice_bitcast_fusion.1), channel_id=1, source_target_pairs={{0,1},{1,0},{2,3},{3,2},{4,5},{5,4},{6,7},{7,6},{8,9},{9,8},{10,11... | collective-permute-start | bytes 6291464 | tf_op jit(solution)/shard_map/ppermute | solution.py:1371
  266.6 3.6 copy-start.5
  273.3 94.3 %collective-permute-start.4 = (bf16[256,2048]{1,0:T(8,128)(2,1)}, bf16[256,2048]{1,0:T(8,128)(2,1)}, u32[]{:S(2)}, u32[]{:S(2)}) collective-permute-start(bf16[256,2048]{1,0:T(8,128)(2,1)} %get-tuple-element.166), channel_id=1, source_target_pairs={{0,6},{1,7},{2,4},{3,5},{4,2},{5,3},{6,0},{7,1},{8,14},{9,15},{10,... | collective-permute-start | bytes 3145736 | tf_op jit(solution)/shard_map/ppermute | solution.py:1371
  275.5 92.1 %collective-permute-start.3 = (bf16[256,2048]{1,0:T(8,128)(2,1)}, bf16[256,2048]{1,0:T(8,128)(2,1)}, u32[]{:S(2)}, u32[]{:S(2)}) collective-permute-start(bf16[256,2048]{1,0:T(8,128)(2,1)} %get-tuple-element.167), channel_id=1, source_target_pairs={{0,4},{1,5},{2,6},{3,7},{4,0},{5,1},{6,2},{7,3},{8,12},{9,13},{10,... | collective-permute-start | bytes 3145736 | tf_op jit(solution)/shard_map/ppermute | solution.py:1371
  276.2 91.4 %collective-permute-start.2 = (bf16[256,2048]{1,0:T(8,128)(2,1)}, bf16[256,2048]{1,0:T(8,128)(2,1)}, u32[]{:S(2)}, u32[]{:S(2)}) collective-permute-start(bf16[256,2048]{1,0:T(8,128)(2,1)} %get-tuple-element.168), channel_id=1, source_target_pairs={{0,2},{1,3},{2,0},{3,1},{4,6},{5,7},{6,4},{7,5},{8,10},{9,11},{10,... | collective-permute-start | bytes 3145736 | tf_op jit(solution)/shard_map/ppermute | solution.py:1371
  367.6 2.6 copy-start.9
  370.2 1.4 copy-start
  371.8 22.6 %collective-permute-start.7 = (bf16[64,2048]{1,0:T(8,128)(2,1)S(1)}, bf16[64,2048]{1,0:T(8,128)(2,1)S(1)}, u32[]{:S(2)}, u32[]{:S(2)}) collective-permute-start(bf16[64,2048]{1,0:T(8,128)(2,1)S(1)} %get-tuple-element.176), channel_id=1, source_target_pairs={{0,24},{8,16},{16,8},{24,0},{1,25},{9,17},{17,9},{25,1},{2,26},{10... | collective-permute-start | bytes 786440 | tf_op jit(solution)/shard_map/ppermute | solution.py:1371
  374.8 22.7 %collective-permute-start.6 = (bf16[64,2048]{1,0:T(8,128)(2,1)S(1)}, bf16[64,2048]{1,0:T(8,128)(2,1)S(1)}, u32[]{:S(2)}, u32[]{:S(2)}) collective-permute-start(bf16[64,2048]{1,0:T(8,128)(2,1)S(1)} %get-tuple-element.177), channel_id=1, source_target_pairs={{0,16},{8,24},{16,0},{24,8},{1,17},{9,25},{17,1},{25,9},{2,18},{10... | collective-permute-start | bytes 786440 | tf_op jit(solution)/shard_map/ppermute | solution.py:1371
  374.8 22.7 %collective-permute-start.5 = (bf16[64,2048]{1,0:T(8,128)(2,1)S(1)}, bf16[64,2048]{1,0:T(8,128)(2,1)S(1)}, u32[]{:S(2)}, u32[]{:S(2)}) collective-permute-start(bf16[64,2048]{1,0:T(8,128)(2,1)S(1)} %get-tuple-element.178), channel_id=1, source_target_pairs={{0,8},{8,0},{16,24},{24,16},{1,9},{9,1},{17,25},{25,17},{2,10},{10... | collective-permute-start | bytes 786440 | tf_op jit(solution)/shard_map/ppermute | solution.py:1371
  397.5 8.8 %copy-start.12 = (bf16[128,8,2048]{2,1,0:T(8,128)(2,1)S(1)}, bf16[128,8,2048]{2,1,0:T(8,128)(2,1)}, u32[]{:S(2)}) copy-start(bf16[128,8,2048]{2,1,0:T(8,128)(2,1)} %get-tuple-element.109) | copy-start | bytes 12582916
  405.8 2.3 copy-start.3
  406.0 42.4 %copy-start.10 = (bf16[64,2048]{1,0:T(8,128)(2,1)}, bf16[64,2048]{1,0:T(8,128)(2,1)S(1)}, u32[]{:S(2)}) copy-start(bf16[64,2048]{1,0:T(8,128)(2,1)S(1)} %add_convert_fusion.rest_0_) | copy-start | bytes 786436
  406.2 7.9 %collective-permute-start.8 = (bf16[4,128,2048]{2,1,0:T(8,128)(2,1)S(1)}, bf16[4,128,2048]{2,1,0:T(8,128)(2,1)S(1)}, u32[]{:S(2)}, u32[]{:S(2)}) collective-permute-start(bf16[4,128,2048]{2,1,0:T(8,128)(2,1)S(1)} %dynamic-slice_bitcast_fusion), channel_id=1, source_target_pairs={{0,1},{1,0},{2,3},{3,2},{4,5},{5,4},{6,7},{7,6},{8,9},{9,8},{10,11... | collective-permute-start | bytes 6291464 | tf_op jit(solution)/shard_map/ppermute | solution.py:1371
  415.9 32.5 %collective-permute-start.11 = (bf16[128,2048]{1,0:T(8,128)(2,1)S(1)}, bf16[128,2048]{1,0:T(8,128)(2,1)}, u32[]{:S(2)}, u32[]{:S(2)}) collective-permute-start(bf16[128,2048]{1,0:T(8,128)(2,1)S(1)} %get-tuple-element.170), channel_id=1, source_target_pairs={{0,6},{1,7},{2,4},{3,5},{4,2},{5,3},{6,0},{7,1},{8,14},{9,15},{10,... | collective-permute-start | bytes 1572872 | tf_op jit(solution)/shard_map/ppermute | solution.py:1371
  418.1 32.1 %collective-permute-start.10 = (bf16[128,2048]{1,0:T(8,128)(2,1)S(1)}, bf16[128,2048]{1,0:T(8,128)(2,1)}, u32[]{:S(2)}, u32[]{:S(2)}) collective-permute-start(bf16[128,2048]{1,0:T(8,128)(2,1)S(1)} %get-tuple-element.171), channel_id=1, source_target_pairs={{0,4},{1,5},{2,6},{3,7},{4,0},{5,1},{6,2},{7,3},{8,12},{9,13},{10,... | collective-permute-start | bytes 1572872 | tf_op jit(solution)/shard_map/ppermute | solution.py:1371
  418.8 31.4 %collective-permute-start.9 = (bf16[128,2048]{1,0:T(8,128)(2,1)S(1)}, bf16[128,2048]{1,0:T(8,128)(2,1)}, u32[]{:S(2)}, u32[]{:S(2)}) collective-permute-start(bf16[128,2048]{1,0:T(8,128)(2,1)S(1)} %get-tuple-element.172), channel_id=1, source_target_pairs={{0,2},{1,3},{2,0},{3,1},{4,6},{5,7},{6,4},{7,5},{8,10},{9,11},{10,... | collective-permute-start | bytes 1572872 | tf_op jit(solution)/shard_map/ppermute | solution.py:1371
  419.4 66.1 %collective-permute-start.14 = (bf16[64,2048]{1,0:T(8,128)(2,1)S(1)}, bf16[64,2048]{1,0:T(8,128)(2,1)}, u32[]{:S(2)}, u32[]{:S(2)}) collective-permute-start(bf16[64,2048]{1,0:T(8,128)(2,1)S(1)} %add_convert_fusion.rest_0_), channel_id=1, source_target_pairs={{0,24},{8,16},{16,8},{24,0},{1,25},{9,17},{17,9},{25,1},{2,26},{10... | collective-permute-start | bytes 786440 | tf_op jit(solution)/shard_map/ppermute | solution.py:1371
  422.0 63.5 %collective-permute-start.13 = (bf16[64,2048]{1,0:T(8,128)(2,1)S(1)}, bf16[64,2048]{1,0:T(8,128)(2,1)}, u32[]{:S(2)}, u32[]{:S(2)}) collective-permute-start(bf16[64,2048]{1,0:T(8,128)(2,1)S(1)} %add_convert_fusion.rest_0_), channel_id=1, source_target_pairs={{0,16},{8,24},{16,0},{24,8},{1,17},{9,25},{17,1},{25,9},{2,18},{10... | collective-permute-start | bytes 786440 | tf_op jit(solution)/shard_map/ppermute | solution.py:1371
  448.4 37.1 %collective-permute-start.12 = (bf16[64,2048]{1,0:T(8,128)(2,1)S(1)}, bf16[64,2048]{1,0:T(8,128)(2,1)S(1)}, u32[]{:S(2)}, u32[]{:S(2)}) collective-permute-start(bf16[64,2048]{1,0:T(8,128)(2,1)S(1)} %add_convert_fusion.rest_0_), channel_id=1, source_target_pairs={{0,8},{8,0},{16,24},{24,16},{1,9},{9,1},{17,25},{25,17},{2,10},{10... | collective-permute-start | bytes 786440 | tf_op jit(solution)/shard_map/ppermute | solution.py:1371
  485.5 0.7 copy-start.11

commit v7 on v6

--- a/solution.py
+++ b/solution.py
@@ -112,7 +112,7 @@
     cot_ref[...] = by_time(prompt_cot_ref, piece_cot_ref).reshape(count, D).astype(bf16)
 
 
-CHUNK = 16
+CHUNK = 32
 PREPARE_CHUNK = 32
 
 
@@ -358,7 +358,7 @@
         dt_ref[pl.ds(t, chunk)] = dt
         sig_ref[pl.ds(t, chunk)] = jnp.where(pre >= 0.0, inverse, small * inverse).astype(bf16)
         gate = gate_ref[pl.ds(t + HALO, chunk)].astype(f32)
-        gg = gg_ref[pl.ds(t, chunk)]
+        gg = gg_ref[pl.ds(t, chunk)].astype(f32)
         sig = sigmoid(gate)
         silu = gate * sig
         yg_ref[pl.ds(t, chunk)] = gg * silu
@@ -1462,7 +1462,7 @@
 
     mixture = product([scaled], full_input, bf16, tiled=True)
     mixture = mixture.reshape(-1, steps + HALO, SEQS, WIDE)
-    gated_grad = product([cotangent], full_output, f32, across=True, tiled=True)
+    gated_grad = product([cotangent], full_output, bf16, across=True, tiled=True)
     gated_grad = gated_grad.reshape(-1, steps, SEQS, WIDE)
     act, bend, proj = front(mixture, fw, fb, select_pad, steps)
     groups = 1 if split == 1 else 2

time: 491 us -> 489 us (level)
  no operation moved by 1% of the time
where the time goes in v7:
time: 489 us; the launch traced here: 488 us
  Pallas kernels  387 us (79%)
  local copies, waits for them, and re-layouts  32.1 us (7%)
  matrix products  31.9 us (7%)
  starting transfers between devices  17 us (3%)
  other arithmetic  15.7 us (3%)
    pallas_call x1, Pallas kernels, backward(): pl.pallas_call(backward_kernel, grid=(grid,), in_specs=[pl.BlockSpec((ste...  90.8 us
    pallas_call x1, Pallas kernels, gather(): pl.pallas_call(gather_kernel, in_specs=[vmem] * 4, out_specs=[hbm] * 4, o...  50.4 us
    pallas_call x1, Pallas kernels, piece(): pl.pallas_call(piece_kernel, grid=(grid,), in_specs=[pl.BlockSpec((steps...  50.3 us
    pallas_call x1, Pallas kernels, forward(): pl.pallas_call(forward_kernel, grid=(grid,), in_specs=[pl.BlockSpec((step...  49.1 us
    pallas_call x3, Pallas kernels, product(): pl.pallas_call(functools.partial(product_kernel, across), grid=(columns /...  38 us
    pallas_call x1, Pallas kernels, tail(): pl.pallas_call(tail_kernel, in_specs=[pl.BlockSpec(memory_space=pltpu.SME...  35.2 us
    dot_general x3, matrix products, contract_rows(): lax.dot_general(left_side, right_side, (((0,), (0,)), ((), ())), preferre...  25.9 us
    pallas_call x1, Pallas kernels, chain(): pl.pallas_call(chain_kernel, in_specs=[pl.BlockSpec(memory_space=pltpu.SM...  24.5 us
  transfers between devices with their start and end apart: 15, of which 1 were waited for; matrix products, arithmetic and copies ran while one was open for 5% of the time, Pallas kernels for 35%

profile of v7, /device:TPU:0, one launch (start us, length us, event | category | flops | bytes accessed | tf_op | source)
XLA Modules:
  0.0 488.1 jit_solution(17697668939147483304)
XLA Ops:
  6.2 1.5 concatenate.15
  10.7 50.4 %gather.7 = (bf16[1024,256]{1,0:T(8,128)(2,1)}, bf16[2048,128]{1,0:T(8,128)(2,1)}, bf16[2048,1024]{1,0:T(8,128)(2,1)}, bf16[1024,4096]{1,0:T(8,128)(2,1)}) custom-call(bf16[128,256]{1,0:T(8,128)(2,1)} %pad.21.rows_ref, bf16[256,128]{1,0:T(8,128)(2,1)} %fusion.14.select_ref, bf16[256,1024]{1,0:T(8,128)(2,1)} %out_ref.1, bf16[128,4096]{1,0:T(8,128)(2,1)} %in_ref.1), custom_call_target="tpu_custom_call" | custom-call | flops 54999998464 | tf_op jit(solution)/shard_map/gather/pallas_call | solution.py:1128
  72.8 6.5 %prepare.1 = (bf16[1056,1024]{1,0:T(8,128)(2,1)}, bf16[1024,1024]{1,0:T(8,128)(2,1)}) custom-call(bf16[4,128,1024]{2,1,0:T(8,128)(2,1)} %prompt_ref.3, bf16[4,128,1024]{2,1,0:T(8,128)(2,1)} %piece_ref.3, bf16[4,128,1024]{2,1,0:T(8,128)(2,1)} %prompt_cot_ref.3, bf16[4,128,1024]{2,1,0:T(8,128)(2,1)} %piece_cot_ref.3, f32[32,1024]{1,0:T(8,128)} %bitcast_convert_fusion.halo_ref, ...), custom_call_target="tpu_custom_call" | custom-call | flops 5000000000 | tf_op jit(solution)/shard_map/prepare/pallas_call | solution.py:123
  79.2 8.5 %product.4 = bf16[8,1024,256]{2,1,0:T(8,128)(2,1)} custom-call(bf16[1024,1024]{1,0:T(8,128)(2,1)} %get-tuple-element.97.refs_0_, bf16[2048,1024]{1,0:T(8,128)(2,1)} %get-tuple-element.98.refs_1_), custom_call_target="tpu_custom_call" | custom-call | flops 10000000 | tf_op jit(solution)/shard_map/product/pallas_call | solution.py:75
  87.7 14.5 %product.3 = bf16[16,1056,256]{2,1,0:T(8,128)(2,1)} custom-call(bf16[1056,1024]{1,0:T(8,128)(2,1)} %get-tuple-element.91.refs_0_, bf16[1024,4096]{1,0:T(8,128)(2,1)} %get-tuple-element.92.refs_1_.refs_2_), custom_call_target="tpu_custom_call" | custom-call | flops 10000000 | tf_op jit(solution)/shard_map/product/pallas_call | solution.py:75
  102.2 11.3 %front.1 = (f32[8,128,8,256]{3,2,1,0:T(8,128)}, bf16[8,128,8,256]{3,2,1,0:T(8,128)(2,1)}, f32[1024,128]{1,0:T(8,128)}) custom-call(bf16[16,132,8,256]{3,2,1,0:T(8,128)(2,1)} %bitcast.103, f32[4,2048]{1,0:T(4,128)} %bitcast.123, f32[1,2048]{1,0:T(1,128)} %bitcast.128, bf16[2048,128]{1,0:T(8,128)(2,1)} %get-tuple-element.93.sel_ref), custom_call_target="tpu_custom_call" | custom-call | flops 16000000000 | tf_op jit(solution)/shard_map/front/pallas_call | solution.py:245
  113.5 50.3 %piece.1 = (f32[8,128,8,256]{3,2,1,0:T(8,128)}, bf16[8,128,8,256]{3,2,1,0:T(8,128)(2,1)}, f32[8,128,8,256]{3,2,1,0:T(8,128)}, bf16[8,128,8,256]{3,2,1,0:T(8,128)...) custom-call(f32[1024,128]{1,0:T(8,128)} %get-tuple-element.96.proj_r, ...), custom_call_target="tpu_custom_call" | custom-call | flops 60000002048 | tf_op jit(solution)/shard_map/piece/pallas_call | solution.py:446
  163.8 24.5 %chain.1 = (f32[8,16,2048]{2,1,0:T(8,128)}, f32[8,16,2048]{2,1,0:T(8,128)}) custom-call(f32[4,4]{1,0:T(4,128)} %fusion.20.one_hot_ref, f32[4,16,2048]{2,1,0:T(8,128)} %get-tuple-element.102.ahead_ref, f32[8,16,2048]{2,1,0:T(8,128)} %get-tuple-element.103.behind_ref, f32[8,2048]{1,0:T(8,128)} %get-tuple-element.104.time_ref, ...), custom_call_target="tpu_custom_call" | custom-call | flops 24999999488 | tf_op jit(solution)/shard_map/chain/pallas_call | solution.py:593
  188.3 49.1 %forward_scan.1 = (bf16[128,8,2048]{2,1,0:T(8,128)(2,1)}, bf16[8,2,129,8,16,128]{5,4,3,2,1,0:T(8,128)(2,1)}, bf16[132,8,2048]{2,1,0:T(8,128)(2,1)}, f32[1,2048]{1,0:T(1,128)}) custom-call(f32[1024,128]{1,0:T(8,128)} %get-tuple-element.96.proj_ref, f32[8,128,8,256]{3,2,1,0:T(8,128)} %get-tuple-element.99.dt_ref, ...), custom_call_target="tpu_custom_call" | custom-call | flops 49999998976 | tf_op jit(solution)/shard_map/forward_scan/pallas_call | solution.py:673
  237.4 9.4 %fusion.7 = bf16[2048,1024]{1,0:T(8,128)(2,1)} fusion(bf16[1024,1024]{1,0:T(8,128)(2,1)} %get-tuple-element.97.refs_0_, bf16[128,8,2048]{2,1,0:T(8,128)(2,1)} %get-tuple-element.109), kind=kOutput, calls=%fused_computation.12 | convolution fusion | flops 4297064448 | bytes 10485760 | tf_op jit(solution)/shard_map/dot_general | solution.py:1359
  246.8 3.2 dynamic-slice_bitcast_fusion.2
  251.1 8.1 %convolution_convert_fusion.1 = bf16[1024,2048]{1,0:T(8,128)(2,1)S(1)} fusion(bf16[1056,1024]{1,0:T(8,128)(2,1)S(1)} %copy-done.6, bf16[132,8,2048]{2,1,0:T(8,128)(2,1)} %get-tuple-element.110), kind=kOutput, calls=%fused_computation.14 | convolution fusion | flops 4431282176 | bytes 10682368 | tf_op jit(solution)/shard_map/dot_general | solution.py:1359
  259.2 2.0 copy-done.3
  265.7 3.4 fusion.2
  270.7 1.7 dynamic-slice_bitcast_fusion.3
  272.4 2.2 collective-permute-start.4
  275.9 90.8 %backward_scan.1 = (f32[8,128,8,256]{3,2,1,0:T(8,128)}, f32[64,2048]{1,0:T(8,128)}, f32[1,2048]{1,0:T(1,128)}, f32[16,2048]{1,0:T(8,128)}, bf16[1024,128]{1,0:T(8,128)(2,1)}) custom-call(f32[1024,128]{1,0:T(8,128)} %get-tuple-element.96.proj_ref, f32[8,128,8,256]{3,2,1,0:T(8,128)} %get-tuple-element.99.dt_ref, ...), custom_call_target="tpu_custom_call" | custom-call | flops 89999998976 | tf_op jit(solution)/shard_map/backward_scan/pallas_call | solution.py:826
  366.8 2.5 convert_add_fusion.3
  370.9 2.9 collective-permute-start.7
  373.9 1.5 collective-permute-start.5
  375.4 17.0 %filter_back.1 = (bf16[132,8,2048]{2,1,0:T(8,128)(2,1)}, f32[128,2048]{1,0:T(8,128)}, f32[4,2048]{1,0:T(4,128)}, f32[1,2048]{1,0:T(1,128)}) custom-call(bf16[16,132,8,256]{3,2,1,0:T(8,128)(2,1)} %bitcast.105, f32[8,128,8,256]{3,2,1,0:T(8,128)} %get-tuple-element.94.act_ref, bf16[8,128,8,256]{3,2,1,0:T(8,128)(2,1)} %get-tuple-element.95.bend_ref, ...), custom_call_target="tpu_custom_call" | custom-call | flops 20000000000 | tf_op jit(solution)/shard_map/filter_back/pallas_call | solution.py:930
  393.5 3.0 collective-permute-done.6
  396.6 8.3 %convolution_convert_fusion = bf16[1024,2048]{1,0:T(8,128)(2,1)S(1)} fusion(bf16[1056,1024]{1,0:T(8,128)(2,1)} %get-tuple-element.91.refs_0_, bf16[132,8,2048]{2,1,0:T(8,128)(2,1)} %get-tuple-element.124), kind=kOutput, calls=%fused_computation.13 | convolution fusion | flops 4431282176 | bytes 10682368 | tf_op jit(solution)/shard_map/dot_general | solution.py:1359
  405.3 1.9 copy-done.5
  407.2 6.0 %fusion.3.mixed_ref = f32[1024,1024]{1,0:T(8,128)} fusion(bf16[2048,1024]{1,0:T(8,128)(2,1)S(1)} %copy-done.5, bf16[128,8,2048]{2,1,0:T(8,128)(2,1)S(1)} %copy-done.12), kind=kOutput, calls=%fused_computation.8 | convolution fusion | flops 4294967296 | bytes 12582912 | tf_op jit(solution)/shard_map/dot_general | solution.py:1530
  415.1 2.2 collective-permute-start.11
  418.6 2.6 collective-permute-start.14
  421.2 15.1 %product.5.grad_ref.grad_halo_ref = f32[1056,1024]{1,0:T(8,128)} custom-call(bf16[1056,2048]{1,0:T(8,128)(2,1)} %bitcast.109, bf16[1056,2048]{1,0:T(8,128)(2,1)} %bitcast.108, bf16[1024,4096]{1,0:T(8,128)(2,1)} %get-tuple-element.92.refs_1_.refs_2_), custom_call_target="tpu_custom_call" | custom-call | flops 10000000 | tf_op jit(solution)/shard_map/product/pallas_call | solution.py:75
  436.3 10.3 %finish.1 = (bf16[4,128,1024]{2,1,0:T(8,128)(2,1)}, bf16[4,128,1024]{2,1,0:T(8,128)(2,1)}, f32[4,128,1024]{2,1,0:T(8,128)}, f32[4,128,1024]{2,1,0:T(8,128)}, f32[32,1024]{1,0:T(8,128)}, /*index=5*/f32[1,1024]{1,0:T(1,128)}) custom-call(f32[1024,1024]{1,0:T(8,128)} %fusion.3.mixed_ref, f32[1056,1024]{1,0:T(8,128)} %product.5.grad_ref.grad_halo_ref, ...), custom_call_target="tpu_custom_call" | custom-call | flops 10000000 | tf_op jit(solution)/shard_map/finish/pallas_call | solution.py:189
  446.6 1.8 collective-permute-start.12
  448.4 35.2 %tail.1 = (bf16[128,2048]{1,0:T(8,128)(2,1)}, bf16[192,256]{1,0:T(8,128)(2,1)}, f32[16,1024]{1,0:T(8,128)}) custom-call(f32[4,4]{1,0:T(4,128)} %fusion.20.one_hot_ref, bf16[128,2048]{1,0:T(8,128)(2,1)} %get-tuple-element.136.b0, bf16[128,2048]{1,0:T(8,128)(2,1)} %collective-permute-done.9.b1, bf16[128,2048]{1,0:T(8,128)(2,1)} %collective-permute-done.10.b2, ...), custom_call_target="tpu_custom_call" | custom-call | flops 30000001024 | tf_op jit(solution)/shard_map/tail/pallas_call | solution.py:1278
  484.4 3.5 deliver.1
  (103 shorter events, 35.2 us)
Async XLA Ops:
  61.1 10.1 %copy-start.8 = (bf16[2048,128]{1,0:T(8,128)(2,1)S(1)}, bf16[2048,128]{1,0:T(8,128)(2,1)}, u32[]{:S(2)}) copy-start(bf16[2048,128]{1,0:T(8,128)(2,1)} %get-tuple-element.93.sel_ref) | copy-start | bytes 1572868
  69.4 0.8 copy-start.1
  246.8 4.2 copy-start.6
  250.1 15.6 %collective-permute-start = (bf16[4,256,1024]{2,1,0:T(8,128)(2,1)}, bf16[4,256,1024]{2,1,0:T(8,128)(2,1)}, u32[]{:S(2)}, u32[]{:S(2)}) collective-permute-start(bf16[4,256,1024]{2,1,0:T(8,128)(2,1)} %dynamic-slice_bitcast_fusion.2), channel_id=1, source_target_pairs={{0,1},{1,0},{2,3},{3,2},{4,5},{5,4},{6,7},{7,6},{8,9},{9,8},{10,11... | collective-permute-start | bytes 6291464 | tf_op jit(solution)/shard_map/ppermute | solution.py:1371
  259.2 2.0 copy-start.3
  259.2 3.5 copy-start.7
  259.2 4.4 copy-start.2
  262.7 6.6 %collective-permute-start.1 = (bf16[4,128,2048]{2,1,0:T(8,128)(2,1)}, bf16[4,128,2048]{2,1,0:T(8,128)(2,1)S(1)}, u32[]{:S(2)}, u32[]{:S(2)}) collective-permute-start(bf16[4,128,2048]{2,1,0:T(8,128)(2,1)} %dynamic-slice_bitcast_fusion.1), channel_id=1, source_target_pairs={{0,1},{1,0},{2,3},{3,2},{4,5},{5,4},{6,7},{7,6},{8,9},{9,8},{10,11... | collective-permute-start | bytes 6291464 | tf_op jit(solution)/shard_map/ppermute | solution.py:1371
  265.7 3.6 copy-start.4
  272.4 94.3 %collective-permute-start.4 = (bf16[256,2048]{1,0:T(8,128)(2,1)}, bf16[256,2048]{1,0:T(8,128)(2,1)}, u32[]{:S(2)}, u32[]{:S(2)}) collective-permute-start(bf16[256,2048]{1,0:T(8,128)(2,1)} %get-tuple-element.166), channel_id=1, source_target_pairs={{0,6},{1,7},{2,4},{3,5},{4,2},{5,3},{6,0},{7,1},{8,14},{9,15},{10,... | collective-permute-start | bytes 3145736 | tf_op jit(solution)/shard_map/ppermute | solution.py:1371
  274.6 92.1 %collective-permute-start.3 = (bf16[256,2048]{1,0:T(8,128)(2,1)}, bf16[256,2048]{1,0:T(8,128)(2,1)}, u32[]{:S(2)}, u32[]{:S(2)}) collective-permute-start(bf16[256,2048]{1,0:T(8,128)(2,1)} %get-tuple-element.167), channel_id=1, source_target_pairs={{0,4},{1,5},{2,6},{3,7},{4,0},{5,1},{6,2},{7,3},{8,12},{9,13},{10,... | collective-permute-start | bytes 3145736 | tf_op jit(solution)/shard_map/ppermute | solution.py:1371
  275.3 91.4 %collective-permute-start.2 = (bf16[256,2048]{1,0:T(8,128)(2,1)}, bf16[256,2048]{1,0:T(8,128)(2,1)}, u32[]{:S(2)}, u32[]{:S(2)}) collective-permute-start(bf16[256,2048]{1,0:T(8,128)(2,1)} %get-tuple-element.168), channel_id=1, source_target_pairs={{0,2},{1,3},{2,0},{3,1},{4,6},{5,7},{6,4},{7,5},{8,10},{9,11},{10,... | collective-permute-start | bytes 3145736 | tf_op jit(solution)/shard_map/ppermute | solution.py:1371
  366.7 2.6 copy-start.9
  369.3 1.4 copy-start
  370.9 22.6 %collective-permute-start.7 = (bf16[64,2048]{1,0:T(8,128)(2,1)S(1)}, bf16[64,2048]{1,0:T(8,128)(2,1)S(1)}, u32[]{:S(2)}, u32[]{:S(2)}) collective-permute-start(bf16[64,2048]{1,0:T(8,128)(2,1)S(1)} %get-tuple-element.176), channel_id=1, source_target_pairs={{0,24},{8,16},{16,8},{24,0},{1,25},{9,17},{17,9},{25,1},{2,26},{10... | collective-permute-start | bytes 786440 | tf_op jit(solution)/shard_map/ppermute | solution.py:1371
  373.9 22.7 %collective-permute-start.6 = (bf16[64,2048]{1,0:T(8,128)(2,1)S(1)}, bf16[64,2048]{1,0:T(8,128)(2,1)S(1)}, u32[]{:S(2)}, u32[]{:S(2)}) collective-permute-start(bf16[64,2048]{1,0:T(8,128)(2,1)S(1)} %get-tuple-element.177), channel_id=1, source_target_pairs={{0,16},{8,24},{16,0},{24,8},{1,17},{9,25},{17,1},{25,9},{2,18},{10... | collective-permute-start | bytes 786440 | tf_op jit(solution)/shard_map/ppermute | solution.py:1371
  373.9 22.7 %collective-permute-start.5 = (bf16[64,2048]{1,0:T(8,128)(2,1)S(1)}, bf16[64,2048]{1,0:T(8,128)(2,1)S(1)}, u32[]{:S(2)}, u32[]{:S(2)}) collective-permute-start(bf16[64,2048]{1,0:T(8,128)(2,1)S(1)} %get-tuple-element.178), channel_id=1, source_target_pairs={{0,8},{8,0},{16,24},{24,16},{1,9},{9,1},{17,25},{25,17},{2,10},{10... | collective-permute-start | bytes 786440 | tf_op jit(solution)/shard_map/ppermute | solution.py:1371
  396.6 8.7 %copy-start.12 = (bf16[128,8,2048]{2,1,0:T(8,128)(2,1)S(1)}, bf16[128,8,2048]{2,1,0:T(8,128)(2,1)}, u32[]{:S(2)}) copy-start(bf16[128,8,2048]{2,1,0:T(8,128)(2,1)} %get-tuple-element.109) | copy-start | bytes 12582916
  404.9 2.3 copy-start.5
  405.1 41.5 %copy-start.10 = (bf16[64,2048]{1,0:T(8,128)(2,1)}, bf16[64,2048]{1,0:T(8,128)(2,1)S(1)}, u32[]{:S(2)}) copy-start(bf16[64,2048]{1,0:T(8,128)(2,1)S(1)} %add_convert_fusion.rest_0_) | copy-start | bytes 786436
  405.2 8.0 %collective-permute-start.8 = (bf16[4,128,2048]{2,1,0:T(8,128)(2,1)S(1)}, bf16[4,128,2048]{2,1,0:T(8,128)(2,1)S(1)}, u32[]{:S(2)}, u32[]{:S(2)}) collective-permute-start(bf16[4,128,2048]{2,1,0:T(8,128)(2,1)S(1)} %dynamic-slice_bitcast_fusion), channel_id=1, source_target_pairs={{0,1},{1,0},{2,3},{3,2},{4,5},{5,4},{6,7},{7,6},{8,9},{9,8},{10,11... | collective-permute-start | bytes 6291464 | tf_op jit(solution)/shard_map/ppermute | solution.py:1371
  415.1 31.5 %collective-permute-start.11 = (bf16[128,2048]{1,0:T(8,128)(2,1)S(1)}, bf16[128,2048]{1,0:T(8,128)(2,1)}, u32[]{:S(2)}, u32[]{:S(2)}) collective-permute-start(bf16[128,2048]{1,0:T(8,128)(2,1)S(1)} %get-tuple-element.170), channel_id=1, source_target_pairs={{0,6},{1,7},{2,4},{3,5},{4,2},{5,3},{6,0},{7,1},{8,14},{9,15},{10,... | collective-permute-start | bytes 1572872 | tf_op jit(solution)/shard_map/ppermute | solution.py:1371
  417.3 31.1 %collective-permute-start.10 = (bf16[128,2048]{1,0:T(8,128)(2,1)S(1)}, bf16[128,2048]{1,0:T(8,128)(2,1)}, u32[]{:S(2)}, u32[]{:S(2)}) collective-permute-start(bf16[128,2048]{1,0:T(8,128)(2,1)S(1)} %get-tuple-element.171), channel_id=1, source_target_pairs={{0,4},{1,5},{2,6},{3,7},{4,0},{5,1},{6,2},{7,3},{8,12},{9,13},{10,... | collective-permute-start | bytes 1572872 | tf_op jit(solution)/shard_map/ppermute | solution.py:1371
  418.0 30.4 %collective-permute-start.9 = (bf16[128,2048]{1,0:T(8,128)(2,1)S(1)}, bf16[128,2048]{1,0:T(8,128)(2,1)}, u32[]{:S(2)}, u32[]{:S(2)}) collective-permute-start(bf16[128,2048]{1,0:T(8,128)(2,1)S(1)} %get-tuple-element.172), channel_id=1, source_target_pairs={{0,2},{1,3},{2,0},{3,1},{4,6},{5,7},{6,4},{7,5},{8,10},{9,11},{10,... | collective-permute-start | bytes 1572872 | tf_op jit(solution)/shard_map/ppermute | solution.py:1371
  418.6 65.1 %collective-permute-start.14 = (bf16[64,2048]{1,0:T(8,128)(2,1)S(1)}, bf16[64,2048]{1,0:T(8,128)(2,1)}, u32[]{:S(2)}, u32[]{:S(2)}) collective-permute-start(bf16[64,2048]{1,0:T(8,128)(2,1)S(1)} %add_convert_fusion.rest_0_), channel_id=1, source_target_pairs={{0,24},{8,16},{16,8},{24,0},{1,25},{9,17},{17,9},{25,1},{2,26},{10... | collective-permute-start | bytes 786440 | tf_op jit(solution)/shard_map/ppermute | solution.py:1371
  421.2 62.4 %collective-permute-start.13 = (bf16[64,2048]{1,0:T(8,128)(2,1)S(1)}, bf16[64,2048]{1,0:T(8,128)(2,1)}, u32[]{:S(2)}, u32[]{:S(2)}) collective-permute-start(bf16[64,2048]{1,0:T(8,128)(2,1)S(1)} %add_convert_fusion.rest_0_), channel_id=1, source_target_pairs={{0,16},{8,24},{16,0},{24,8},{1,17},{9,25},{17,1},{25,9},{2,18},{10... | collective-permute-start | bytes 786440 | tf_op jit(solution)/shard_map/ppermute | solution.py:1371
  446.6 37.1 %collective-permute-start.12 = (bf16[64,2048]{1,0:T(8,128)(2,1)S(1)}, bf16[64,2048]{1,0:T(8,128)(2,1)S(1)}, u32[]{:S(2)}, u32[]{:S(2)}) collective-permute-start(bf16[64,2048]{1,0:T(8,128)(2,1)S(1)} %add_convert_fusion.rest_0_), channel_id=1, source_target_pairs={{0,8},{8,0},{16,24},{24,16},{1,9},{9,1},{17,25},{25,17},{2,10},{10... | collective-permute-start | bytes 786440 | tf_op jit(solution)/shard_map/ppermute | solution.py:1371
  483.7 0.7 copy-start.11
